TPU v7x, 128 devices: a whole 4x4x4 slice. The times are simulated.
128 devices in a mesh: layer: 2 (over core), rows: 64 (over y, x, z).
Axes of the slice: x: 4, y: 4, z: 4, core: 2. Of those that a mesh axis runs over, the one named last changes fastest.
Arguments:
- frames: bfloat16 [3, 4, 128, 64, 128], P(None, None, 'rows'), may hold values from -6 to 6
- hidden_in: bfloat16 [4, 4, 128, 64, 128], P('layer', None, 'rows'), may hold values from -4 to 4
- cell_in: bfloat16 [4, 4, 128, 64, 128], P('layer', None, 'rows'), may hold values from -6 to 6
- memory_in: bfloat16 [4, 128, 64, 128], P(None, 'rows'), may hold values from -6 to 6
- w_x: bfloat16 [4, 576, 448], P('layer'), may hold values from -0.25 to 0.25
- w_h: bfloat16 [4, 576, 256], P('layer'), may hold values from -0.25 to 0.25
- w_m: bfloat16 [4, 576, 192], P('layer'), may hold values from -0.25 to 0.25
- w_o: bfloat16 [4, 1152, 64], P('layer'), may hold values from -0.1875 to 0.1875
- w_last: bfloat16 [4, 128, 64], P('layer'), may hold values from -0.5 to 0.5
Outputs:
- hidden_out: bfloat16 [4, 4, 128, 64, 128], P('layer', None, 'rows')
- cell_out: bfloat16 [4, 4, 128, 64, 128], P('layer', None, 'rows')
- memory_out: bfloat16 [2, 4, 128, 64, 128], P('layer', None, 'rows')
All inputs are finite; a program needn't handle non-finite values.
Results may differ from a plain program's by a relative error of at most 0.014.
Values may be sent and summed in bfloat16 or wider, within the bound.
No kernel may reach another device: no remote copies, remote signals or barrier semaphores. Data moves between devices by JAX's collectives and lax.ppermute only.
A program may use at most 64 MiB of HBM per device.

v0:
```python
import jax
import jax.numpy as jnp
from jax import lax
from jax.sharding import PartitionSpec as P


def with_halo(block, sides, width):
    for axis, dim in sides:
        count = lax.axis_size(axis)
        forward = [(i, i + 1) for i in range(count - 1)]
        backward = [(target, source) for source, target in forward]
        low = lax.ppermute(
            lax.slice_in_dim(block, block.shape[dim] - width, None, axis=dim), axis, forward
        )
        high = lax.ppermute(lax.slice_in_dim(block, 0, width, axis=dim), axis, backward)
        block = jnp.concatenate([low, block, high], axis=dim)
    return block


def shifted(block, axis, distance):
    devices = range(lax.axis_size(axis))
    route = [(i - distance, i) for i in devices if i - distance in devices]
    return lax.ppermute(block, axis, route)


def shifted_taps(padded, height):
    pieces = []
    for row_offset in range(3):
        row_band = padded[:, row_offset : row_offset + height]
        zero_column = jnp.zeros_like(row_band[..., :1])
        pieces.append(jnp.concatenate([zero_column, row_band[..., :-1]], axis=-1))
        pieces.append(row_band)
        pieces.append(jnp.concatenate([row_band[..., 1:], zero_column], axis=-1))
    return jnp.concatenate(pieces, axis=2)


def convolve(padded, weight, height):
    taps = shifted_taps(padded, height)
    return jnp.einsum("ko,brkw->brow", weight, taps, preferred_element_type=jnp.float32)


def gate_math(input_gates, hidden_gates, memory_gates, cell_prev, memory_prev):
    parts_x = jnp.split(input_gates, 7, axis=2)
    parts_h = jnp.split(hidden_gates, 4, axis=2)
    parts_m = jnp.split(memory_gates, 3, axis=2)
    cell_new = (
        jax.nn.sigmoid(parts_x[1] + parts_h[1] + 1.0) * cell_prev.astype(jnp.float32)
        + jax.nn.sigmoid(parts_x[0] + parts_h[0]) * jnp.tanh(parts_x[2] + parts_h[2])
    ).astype(jnp.bfloat16)
    memory_new = (
        jax.nn.sigmoid(parts_x[4] + parts_m[1] + 1.0) * memory_prev.astype(jnp.float32)
        + jax.nn.sigmoid(parts_x[3] + parts_m[0]) * jnp.tanh(parts_x[5] + parts_m[2])
    ).astype(jnp.bfloat16)
    return (cell_new, memory_new, parts_x[6] + parts_h[3])


def memory_cell(
    layer_input,
    hidden_prev,
    cell_prev,
    memory_prev,
    weight_x,
    weight_h,
    weight_m,
    weight_o,
    weight_last,
):
    height = layer_input.shape[1]
    channels = layer_input.shape[2]
    stacked = jnp.stack([layer_input, hidden_prev, memory_prev])
    padded = with_halo(stacked, (("rows", 2),), 1)
    input_gates = convolve(padded[0], weight_x, height)
    hidden_gates = convolve(padded[1], weight_h, height)
    memory_gates = convolve(padded[2], weight_m, height)
    cell_new, memory_new, output_part = gate_math(
        input_gates, hidden_gates, memory_gates, cell_prev, memory_prev
    )
    memory_pair = jnp.concatenate([cell_new, memory_new], axis=2)
    padded_pair = with_halo(memory_pair, (("rows", 1),), 1)
    output_gate = jax.nn.sigmoid(output_part + convolve(padded_pair, weight_o, height))
    mixed = jnp.einsum(
        "ko,brkw->brow", weight_last, memory_pair, preferred_element_type=jnp.float32
    )
    hidden_new = (output_gate * jnp.tanh(mixed)).astype(jnp.bfloat16)
    return (hidden_new, memory_pair[:, :, :channels], memory_pair[:, :, channels:])


def on_device(frames, hidden_in, cell_in, memory_in, w_x, w_h, w_m, w_o, w_last):
    steps_total = frames.shape[0]
    local_layers = hidden_in.shape[0]
    seq_count = frames.shape[1]
    groups = seq_count // seq_count
    job_total = steps_total * groups
    tick_count = 2 * steps_total
    first_section = lax.axis_index("layer") == 0
    anchor_index = jnp.int32(0)
    empty_block = jnp.zeros((seq_count,) + frames.shape[2:], jnp.bfloat16)

    def advance(tick_index, states):
        hidden_loc, cell_loc, wrapped, fwd_hidden, fwd_memory, top_memory = states
        lower_job = tick_index // 2
        lower_active = tick_index % 2 == 0
        upper_job = (tick_index - 1) // 2
        upper_active = tick_index % 2 == 1
        job_index = jnp.clip(
            jnp.where(first_section, lower_job, upper_job), 0, job_total - 1
        ).astype(jnp.int32)
        active = jnp.where(first_section, lower_active, upper_active)
        time_index = job_index // groups
        seq_start = job_index % groups * seq_count
        frame_block = lax.dynamic_index_in_dim(frames, time_index, 0, keepdims=False)
        layer_input = jnp.where(first_section, frame_block, fwd_hidden)
        memory_now = jnp.where(first_section, wrapped, fwd_memory)
        block_shape = (1, seq_count) + hidden_loc.shape[2:]
        for layer_index in range(local_layers):
            corner = (jnp.int32(layer_index), seq_start, anchor_index, anchor_index, anchor_index)
            hidden_prev = lax.dynamic_slice(hidden_loc, corner, block_shape)[0]
            cell_prev = lax.dynamic_slice(cell_loc, corner, block_shape)[0]
            hidden_new, cell_new, memory_new = memory_cell(
                layer_input,
                hidden_prev,
                cell_prev,
                memory_now,
                w_x[layer_index],
                w_h[layer_index],
                w_m[layer_index],
                w_o[layer_index],
                w_last[layer_index],
            )
            hidden_loc = lax.dynamic_update_slice(
                hidden_loc, jnp.where(active, hidden_new, hidden_prev)[None], corner
            )
            cell_loc = lax.dynamic_update_slice(
                cell_loc, jnp.where(active, cell_new, cell_prev)[None], corner
            )
            layer_input = hidden_new
            memory_now = memory_new
        top_corner = (seq_start, anchor_index, anchor_index, anchor_index)
        top_prev = lax.dynamic_slice(top_memory, top_corner, memory_now.shape)
        top_memory = lax.dynamic_update_slice(
            top_memory, jnp.where(active, memory_now, top_prev), top_corner
        )
        passed_up = shifted(jnp.stack([layer_input, memory_now]), "layer", 1)
        passed_down = shifted(memory_now, "layer", -1)
        upper_index = jnp.clip(upper_job, 0, job_total - 1).astype(jnp.int32)
        upper_start = upper_index % groups * seq_count
        wrap_corner = (upper_start, anchor_index, anchor_index, anchor_index)
        store_wrap = first_section & upper_active
        wrapped_prev = lax.dynamic_slice(wrapped, wrap_corner, passed_down.shape)
        wrapped = lax.dynamic_update_slice(
            wrapped, jnp.where(store_wrap, passed_down, wrapped_prev), wrap_corner
        )
        return (hidden_loc, cell_loc, wrapped, passed_up[0], passed_up[1], top_memory)

    initial = (hidden_in, cell_in, memory_in, empty_block, empty_block, jnp.zeros_like(memory_in))
    finished = lax.fori_loop(0, tick_count, advance, initial)
    hidden_done = finished[0]
    cell_done = finished[1]
    top_done = finished[5][None]
    return (hidden_done, cell_done, top_done)


def solution(mesh):
    return jax.shard_map(
        on_device,
        mesh=mesh,
        in_specs=(
            P(None, None, "rows", None, None),
            P("layer", None, "rows", None, None),
            P("layer", None, "rows", None, None),
            P(None, "rows", None, None),
            P("layer", None, None),
            P("layer", None, None),
            P("layer", None, None),
            P("layer", None, None),
            P("layer", None, None),
        ),
        out_specs=(
            P("layer", None, "rows", None, None),
            P("layer", None, "rows", None, None),
            P("layer", None, "rows", None, None),
        ),
        check_vma=False,
    )
```

profile of v0, /device:TPU:25, one launch (start us, length us, event | category | flops | bytes accessed | tf_op | source)
XLA Modules:
  0.0 455.9 jit_solution(3836010967363702486)
XLA Ops:
  2.1 452.9 %while.27 = (s32[]{:T(128)}, bf16[2,4,2,64,128]{4,3,2,1,0:T(8,128)(2,1)S(1)}, bf16[2,4,2,64,128]{4,3,2,1,0:T(8,128)(2,1)S(1)}, bf16[4,2,64,128]{3,2,1,0:T(8,128)...) while((s32[]{:T(128)}, ...), condition=%wide.region_1.2_spmd.clone, body=%wide.region_0.1_spmd.clone.sunk | while | flops 2467938304 | bytes 100801512 | solution.py:156
  3.2 8.0 %collective-permute-start = (bf16[3,4,1,64,128]{4,3,2,1,0:T(8,128)(2,1)S(1)}, bf16[3,4,1,64,128]{4,3,2,1,0:T(8,128)(2,1)S(1)}, u32[]{:S(2)}, u32[]{:S(2)}) collective-permute-start(bf16[3,4,1,64,128]{4,3,2,1,0:T(8,128)(2,1)S(1)} %get-tuple-element.705), channel_id=1, source_target_pairs={{1,0},{2,1},{3,2},{4,3},{5,4},{6,5},{7,6},{8,7},{9,8},{10,9},{11,1... | collective-permute-start | bytes 589832 | tf_op jit(solution)/shard_map/while/body/eval_jaxpr/ppermute | solution.py:15
  14.8 8.1 %collective-permute-done.1 = bf16[3,4,1,64,128]{4,3,2,1,0:T(8,128)(2,1)S(1)} collective-permute-done((bf16[3,4,1,64,128]{4,3,2,1,0:T(8,128)(2,1)S(1)}, bf16[3,4,1,64,128]{4,3,2,1,0:T(8,128)(2,1)S(1)}, u32[]{:S(2)}, u32[]{:S(2)}) %collective-permute-start.1) | collective-permute-done | bytes 196640 | tf_op jit(solution)/shard_map/while/body/eval_jaxpr/ppermute | solution.py:12
  34.4 6.1 %collective-permute-done.3 = bf16[4,1,128,128]{3,2,1,0:T(8,128)(2,1)S(1)} collective-permute-done((bf16[4,1,128,128]{3,2,1,0:T(8,128)(2,1)S(1)}, bf16[4,1,128,128]{3,2,1,0:T(8,128)(2,1)S(1)}, u32[]{:S(2)}, u32[]{:S(2)}) %collective-permute-start.3) | collective-permute-done | bytes 131104 | tf_op jit(solution)/shard_map/while/body/eval_jaxpr/ppermute | solution.py:12
  49.6 6.1 %collective-permute-done.5 = bf16[3,4,1,64,128]{4,3,2,1,0:T(8,128)(2,1)S(1)} collective-permute-done((bf16[3,4,1,64,128]{4,3,2,1,0:T(8,128)(2,1)S(1)}, bf16[3,4,1,64,128]{4,3,2,1,0:T(8,128)(2,1)S(1)}, u32[]{:S(2)}, u32[]{:S(2)}) %collective-permute-start.5) | collective-permute-done | bytes 196640 | tf_op jit(solution)/shard_map/while/body/eval_jaxpr/ppermute | solution.py:12
  66.5 6.6 %collective-permute-start.8 = (bf16[4,2,64,128]{3,2,1,0:T(8,128)(2,1)S(1)}, bf16[4,2,64,128]{3,2,1,0:T(8,128)(2,1)S(1)}, u32[]{:S(2)}, u32[]{:S(2)}) collective-permute-start(bf16[4,2,64,128]{3,2,1,0:T(8,128)(2,1)S(1)} %get-tuple-element.758), channel_id=1, source_target_pairs={{64,0},{65,1},{66,2},{67,3},{68,4},{69,5},{70,6},{71,7},{72,8},{73... | collective-permute-start | bytes 393224 | tf_op jit(solution)/shard_map/while/body/eval_jaxpr/ppermute | solution.py:23
  91.9 6.1 %collective-permute-done.1 = bf16[3,4,1,64,128]{4,3,2,1,0:T(8,128)(2,1)S(1)} collective-permute-done((bf16[3,4,1,64,128]{4,3,2,1,0:T(8,128)(2,1)S(1)}, bf16[3,4,1,64,128]{4,3,2,1,0:T(8,128)(2,1)S(1)}, u32[]{:S(2)}, u32[]{:S(2)}) %collective-permute-start.1) | collective-permute-done | bytes 196640 | tf_op jit(solution)/shard_map/while/body/eval_jaxpr/ppermute | solution.py:12
  109.4 6.1 %collective-permute-done.3 = bf16[4,1,128,128]{3,2,1,0:T(8,128)(2,1)S(1)} collective-permute-done((bf16[4,1,128,128]{3,2,1,0:T(8,128)(2,1)S(1)}, bf16[4,1,128,128]{3,2,1,0:T(8,128)(2,1)S(1)}, u32[]{:S(2)}, u32[]{:S(2)}) %collective-permute-start.3) | collective-permute-done | bytes 131104 | tf_op jit(solution)/shard_map/while/body/eval_jaxpr/ppermute | solution.py:12
  124.7 6.1 %collective-permute-done.5 = bf16[3,4,1,64,128]{4,3,2,1,0:T(8,128)(2,1)S(1)} collective-permute-done((bf16[3,4,1,64,128]{4,3,2,1,0:T(8,128)(2,1)S(1)}, bf16[3,4,1,64,128]{4,3,2,1,0:T(8,128)(2,1)S(1)}, u32[]{:S(2)}, u32[]{:S(2)}) %collective-permute-start.5) | collective-permute-done | bytes 196640 | tf_op jit(solution)/shard_map/while/body/eval_jaxpr/ppermute | solution.py:12
  141.6 6.0 %collective-permute-start.8 = (bf16[4,2,64,128]{3,2,1,0:T(8,128)(2,1)S(1)}, bf16[4,2,64,128]{3,2,1,0:T(8,128)(2,1)S(1)}, u32[]{:S(2)}, u32[]{:S(2)}) collective-permute-start(bf16[4,2,64,128]{3,2,1,0:T(8,128)(2,1)S(1)} %get-tuple-element.758), channel_id=1, source_target_pairs={{64,0},{65,1},{66,2},{67,3},{68,4},{69,5},{70,6},{71,7},{72,8},{73... | collective-permute-start | bytes 393224 | tf_op jit(solution)/shard_map/while/body/eval_jaxpr/ppermute | solution.py:23
  166.4 6.1 %collective-permute-done.1 = bf16[3,4,1,64,128]{4,3,2,1,0:T(8,128)(2,1)S(1)} collective-permute-done((bf16[3,4,1,64,128]{4,3,2,1,0:T(8,128)(2,1)S(1)}, bf16[3,4,1,64,128]{4,3,2,1,0:T(8,128)(2,1)S(1)}, u32[]{:S(2)}, u32[]{:S(2)}) %collective-permute-start.1) | collective-permute-done | bytes 196640 | tf_op jit(solution)/shard_map/while/body/eval_jaxpr/ppermute | solution.py:12
  183.9 6.1 %collective-permute-done.3 = bf16[4,1,128,128]{3,2,1,0:T(8,128)(2,1)S(1)} collective-permute-done((bf16[4,1,128,128]{3,2,1,0:T(8,128)(2,1)S(1)}, bf16[4,1,128,128]{3,2,1,0:T(8,128)(2,1)S(1)}, u32[]{:S(2)}, u32[]{:S(2)}) %collective-permute-start.3) | collective-permute-done | bytes 131104 | tf_op jit(solution)/shard_map/while/body/eval_jaxpr/ppermute | solution.py:12
  199.2 6.1 %collective-permute-done.5 = bf16[3,4,1,64,128]{4,3,2,1,0:T(8,128)(2,1)S(1)} collective-permute-done((bf16[3,4,1,64,128]{4,3,2,1,0:T(8,128)(2,1)S(1)}, bf16[3,4,1,64,128]{4,3,2,1,0:T(8,128)(2,1)S(1)}, u32[]{:S(2)}, u32[]{:S(2)}) %collective-permute-start.5) | collective-permute-done | bytes 196640 | tf_op jit(solution)/shard_map/while/body/eval_jaxpr/ppermute | solution.py:12
  216.1 6.0 %collective-permute-start.8 = (bf16[4,2,64,128]{3,2,1,0:T(8,128)(2,1)S(1)}, bf16[4,2,64,128]{3,2,1,0:T(8,128)(2,1)S(1)}, u32[]{:S(2)}, u32[]{:S(2)}) collective-permute-start(bf16[4,2,64,128]{3,2,1,0:T(8,128)(2,1)S(1)} %get-tuple-element.758), channel_id=1, source_target_pairs={{64,0},{65,1},{66,2},{67,3},{68,4},{69,5},{70,6},{71,7},{72,8},{73... | collective-permute-start | bytes 393224 | tf_op jit(solution)/shard_map/while/body/eval_jaxpr/ppermute | solution.py:23
  240.9 6.1 %collective-permute-done.1 = bf16[3,4,1,64,128]{4,3,2,1,0:T(8,128)(2,1)S(1)} collective-permute-done((bf16[3,4,1,64,128]{4,3,2,1,0:T(8,128)(2,1)S(1)}, bf16[3,4,1,64,128]{4,3,2,1,0:T(8,128)(2,1)S(1)}, u32[]{:S(2)}, u32[]{:S(2)}) %collective-permute-start.1) | collective-permute-done | bytes 196640 | tf_op jit(solution)/shard_map/while/body/eval_jaxpr/ppermute | solution.py:12
  258.4 6.1 %collective-permute-done.3 = bf16[4,1,128,128]{3,2,1,0:T(8,128)(2,1)S(1)} collective-permute-done((bf16[4,1,128,128]{3,2,1,0:T(8,128)(2,1)S(1)}, bf16[4,1,128,128]{3,2,1,0:T(8,128)(2,1)S(1)}, u32[]{:S(2)}, u32[]{:S(2)}) %collective-permute-start.3) | collective-permute-done | bytes 131104 | tf_op jit(solution)/shard_map/while/body/eval_jaxpr/ppermute | solution.py:12
  273.7 6.1 %collective-permute-done.5 = bf16[3,4,1,64,128]{4,3,2,1,0:T(8,128)(2,1)S(1)} collective-permute-done((bf16[3,4,1,64,128]{4,3,2,1,0:T(8,128)(2,1)S(1)}, bf16[3,4,1,64,128]{4,3,2,1,0:T(8,128)(2,1)S(1)}, u32[]{:S(2)}, u32[]{:S(2)}) %collective-permute-start.5) | collective-permute-done | bytes 196640 | tf_op jit(solution)/shard_map/while/body/eval_jaxpr/ppermute | solution.py:12
  290.6 6.0 %collective-permute-start.8 = (bf16[4,2,64,128]{3,2,1,0:T(8,128)(2,1)S(1)}, bf16[4,2,64,128]{3,2,1,0:T(8,128)(2,1)S(1)}, u32[]{:S(2)}, u32[]{:S(2)}) collective-permute-start(bf16[4,2,64,128]{3,2,1,0:T(8,128)(2,1)S(1)} %get-tuple-element.758), channel_id=1, source_target_pairs={{64,0},{65,1},{66,2},{67,3},{68,4},{69,5},{70,6},{71,7},{72,8},{73... | collective-permute-start | bytes 393224 | tf_op jit(solution)/shard_map/while/body/eval_jaxpr/ppermute | solution.py:23
  315.4 6.1 %collective-permute-done.1 = bf16[3,4,1,64,128]{4,3,2,1,0:T(8,128)(2,1)S(1)} collective-permute-done((bf16[3,4,1,64,128]{4,3,2,1,0:T(8,128)(2,1)S(1)}, bf16[3,4,1,64,128]{4,3,2,1,0:T(8,128)(2,1)S(1)}, u32[]{:S(2)}, u32[]{:S(2)}) %collective-permute-start.1) | collective-permute-done | bytes 196640 | tf_op jit(solution)/shard_map/while/body/eval_jaxpr/ppermute | solution.py:12
  332.9 6.1 %collective-permute-done.3 = bf16[4,1,128,128]{3,2,1,0:T(8,128)(2,1)S(1)} collective-permute-done((bf16[4,1,128,128]{3,2,1,0:T(8,128)(2,1)S(1)}, bf16[4,1,128,128]{3,2,1,0:T(8,128)(2,1)S(1)}, u32[]{:S(2)}, u32[]{:S(2)}) %collective-permute-start.3) | collective-permute-done | bytes 131104 | tf_op jit(solution)/shard_map/while/body/eval_jaxpr/ppermute | solution.py:12
  348.2 6.1 %collective-permute-done.5 = bf16[3,4,1,64,128]{4,3,2,1,0:T(8,128)(2,1)S(1)} collective-permute-done((bf16[3,4,1,64,128]{4,3,2,1,0:T(8,128)(2,1)S(1)}, bf16[3,4,1,64,128]{4,3,2,1,0:T(8,128)(2,1)S(1)}, u32[]{:S(2)}, u32[]{:S(2)}) %collective-permute-start.5) | collective-permute-done | bytes 196640 | tf_op jit(solution)/shard_map/while/body/eval_jaxpr/ppermute | solution.py:12
  389.9 6.1 %collective-permute-done.1 = bf16[3,4,1,64,128]{4,3,2,1,0:T(8,128)(2,1)S(1)} collective-permute-done((bf16[3,4,1,64,128]{4,3,2,1,0:T(8,128)(2,1)S(1)}, bf16[3,4,1,64,128]{4,3,2,1,0:T(8,128)(2,1)S(1)}, u32[]{:S(2)}, u32[]{:S(2)}) %collective-permute-start.1) | collective-permute-done | bytes 196640 | tf_op jit(solution)/shard_map/while/body/eval_jaxpr/ppermute | solution.py:12
  407.4 6.1 %collective-permute-done.3 = bf16[4,1,128,128]{3,2,1,0:T(8,128)(2,1)S(1)} collective-permute-done((bf16[4,1,128,128]{3,2,1,0:T(8,128)(2,1)S(1)}, bf16[4,1,128,128]{3,2,1,0:T(8,128)(2,1)S(1)}, u32[]{:S(2)}, u32[]{:S(2)}) %collective-permute-start.3) | collective-permute-done | bytes 131104 | tf_op jit(solution)/shard_map/while/body/eval_jaxpr/ppermute | solution.py:12
  422.7 6.1 %collective-permute-done.5 = bf16[3,4,1,64,128]{4,3,2,1,0:T(8,128)(2,1)S(1)} collective-permute-done((bf16[3,4,1,64,128]{4,3,2,1,0:T(8,128)(2,1)S(1)}, bf16[3,4,1,64,128]{4,3,2,1,0:T(8,128)(2,1)S(1)}, u32[]{:S(2)}, u32[]{:S(2)}) %collective-permute-start.5) | collective-permute-done | bytes 196640 | tf_op jit(solution)/shard_map/while/body/eval_jaxpr/ppermute | solution.py:12
  (877 shorter events, 303.9 us)
Async XLA Ops:
  3.2 11.6 %collective-permute-start = (bf16[3,4,1,64,128]{4,3,2,1,0:T(8,128)(2,1)S(1)}, bf16[3,4,1,64,128]{4,3,2,1,0:T(8,128)(2,1)S(1)}, u32[]{:S(2)}, u32[]{:S(2)}) collective-permute-start(bf16[3,4,1,64,128]{4,3,2,1,0:T(8,128)(2,1)S(1)} %get-tuple-element.705), channel_id=1, source_target_pairs={{1,0},{2,1},{3,2},{4,3},{5,4},{6,5},{7,6},{8,7},{9,8},{10,9},{11,1... | collective-permute-start | bytes 589832 | tf_op jit(solution)/shard_map/while/body/eval_jaxpr/ppermute | solution.py:15
  11.3 11.6 %collective-permute-start.1 = (bf16[3,4,1,64,128]{4,3,2,1,0:T(8,128)(2,1)S(1)}, bf16[3,4,1,64,128]{4,3,2,1,0:T(8,128)(2,1)S(1)}, u32[]{:S(2)}, u32[]{:S(2)}) collective-permute-start(bf16[3,4,1,64,128]{4,3,2,1,0:T(8,128)(2,1)S(1)} %get-tuple-element.706), channel_id=1, source_target_pairs={{0,1},{1,2},{2,3},{3,4},{4,5},{5,6},{6,7},{7,8},{8,9},{9,10},{10,1... | collective-permute-start | bytes 589832 | tf_op jit(solution)/shard_map/while/body/eval_jaxpr/ppermute | solution.py:12
  30.6 9.9 %collective-permute-start.3 = (bf16[4,1,128,128]{3,2,1,0:T(8,128)(2,1)S(1)}, bf16[4,1,128,128]{3,2,1,0:T(8,128)(2,1)S(1)}, u32[]{:S(2)}, u32[]{:S(2)}) collective-permute-start(bf16[4,1,128,128]{3,2,1,0:T(8,128)(2,1)S(1)} %get-tuple-element.731), channel_id=1, source_target_pairs={{0,1},{1,2},{2,3},{3,4},{4,5},{5,6},{6,7},{7,8},{8,9},{9,10},{10,1... | collective-permute-start | bytes 393224 | tf_op jit(solution)/shard_map/while/body/eval_jaxpr/ppermute | solution.py:12
  45.2 10.6 %collective-permute-start.5 = (bf16[3,4,1,64,128]{4,3,2,1,0:T(8,128)(2,1)S(1)}, bf16[3,4,1,64,128]{4,3,2,1,0:T(8,128)(2,1)S(1)}, u32[]{:S(2)}, u32[]{:S(2)}) collective-permute-start(bf16[3,4,1,64,128]{4,3,2,1,0:T(8,128)(2,1)S(1)} %get-tuple-element.743), channel_id=1, source_target_pairs={{0,1},{1,2},{2,3},{3,4},{4,5},{5,6},{6,7},{7,8},{8,9},{9,10},{10,1... | collective-permute-start | bytes 589832 | tf_op jit(solution)/shard_map/while/body/eval_jaxpr/ppermute | solution.py:12
  61.0 12.2 %collective-permute-start.6 = (bf16[4,1,128,128]{3,2,1,0:T(8,128)(2,1)S(1)}, bf16[4,1,128,128]{3,2,1,0:T(8,128)(2,1)S(1)}, u32[]{:S(2)}, u32[]{:S(2)}) collective-permute-start(bf16[4,1,128,128]{3,2,1,0:T(8,128)(2,1)S(1)} %get-tuple-element.766), channel_id=1, source_target_pairs={{1,0},{2,1},{3,2},{4,3},{5,4},{6,5},{7,6},{8,7},{9,8},{10,9},{11,1... | collective-permute-start | bytes 393224 | tf_op jit(solution)/shard_map/while/body/eval_jaxpr/ppermute | solution.py:15
  63.0 10.3 %collective-permute-start.7 = (bf16[4,1,128,128]{3,2,1,0:T(8,128)(2,1)S(1)}, bf16[4,1,128,128]{3,2,1,0:T(8,128)(2,1)S(1)}, u32[]{:S(2)}, u32[]{:S(2)}) collective-permute-start(bf16[4,1,128,128]{3,2,1,0:T(8,128)(2,1)S(1)} %get-tuple-element.767), channel_id=1, source_target_pairs={{0,1},{1,2},{2,3},{3,4},{4,5},{5,6},{6,7},{7,8},{8,9},{9,10},{10,1... | collective-permute-start | bytes 393224 | tf_op jit(solution)/shard_map/while/body/eval_jaxpr/ppermute | solution.py:12
  66.5 10.2 %collective-permute-start.8 = (bf16[4,2,64,128]{3,2,1,0:T(8,128)(2,1)S(1)}, bf16[4,2,64,128]{3,2,1,0:T(8,128)(2,1)S(1)}, u32[]{:S(2)}, u32[]{:S(2)}) collective-permute-start(bf16[4,2,64,128]{3,2,1,0:T(8,128)(2,1)S(1)} %get-tuple-element.758), channel_id=1, source_target_pairs={{64,0},{65,1},{66,2},{67,3},{68,4},{69,5},{70,6},{71,7},{72,8},{73... | collective-permute-start | bytes 393224 | tf_op jit(solution)/shard_map/while/body/eval_jaxpr/ppermute | solution.py:23
  85.8 12.2 %collective-permute-start.1 = (bf16[3,4,1,64,128]{4,3,2,1,0:T(8,128)(2,1)S(1)}, bf16[3,4,1,64,128]{4,3,2,1,0:T(8,128)(2,1)S(1)}, u32[]{:S(2)}, u32[]{:S(2)}) collective-permute-start(bf16[3,4,1,64,128]{4,3,2,1,0:T(8,128)(2,1)S(1)} %get-tuple-element.706), channel_id=1, source_target_pairs={{0,1},{1,2},{2,3},{3,4},{4,5},{5,6},{6,7},{7,8},{8,9},{9,10},{10,1... | collective-permute-start | bytes 589832 | tf_op jit(solution)/shard_map/while/body/eval_jaxpr/ppermute | solution.py:12
  105.7 9.9 %collective-permute-start.3 = (bf16[4,1,128,128]{3,2,1,0:T(8,128)(2,1)S(1)}, bf16[4,1,128,128]{3,2,1,0:T(8,128)(2,1)S(1)}, u32[]{:S(2)}, u32[]{:S(2)}) collective-permute-start(bf16[4,1,128,128]{3,2,1,0:T(8,128)(2,1)S(1)} %get-tuple-element.731), channel_id=1, source_target_pairs={{0,1},{1,2},{2,3},{3,4},{4,5},{5,6},{6,7},{7,8},{8,9},{9,10},{10,1... | collective-permute-start | bytes 393224 | tf_op jit(solution)/shard_map/while/body/eval_jaxpr/ppermute | solution.py:12
  120.2 10.6 %collective-permute-start.5 = (bf16[3,4,1,64,128]{4,3,2,1,0:T(8,128)(2,1)S(1)}, bf16[3,4,1,64,128]{4,3,2,1,0:T(8,128)(2,1)S(1)}, u32[]{:S(2)}, u32[]{:S(2)}) collective-permute-start(bf16[3,4,1,64,128]{4,3,2,1,0:T(8,128)(2,1)S(1)} %get-tuple-element.743), channel_id=1, source_target_pairs={{0,1},{1,2},{2,3},{3,4},{4,5},{5,6},{6,7},{7,8},{8,9},{9,10},{10,1... | collective-permute-start | bytes 589832 | tf_op jit(solution)/shard_map/while/body/eval_jaxpr/ppermute | solution.py:12
  136.1 11.7 %collective-permute-start.6 = (bf16[4,1,128,128]{3,2,1,0:T(8,128)(2,1)S(1)}, bf16[4,1,128,128]{3,2,1,0:T(8,128)(2,1)S(1)}, u32[]{:S(2)}, u32[]{:S(2)}) collective-permute-start(bf16[4,1,128,128]{3,2,1,0:T(8,128)(2,1)S(1)} %get-tuple-element.766), channel_id=1, source_target_pairs={{1,0},{2,1},{3,2},{4,3},{5,4},{6,5},{7,6},{8,7},{9,8},{10,9},{11,1... | collective-permute-start | bytes 393224 | tf_op jit(solution)/shard_map/while/body/eval_jaxpr/ppermute | solution.py:15
  138.0 9.9 %collective-permute-start.7 = (bf16[4,1,128,128]{3,2,1,0:T(8,128)(2,1)S(1)}, bf16[4,1,128,128]{3,2,1,0:T(8,128)(2,1)S(1)}, u32[]{:S(2)}, u32[]{:S(2)}) collective-permute-start(bf16[4,1,128,128]{3,2,1,0:T(8,128)(2,1)S(1)} %get-tuple-element.767), channel_id=1, source_target_pairs={{0,1},{1,2},{2,3},{3,4},{4,5},{5,6},{6,7},{7,8},{8,9},{9,10},{10,1... | collective-permute-start | bytes 393224 | tf_op jit(solution)/shard_map/while/body/eval_jaxpr/ppermute | solution.py:12
  160.3 12.2 %collective-permute-start.1 = (bf16[3,4,1,64,128]{4,3,2,1,0:T(8,128)(2,1)S(1)}, bf16[3,4,1,64,128]{4,3,2,1,0:T(8,128)(2,1)S(1)}, u32[]{:S(2)}, u32[]{:S(2)}) collective-permute-start(bf16[3,4,1,64,128]{4,3,2,1,0:T(8,128)(2,1)S(1)} %get-tuple-element.706), channel_id=1, source_target_pairs={{0,1},{1,2},{2,3},{3,4},{4,5},{5,6},{6,7},{7,8},{8,9},{9,10},{10,1... | collective-permute-start | bytes 589832 | tf_op jit(solution)/shard_map/while/body/eval_jaxpr/ppermute | solution.py:12
  194.7 10.6 %collective-permute-start.5 = (bf16[3,4,1,64,128]{4,3,2,1,0:T(8,128)(2,1)S(1)}, bf16[3,4,1,64,128]{4,3,2,1,0:T(8,128)(2,1)S(1)}, u32[]{:S(2)}, u32[]{:S(2)}) collective-permute-start(bf16[3,4,1,64,128]{4,3,2,1,0:T(8,128)(2,1)S(1)} %get-tuple-element.743), channel_id=1, source_target_pairs={{0,1},{1,2},{2,3},{3,4},{4,5},{5,6},{6,7},{7,8},{8,9},{9,10},{10,1... | collective-permute-start | bytes 589832 | tf_op jit(solution)/shard_map/while/body/eval_jaxpr/ppermute | solution.py:12
  210.6 11.7 %collective-permute-start.6 = (bf16[4,1,128,128]{3,2,1,0:T(8,128)(2,1)S(1)}, bf16[4,1,128,128]{3,2,1,0:T(8,128)(2,1)S(1)}, u32[]{:S(2)}, u32[]{:S(2)}) collective-permute-start(bf16[4,1,128,128]{3,2,1,0:T(8,128)(2,1)S(1)} %get-tuple-element.766), channel_id=1, source_target_pairs={{1,0},{2,1},{3,2},{4,3},{5,4},{6,5},{7,6},{8,7},{9,8},{10,9},{11,1... | collective-permute-start | bytes 393224 | tf_op jit(solution)/shard_map/while/body/eval_jaxpr/ppermute | solution.py:15
  234.8 12.2 %collective-permute-start.1 = (bf16[3,4,1,64,128]{4,3,2,1,0:T(8,128)(2,1)S(1)}, bf16[3,4,1,64,128]{4,3,2,1,0:T(8,128)(2,1)S(1)}, u32[]{:S(2)}, u32[]{:S(2)}) collective-permute-start(bf16[3,4,1,64,128]{4,3,2,1,0:T(8,128)(2,1)S(1)} %get-tuple-element.706), channel_id=1, source_target_pairs={{0,1},{1,2},{2,3},{3,4},{4,5},{5,6},{6,7},{7,8},{8,9},{9,10},{10,1... | collective-permute-start | bytes 589832 | tf_op jit(solution)/shard_map/while/body/eval_jaxpr/ppermute | solution.py:12
  269.2 10.6 %collective-permute-start.5 = (bf16[3,4,1,64,128]{4,3,2,1,0:T(8,128)(2,1)S(1)}, bf16[3,4,1,64,128]{4,3,2,1,0:T(8,128)(2,1)S(1)}, u32[]{:S(2)}, u32[]{:S(2)}) collective-permute-start(bf16[3,4,1,64,128]{4,3,2,1,0:T(8,128)(2,1)S(1)} %get-tuple-element.743), channel_id=1, source_target_pairs={{0,1},{1,2},{2,3},{3,4},{4,5},{5,6},{6,7},{7,8},{8,9},{9,10},{10,1... | collective-permute-start | bytes 589832 | tf_op jit(solution)/shard_map/while/body/eval_jaxpr/ppermute | solution.py:12
  285.1 11.7 %collective-permute-start.6 = (bf16[4,1,128,128]{3,2,1,0:T(8,128)(2,1)S(1)}, bf16[4,1,128,128]{3,2,1,0:T(8,128)(2,1)S(1)}, u32[]{:S(2)}, u32[]{:S(2)}) collective-permute-start(bf16[4,1,128,128]{3,2,1,0:T(8,128)(2,1)S(1)} %get-tuple-element.766), channel_id=1, source_target_pairs={{1,0},{2,1},{3,2},{4,3},{5,4},{6,5},{7,6},{8,7},{9,8},{10,9},{11,1... | collective-permute-start | bytes 393224 | tf_op jit(solution)/shard_map/while/body/eval_jaxpr/ppermute | solution.py:15
  309.3 12.2 %collective-permute-start.1 = (bf16[3,4,1,64,128]{4,3,2,1,0:T(8,128)(2,1)S(1)}, bf16[3,4,1,64,128]{4,3,2,1,0:T(8,128)(2,1)S(1)}, u32[]{:S(2)}, u32[]{:S(2)}) collective-permute-start(bf16[3,4,1,64,128]{4,3,2,1,0:T(8,128)(2,1)S(1)} %get-tuple-element.706), channel_id=1, source_target_pairs={{0,1},{1,2},{2,3},{3,4},{4,5},{5,6},{6,7},{7,8},{8,9},{9,10},{10,1... | collective-permute-start | bytes 589832 | tf_op jit(solution)/shard_map/while/body/eval_jaxpr/ppermute | solution.py:12
  343.7 10.6 %collective-permute-start.5 = (bf16[3,4,1,64,128]{4,3,2,1,0:T(8,128)(2,1)S(1)}, bf16[3,4,1,64,128]{4,3,2,1,0:T(8,128)(2,1)S(1)}, u32[]{:S(2)}, u32[]{:S(2)}) collective-permute-start(bf16[3,4,1,64,128]{4,3,2,1,0:T(8,128)(2,1)S(1)} %get-tuple-element.743), channel_id=1, source_target_pairs={{0,1},{1,2},{2,3},{3,4},{4,5},{5,6},{6,7},{7,8},{8,9},{9,10},{10,1... | collective-permute-start | bytes 589832 | tf_op jit(solution)/shard_map/while/body/eval_jaxpr/ppermute | solution.py:12
  359.6 11.7 %collective-permute-start.6 = (bf16[4,1,128,128]{3,2,1,0:T(8,128)(2,1)S(1)}, bf16[4,1,128,128]{3,2,1,0:T(8,128)(2,1)S(1)}, u32[]{:S(2)}, u32[]{:S(2)}) collective-permute-start(bf16[4,1,128,128]{3,2,1,0:T(8,128)(2,1)S(1)} %get-tuple-element.766), channel_id=1, source_target_pairs={{1,0},{2,1},{3,2},{4,3},{5,4},{6,5},{7,6},{8,7},{9,8},{10,9},{11,1... | collective-permute-start | bytes 393224 | tf_op jit(solution)/shard_map/while/body/eval_jaxpr/ppermute | solution.py:15
  383.8 12.2 %collective-permute-start.1 = (bf16[3,4,1,64,128]{4,3,2,1,0:T(8,128)(2,1)S(1)}, bf16[3,4,1,64,128]{4,3,2,1,0:T(8,128)(2,1)S(1)}, u32[]{:S(2)}, u32[]{:S(2)}) collective-permute-start(bf16[3,4,1,64,128]{4,3,2,1,0:T(8,128)(2,1)S(1)} %get-tuple-element.706), channel_id=1, source_target_pairs={{0,1},{1,2},{2,3},{3,4},{4,5},{5,6},{6,7},{7,8},{8,9},{9,10},{10,1... | collective-permute-start | bytes 589832 | tf_op jit(solution)/shard_map/while/body/eval_jaxpr/ppermute | solution.py:12
  418.2 10.6 %collective-permute-start.5 = (bf16[3,4,1,64,128]{4,3,2,1,0:T(8,128)(2,1)S(1)}, bf16[3,4,1,64,128]{4,3,2,1,0:T(8,128)(2,1)S(1)}, u32[]{:S(2)}, u32[]{:S(2)}) collective-permute-start(bf16[3,4,1,64,128]{4,3,2,1,0:T(8,128)(2,1)S(1)} %get-tuple-element.743), channel_id=1, source_target_pairs={{0,1},{1,2},{2,3},{3,4},{4,5},{5,6},{6,7},{7,8},{8,9},{9,10},{10,1... | collective-permute-start | bytes 589832 | tf_op jit(solution)/shard_map/while/body/eval_jaxpr/ppermute | solution.py:12
  434.1 11.7 %collective-permute-start.6 = (bf16[4,1,128,128]{3,2,1,0:T(8,128)(2,1)S(1)}, bf16[4,1,128,128]{3,2,1,0:T(8,128)(2,1)S(1)}, u32[]{:S(2)}, u32[]{:S(2)}) collective-permute-start(bf16[4,1,128,128]{3,2,1,0:T(8,128)(2,1)S(1)} %get-tuple-element.766), channel_id=1, source_target_pairs={{1,0},{2,1},{3,2},{4,3},{5,4},{6,5},{7,6},{8,7},{9,8},{10,9},{11,1... | collective-permute-start | bytes 393224 | tf_op jit(solution)/shard_map/while/body/eval_jaxpr/ppermute | solution.py:15
  (61 other events, 310.5 us)
where the time goes:
time: 458 us; the launch traced here: 456 us
  starting transfers between devices  176 us (38%)
  waiting for transfers between devices  169 us (37%)
  local copies, waits for them, and re-layouts  52.1 us (11%)
  matrix products  33.6 us (7%)
  other arithmetic  17.5 us (4%)
  loops' own time  6.37 us (1%)
    ppermute x24, waiting for transfers between devices, with_halo(): lax.ppermute(lax.slice_in_dim(block, block.shape[dim] - width, None, axis...  113 us
    ppermute x24, starting transfers between devices, with_halo(): lax.ppermute(lax.slice_in_dim(block, block.shape[dim] - width, None, axis...  78.3 us
    ppermute x24, starting transfers between devices, with_halo(): lax.ppermute(lax.slice_in_dim(block, 0, width, axis=dim), axis, backward)  53.2 us
    ppermute x12, starting transfers between devices, shifted(): return lax.ppermute(block, axis, route)  44.6 us
    while x432, local copies, waits for them, and re-layouts  34.6 us
    ppermute x12, waiting for transfers between devices, shifted(): return lax.ppermute(block, axis, route)  33.9 us
    dot_general x48, matrix products, convolve(): jnp.einsum('ko,brkw->brow', weight, taps, preferred_element_type=jnp.floa...  31.5 us
    ppermute x24, waiting for transfers between devices, with_halo(): lax.ppermute(lax.slice_in_dim(block, 0, width, axis=dim), axis, backward)  22.7 us
  transfers between devices with their start and end apart: 60, of which 41 were waited for; matrix products, arithmetic and copies ran while one was open for 4% of the time, Pallas kernels for 0%

commit v1 on v0

v1 whole, which is shorter than its diff:
```python
import functools

import jax
import jax.numpy as jnp
from jax import lax
from jax.experimental import pallas as pl
from jax.experimental.pallas import tpu as pltpu
from jax.sharding import PartitionSpec as P

CH = 64
GW = 128
OWN = 4
BF = jnp.bfloat16
F32 = jnp.float32

RUN = {"HT": (0, 4), "M": (4, 4), "HB": (8, 4), "CB": (12, 3), "CT": (15, 1)}
RUN_UNITS = 16
FIRST_A = {"HT": (0, 2), "M": (2, 4), "HB": (6, 4), "CB": (10, 3), "CT": (13, 1), "F0": (14, 4)}
FIRST_B = {"HT": (0, 2), "HB": (2, 4), "CB": (6, 3), "CT": (9, 1), "F1": (10, 4), "F2": (14, 4)}


def sigmoid(v):
    return 0.5 * jnp.tanh(0.5 * v) + 0.5


def taps_of(row):
    lane = lax.broadcasted_iota(jnp.int32, row.shape, 1)
    zero = jnp.zeros_like(row)
    before = jnp.where(lane == 0, zero, pltpu.roll(row, 1, 1))
    after = jnp.where(lane == GW - 1, zero, pltpu.roll(row, GW - 1, 1))
    return jnp.concatenate([before, row, after], axis=0)


def phase_kernel(plan, last, *refs):
    names = plan["names"]
    n_in = len(names)
    ref = dict(zip(names, refs[:n_in]))
    rest = list(refs[n_in:])
    state_out = rest.pop(0)
    if not last:
        near_out = rest.pop(0)
        far_out = rest.pop(0)
    tx, th, tm, tx2, th2, tm2, yb, ob = rest
    core = ref["sc"][0]
    top = ref["sc"][1]
    first_core = core == 0

    def valid(row):
        g = top + row
        return jnp.logical_and(g >= 0, g < 128)

    def keep(row, value):
        return jnp.where(valid(row), value, jnp.zeros_like(value))

    def fetch(field, row):
        own, (near, far, offset, count) = plan["fields"][field]
        if 0 <= row < OWN:
            return ref[own[0]][own[1], row] if own[1] is not None else ref[own[0]][row]
        if row < 0:
            unit = offset + count + row
            value = jnp.where(first_core, ref[far][unit], ref[near][unit])
        else:
            unit = offset + row - OWN
            value = jnp.where(first_core, ref[near][unit], ref[far][unit])
        return keep(row, value)

    def fill(buf, field, reach):
        for i, row in enumerate(range(-reach, OWN + reach)):
            buf[i] = taps_of(fetch(field, row))

    def cell(index, reach, bx, bh, bm, cell_prev, memory_prev, on_cell, on_memory, on_hidden, bm_next):
        w1 = ref["w1"][index]
        w2 = ref["w2"][index]
        wo = ref["wo"][index]
        rows = list(range(-reach, OWN + reach))
        for q in range(0, len(rows), 2):
            cols_1, cols_2 = [], []
            for i in (q, q + 1):
                x_part = [bx[i + a] for a in range(3)]
                cols_1.append(jnp.concatenate(x_part + [bh[i + a] for a in range(3)], axis=0))
                cols_2.append(jnp.concatenate(x_part + [bm[i + a] for a in range(3)], axis=0))
            acc1 = jnp.dot(w1, jnp.concatenate(cols_1, axis=1), preferred_element_type=F32)
            acc2 = jnp.dot(w2, jnp.concatenate(cols_2, axis=1), preferred_element_type=F32)
            c_prev = jnp.concatenate([cell_prev(rows[q]), cell_prev(rows[q + 1])], axis=1).astype(F32)
            m_prev = jnp.concatenate([memory_prev(rows[q]), memory_prev(rows[q + 1])], axis=1).astype(F32)
            c_new = sigmoid(acc1[64:128] + 1.0) * c_prev + sigmoid(acc1[0:64]) * jnp.tanh(acc1[128:192])
            m_new = sigmoid(acc2[64:128] + 1.0) * m_prev + sigmoid(acc2[0:64]) * jnp.tanh(acc2[128:192])
            c_new = c_new.astype(BF)
            m_new = m_new.astype(BF)
            ob[:, q * GW : (q + 2) * GW] = acc1[192:256]
            pair = []
            for j in range(2):
                row = rows[q + j]
                c_row = c_new[:, j * GW : (j + 1) * GW]
                m_row = m_new[:, j * GW : (j + 1) * GW]
                if not 0 <= row < OWN:
                    c_row = keep(row, c_row)
                    m_row = keep(row, m_row)
                on_cell(row, c_row)
                on_memory(row, m_row)
                m_taps = taps_of(m_row)
                if bm_next is not None:
                    bm_next[q + j] = m_taps
                pair.append(jnp.concatenate([taps_of(c_row), m_taps], axis=0))
            yb[:, q * GW : (q + 2) * GW] = jnp.dot(
                wo, jnp.concatenate(pair, axis=1), preferred_element_type=F32
            )
        for q in range(1, len(rows) - 1):
            lanes = slice(q * GW, (q + 1) * GW)
            gate = (
                ob[:, lanes]
                + yb[0:64, (q - 1) * GW : q * GW]
                + yb[64:128, lanes]
                + yb[128:192, (q + 1) * GW : (q + 2) * GW]
            )
            h_new = (sigmoid(gate) * jnp.tanh(yb[192:256, lanes])).astype(BF)
            row = rows[q]
            if not 0 <= row < OWN:
                h_new = keep(row, h_new)
            on_hidden(row, h_new)

    fill(tx, "X", 4)
    fill(th, "HB", 4)
    fill(tm, "M", 4)
    fill(th2, "HT", 2)

    def put(slot):
        def store(row, value):
            if 0 <= row < OWN:
                state_out[slot, row] = value

        return store

    def hidden_first(row, value):
        tx2[row + 2] = taps_of(value)
        if 0 <= row < OWN:
            state_out[0, row] = value

    def nothing(row, value):
        del row, value

    cell(
        0, 3, tx, th, tm,
        lambda row: fetch("CB", row),
        lambda row: fetch("M", row),
        put(2), nothing, hidden_first, tm2,
    )
    tm2_in = tm2.at[1:9]
    cell(
        1, 1, tx2, th2, tm2_in,
        lambda row: fetch("CT", row),
        lambda row: tm2[row + 3, 64:128],
        put(3), put(4), put(1), None,
    )
    if not last:
        for field, slot in (("HT", 1), ("M", 4), ("HB", 0), ("CB", 2), ("CT", 3)):
            offset, count = RUN[field]
            for u in range(count):
                low = state_out[slot, u]
                high = state_out[slot, OWN - count + u]
                near_out[offset + u] = jnp.where(first_core, high, low)
                far_out[offset + u] = jnp.where(first_core, low, high)


def run_phase(operands, plan, last):
    names = list(operands)
    plan = dict(plan, names=names)
    unit = (CH, GW)
    out_shape = [jax.ShapeDtypeStruct((5, OWN) + unit, BF)]
    if not last:
        out_shape += [jax.ShapeDtypeStruct((RUN_UNITS,) + unit, BF)] * 2
    in_specs = [
        pl.BlockSpec(memory_space=pltpu.SMEM if name == "sc" else pltpu.VMEM) for name in names
    ]
    out_specs = [pl.BlockSpec(memory_space=pltpu.VMEM) for _ in out_shape]
    return pl.pallas_call(
        functools.partial(phase_kernel, plan, last),
        out_shape=out_shape,
        in_specs=in_specs,
        out_specs=out_specs,
        scratch_shapes=[
            pltpu.VMEM((12, 3 * CH, GW), BF),
            pltpu.VMEM((12, 3 * CH, GW), BF),
            pltpu.VMEM((12, 3 * CH, GW), BF),
            pltpu.VMEM((8, 3 * CH, GW), BF),
            pltpu.VMEM((8, 3 * CH, GW), BF),
            pltpu.VMEM((10, 3 * CH, GW), BF),
            pltpu.VMEM((4 * CH, 10 * GW), F32),
            pltpu.VMEM((CH, 10 * GW), F32),
        ],
        compiler_params=pltpu.CompilerParams(vmem_limit_bytes=24 << 20),
        name="two_layers_last" if last else "two_layers",
    )(*[operands[name] for name in names])


def prepare_weights(w_x, w_h, w_m, w_o, w_last):
    layers = w_x.shape[0]
    x = jnp.swapaxes(w_x, 1, 2)
    x_c = jnp.concatenate([x[:, 0:192], x[:, 384:448]], axis=1)
    w1 = jnp.concatenate([x_c, jnp.swapaxes(w_h, 1, 2)], axis=2)
    w2 = jnp.concatenate([x[:, 192:384], jnp.swapaxes(w_m, 1, 2)], axis=2)
    o = w_o.reshape(layers, 3, 3, 2, CH, CH).transpose(0, 1, 5, 3, 2, 4).reshape(layers, 192, 384)
    last = w_last.reshape(layers, 2, CH, CH).transpose(0, 3, 1, 2)
    mix = jnp.zeros((layers, CH, 2, 3, CH), BF).at[:, :, :, 1].set(last).reshape(layers, CH, 384)
    return w1, w2, jnp.concatenate([o, mix], axis=1)


def on_device(frames, hidden_in, cell_in, memory_in, w_x, w_h, w_m, w_o, w_last):
    core = lax.axis_index("layer")
    chip = lax.axis_index("rows")
    lower = core == 0
    chips = lax.axis_size("rows")
    swap = [(0, 1), (1, 0)]
    groups = [[4 * i + j for j in range(4)] for i in range(chips // 4)]
    across = []
    for i in range(chips):
        across.append((chips + i, (i + 4) % chips))
        across.append((i, chips + (i - 4) % chips))

    def to_partner(value):
        return lax.ppermute(value, "layer", swap)

    def to_neighbour(value):
        return lax.ppermute(value, ("layer", "rows"), across)

    own_w = prepare_weights(w_x, w_h, w_m, w_o, w_last)
    other_w = [to_partner(w) for w in own_w]
    w_low = [jnp.where(lower, a, b) for a, b in zip(own_w, other_w)]
    w_high = [jnp.where(lower, b, a) for a, b in zip(own_w, other_w)]

    extra = jnp.where(
        lower,
        jnp.stack([memory_in, frames[0]], axis=1),
        jnp.stack([frames[1], frames[2]], axis=1),
    )
    mine = jnp.concatenate(
        [hidden_in.transpose(1, 0, 2, 3, 4), cell_in.transpose(1, 0, 2, 3, 4), extra], axis=1
    )
    mine = lax.all_to_all(mine, "rows", 0, 0, axis_index_groups=groups, tiled=True)
    mine = mine.transpose(1, 0, 2, 3, 4).reshape(6, 8, CH, GW)
    theirs = to_partner(mine)
    low = jnp.where(lower, mine, theirs)
    high = jnp.where(lower, theirs, mine)
    low_own = lax.dynamic_slice_in_dim(low, 4 * core, OWN, axis=1)
    high_own = lax.dynamic_slice_in_dim(high, 4 * core, OWN, axis=1)
    low_partner = lax.dynamic_slice_in_dim(low, 4 * (1 - core), OWN, axis=1)
    high_partner = lax.dynamic_slice_in_dim(high, 4 * (1 - core), OWN, axis=1)

    def message(stack, order, layout, last_rows):
        parts = []
        for index, name in order:
            count = layout[name][1]
            parts.append(
                jnp.where(last_rows, stack[index, OWN - count :], stack[index, :count])
            )
        return jnp.concatenate(parts, axis=0)

    order_a = ((1, "HT"), (4, "M"), (0, "HB"), (2, "CB"), (3, "CT"), (5, "F0"))
    order_b = ((1, "HT"), (0, "HB"), (2, "CB"), (3, "CT"), (4, "F1"), (5, "F2"))
    upper = jnp.logical_not(lower)
    near_a = message(low_partner, order_a, FIRST_A, upper)
    near_b = message(high_partner, order_b, FIRST_B, upper)
    far_a = to_neighbour(message(low_own, order_a, FIRST_A, upper))
    far_b = to_neighbour(message(high_own, order_b, FIRST_B, upper))

    scalars = jnp.stack([core, 8 * (chip // 4) + 4 * core]).astype(jnp.int32)
    base = {"sc": scalars}
    low_state = ("low_state", low_own)
    high_state = ("high_state", high_own)
    halo_low = {k: ("na", "fa") + FIRST_A[k] for k in ("HB", "HT", "CB", "CT")}
    halo_high = {k: ("nb", "fb") + FIRST_B[k] for k in ("HB", "HT", "CB", "CT")}
    halo_m = ("na", "fa") + FIRST_A["M"]
    own_m = ("low0", 4)
    arrays = {"low0": low_own, "high0": high_own, "na": near_a, "fa": far_a, "nb": near_b, "fb": far_b}
    frame_field = (
        (("low0", 5), ("na", "fa") + FIRST_A["F0"]),
        (("high0", 4), ("nb", "fb") + FIRST_B["F1"]),
        (("high0", 5), ("nb", "fb") + FIRST_B["F2"]),
    )
    low_name, high_name = "low0", "high0"
    low_result = high_result = None
    for step in range(3):
        for half in range(2):
            last = step == 2 and half == 1
            tag = f"{step}{half}"
            state_name = high_name if half else low_name
            halo = halo_high if half else halo_low
            fields = {
                k: ((state_name, slot), halo[k])
                for slot, k in enumerate(("HB", "HT", "CB", "CT"))
            }
            fields["M"] = (own_m, halo_m)
            fields["X"] = x_field if half else frame_field[step]
            needed = {f[0][0] for f in fields.values()} | {n for f in fields.values() for n in f[1][:2]}
            operands = dict(base)
            for name in sorted(needed):
                operands[name] = arrays[name]
            for name, w in zip(("w1", "w2", "wo"), w_high if half else w_low):
                operands[name] = w
            outs = run_phase(operands, {"fields": fields}, last)
            state = outs[0]
            arrays["s" + tag] = state
            if half:
                high_name, high_result = "s" + tag, state
            else:
                low_name, low_result = "s" + tag, state
            own_m = ("s" + tag, 4)
            if not last:
                arrays["n" + tag] = to_partner(outs[1])
                arrays["f" + tag] = to_neighbour(outs[2])
                where = ("n" + tag, "f" + tag)
                halo_m = where + RUN["M"]
                new_halo = {k: where + RUN[k] for k in ("HB", "HT", "CB", "CT")}
                if half:
                    halo_high = new_halo
                else:
                    halo_low = new_halo
                    x_field = (("s" + tag, 1), where + RUN["HT"])

    keep = jnp.where(lower, low_result, high_result)
    give = jnp.where(lower, high_result, low_result)
    taken = to_partner(give)
    rows8 = jnp.concatenate(
        [jnp.where(lower, keep, taken), jnp.where(lower, taken, keep)], axis=1
    )
    by_chip = rows8.reshape(5, 4, 2, CH, GW).transpose(1, 0, 2, 3, 4)
    by_seq = lax.all_to_all(by_chip, "rows", 0, 0, axis_index_groups=groups, tiled=True)
    done = by_seq.transpose(1, 0, 2, 3, 4)
    return done[0:2], done[2:4], done[4:5]


def solution(mesh):
    return jax.shard_map(
        on_device,
        mesh=mesh,
        in_specs=(
            P(None, None, "rows", None, None),
            P("layer", None, "rows", None, None),
            P("layer", None, "rows", None, None),
            P(None, "rows", None, None),
            P("layer", None, None),
            P("layer", None, None),
            P("layer", None, None),
            P("layer", None, None),
            P("layer", None, None),
        ),
        out_specs=(
            P("layer", None, "rows", None, None),
            P("layer", None, "rows", None, None),
            P("layer", None, "rows", None, None),
        ),
        check_vma=False,
    )
```

time: 458 us -> 144 us (0.31)
  the two profiles are of different devices: /device:TPU:25 before, /device:TPU:1 now
where the time goes in v1:
time: 144 us
  starting transfers between devices  54.8 us (38%)
  Pallas kernels  34.8 us (24%)
  waiting for transfers between devices  21.9 us (15%)
  blocking collectives  13 us (9%)
  other arithmetic  9.14 us (6%)
  local copies, waits for them, and re-layouts  9.13 us (6%)
    ppermute x10, starting transfers between devices, to_partner(): return lax.ppermute(value, 'layer', swap)  45.3 us
    pallas_call x6, Pallas kernels, run_phase(): pl.pallas_call(functools.partial(phase_kernel, plan, last), out_shape=out...  34.8 us
    all_to_all x1, blocking collectives, on_device(): lax.all_to_all(by_chip, 'rows', 0, 0, axis_index_groups=groups, tiled=True)  13 us
    all_to_all x1, waiting for transfers between devices, on_device(): lax.all_to_all(mine, 'rows', 0, 0, axis_index_groups=groups, tiled=True)  10.8 us
    ppermute x10, waiting for transfers between devices, to_partner(): return lax.ppermute(value, 'layer', swap)  7.01 us
    all_to_all x1, starting transfers between devices, on_device(): lax.all_to_all(mine, 'rows', 0, 0, axis_index_groups=groups, tiled=True)  5.14 us
    select_n x3, other arithmetic, on_device(): w_high = [jnp.where(lower, b, a) for a, b in zip(own_w, other_w)]  4.89 us
    ppermute x7, starting transfers between devices, to_neighbour(): return lax.ppermute(value, ('layer', 'rows'), across)  4.32 us
  transfers between devices with their start and end apart: 18, of which 8 were waited for; matrix products, arithmetic and copies ran while one was open for 8% of the time, Pallas kernels for 4%

profile of v1, /device:TPU:1, one launch (start us, length us, event | category | flops | bytes accessed | tf_op | source)
XLA Modules:
  0.0 143.7 jit_solution(14853713546599796861)
XLA Ops:
  0.6 1.3 fusion.24
  3.2 1.4 pad_maximum_fusion
  4.7 1.4 collective-permute-start.2
  13.1 5.1 %all-to-all-start = ((bf16[4,6,2,64,128]{4,3,2,1,0:T(8,128)(2,1)}), bf16[4,6,2,64,128]{4,3,2,1,0:T(8,128)(2,1)S(1)}, u32[]{:S(2)}, u32[]{:S(2)}) async-start(bf16[4,6,2,64,128]{4,3,2,1,0:T(8,128)(2,1)} %pad_maximum_fusion.2), calls=%async_computation | async-start | bytes 1572864 | tf_op jit(solution)/shard_map/all_to_all | solution.py:239
  19.5 10.8 %all-to-all-done = bf16[4,6,2,64,128]{4,3,2,1,0:T(8,128)(2,1)S(1)} async-done(((bf16[4,6,2,64,128]{4,3,2,1,0:T(8,128)(2,1)}), bf16[4,6,2,64,128]{4,3,2,1,0:T(8,128)(2,1)S(1)}, u32[]{:S(2)}, u32[]{:S(2)}) %all-to-all-start) | async-done | bytes 786464 | tf_op jit(solution)/shard_map/all_to_all | solution.py:239
  30.3 1.3 collective-permute-start
  31.6 1.7 %broadcast_select_fusion.2 = (bf16[2,192,1152]{2,1,0:T(8,128)(2,1)S(1)}, bf16[2,192,1152]{2,1,0:T(8,128)(2,1)S(1)}) fusion(bf16[2,192,1152]{2,1,0:T(8,128)(2,1)} %collective-permute-done.3, pred[]{:T(512)S(6)} %eq.3, bf16[2,192,576]{2,1,0:T(8,128)(2,1)S(1)} %bitcast.143, bf16[2,192,576]{2,1,0:T(8,128)(2,1)S(1)} %get-tuple-element.54), kind=kLoop, calls=%fused_computation.4 | loop fusion | flops 2654208 | bytes 3538945 | tf_op jit(solution)/shard_map/jit(_where)/select_n | solution.py:229
  33.3 2.0 %broadcast_select_fusion = (bf16[2,256,1152]{2,1,0:T(8,128)(2,1)S(1)}, bf16[2,256,1152]{2,1,0:T(8,128)(2,1)S(1)}) fusion(bf16[2,256,1152]{2,1,0:T(8,128)(2,1)} %collective-permute-done.2, pred[]{:T(512)S(6)} %eq.3, bf16[2,256,576]{2,1,0:T(8,128)(2,1)S(1)} %bitcast.133, bf16[2,64,576]{2,1,0:T(8,128)(2,1)S(1)} %slice.222, ...), kind=kLoop, calls=%fused_computation.1 | loop fusion | flops 4718592 | bytes 4718593 | tf_op jit(solution)/shard_map/jit(_where)/select_n | solution.py:229
  35.7 2.1 %collective-permute-start.1 = (bf16[18,64,128]{2,1,0:T(8,128)(2,1)S(1)}, bf16[18,64,128]{2,1,0:T(8,128)(2,1)S(1)}, u32[]{:S(2)}, u32[]{:S(2)}) collective-permute-start(bf16[18,64,128]{2,1,0:T(8,128)(2,1)S(1)} %get-tuple-element.73), channel_id=1, source_target_pairs={{64,4},{0,124},{65,5},{1,125},{66,6},{2,126},{67,7},{3,127},{68,8}... | collective-permute-start | bytes 884744 | tf_op jit(solution)/shard_map/ppermute | solution.py:224
  38.1 4.1 %collective-permute-done.1.refs_1_ = bf16[18,64,128]{2,1,0:T(8,128)(2,1)S(1)} collective-permute-done((bf16[18,64,128]{2,1,0:T(8,128)(2,1)S(1)}, bf16[18,64,128]{2,1,0:T(8,128)(2,1)S(1)}, u32[]{:S(2)}, u32[]{:S(2)}) %collective-permute-start.1) | collective-permute-done | bytes 294944 | tf_op jit(solution)/shard_map/ppermute | solution.py:224
  42.2 5.8 %two_layers.5 = (bf16[5,4,64,128]{3,2,1,0:T(8,128)(2,1)S(1)}, bf16[16,64,128]{2,1,0:T(8,128)(2,1)S(1)}, bf16[16,64,128]{2,1,0:T(8,128)(2,1)S(1)}) custom-call(s32[2]{0:T(128)S(1)} %pad_add_fusion.refs_0_, bf16[18,64,128]{2,1,0:T(8,128)(2,1)S(1)} %collective-permute-done.1.refs_1_, bf16[6,4,64,128]{3,2,1,0:T(8,128)(2,1)S(1)} %constant_dynamic-slice_fusion.1.refs_2_, ...), custom_call_target="tpu_custom_call" | custom-call | tf_op jit(solution)/shard_map/two_layers/pallas_call | solution.py:176
  48.0 1.8 %collective-permute-start.5 = (bf16[16,64,128]{2,1,0:T(8,128)(2,1)S(1)}, bf16[16,64,128]{2,1,0:T(8,128)(2,1)S(1)}, u32[]{:S(2)}, u32[]{:S(2)}) collective-permute-start(bf16[16,64,128]{2,1,0:T(8,128)(2,1)S(1)} %get-tuple-element.30), channel_id=1, source_target_pairs={{64,4},{0,124},{65,5},{1,125},{66,6},{2,126},{67,7},{3,127},{68,8}... | collective-permute-start | bytes 786440 | tf_op jit(solution)/shard_map/ppermute | solution.py:224
  49.8 6.7 %collective-permute-start.7 = (bf16[16,64,128]{2,1,0:T(8,128)(2,1)S(1)}, bf16[16,64,128]{2,1,0:T(8,128)(2,1)S(1)}, u32[]{:S(2)}, u32[]{:S(2)}) collective-permute-start(bf16[16,64,128]{2,1,0:T(8,128)(2,1)S(1)} %get-tuple-element.31), channel_id=1, source_target_pairs={{0,64},{64,0},{1,65},{65,1},{2,66},{66,2},{3,67},{67,3},{4,68},{68... | collective-permute-start | bytes 786440 | tf_op jit(solution)/shard_map/ppermute | solution.py:221
  57.7 5.8 %two_layers.6 = (bf16[5,4,64,128]{3,2,1,0:T(8,128)(2,1)S(1)}, bf16[16,64,128]{2,1,0:T(8,128)(2,1)S(1)}, bf16[16,64,128]{2,1,0:T(8,128)(2,1)S(1)}) custom-call(s32[2]{0:T(128)S(1)} %pad_add_fusion.refs_0_, bf16[16,64,128]{2,1,0:T(8,128)(2,1)S(1)} %collective-permute-done.5.refs_1_, bf16[18,64,128]{2,1,0:T(8,128)(2,1)S(1)} %collective-permute-done.6.refs_2_.refs_3_, ...), custom_call_target="tpu_custom_call" | custom-call | tf_op jit(solution)/shard_map/two_layers/pallas_call | solution.py:176
  63.6 7.9 %collective-permute-start.9 = (bf16[16,64,128]{2,1,0:T(8,128)(2,1)S(1)}, bf16[16,64,128]{2,1,0:T(8,128)(2,1)S(1)}, u32[]{:S(2)}, u32[]{:S(2)}) collective-permute-start(bf16[16,64,128]{2,1,0:T(8,128)(2,1)S(1)} %get-tuple-element.34), channel_id=1, source_target_pairs={{0,64},{64,0},{1,65},{65,1},{2,66},{66,2},{3,67},{67,3},{4,68},{68... | collective-permute-start | bytes 786440 | tf_op jit(solution)/shard_map/ppermute | solution.py:221
  72.7 5.8 %two_layers.7 = (bf16[5,4,64,128]{3,2,1,0:T(8,128)(2,1)S(1)}, bf16[16,64,128]{2,1,0:T(8,128)(2,1)S(1)}, bf16[16,64,128]{2,1,0:T(8,128)(2,1)S(1)}) custom-call(s32[2]{0:T(128)S(1)} %pad_add_fusion.refs_0_, bf16[16,64,128]{2,1,0:T(8,128)(2,1)S(1)} %collective-permute-done.5.refs_1_, bf16[16,64,128]{2,1,0:T(8,128)(2,1)S(1)} %collective-permute-done.8.refs_2_.refs_1_, ...), custom_call_target="tpu_custom_call" | custom-call | tf_op jit(solution)/shard_map/two_layers/pallas_call | solution.py:176
  78.6 8.0 %collective-permute-start.11 = (bf16[16,64,128]{2,1,0:T(8,128)(2,1)S(1)}, bf16[16,64,128]{2,1,0:T(8,128)(2,1)S(1)}, u32[]{:S(2)}, u32[]{:S(2)}) collective-permute-start(bf16[16,64,128]{2,1,0:T(8,128)(2,1)S(1)} %get-tuple-element.37), channel_id=1, source_target_pairs={{0,64},{64,0},{1,65},{65,1},{2,66},{66,2},{3,67},{67,3},{4,68},{68... | collective-permute-start | bytes 786440 | tf_op jit(solution)/shard_map/ppermute | solution.py:221
  87.7 5.8 %two_layers.8 = (bf16[5,4,64,128]{3,2,1,0:T(8,128)(2,1)S(1)}, bf16[16,64,128]{2,1,0:T(8,128)(2,1)S(1)}, bf16[16,64,128]{2,1,0:T(8,128)(2,1)S(1)}) custom-call(s32[2]{0:T(128)S(1)} %pad_add_fusion.refs_0_, bf16[16,64,128]{2,1,0:T(8,128)(2,1)S(1)} %collective-permute-done.8.refs_2_.refs_1_, bf16[16,64,128]{2,1,0:T(8,128)(2,1)S(1)} %collective-permute-done.10.refs_2_.refs_1_, ...), custom_call_target="tpu_custom_call" | custom-call | tf_op jit(solution)/shard_map/two_layers/pallas_call | solution.py:176
  93.6 7.9 %collective-permute-start.13 = (bf16[16,64,128]{2,1,0:T(8,128)(2,1)S(1)}, bf16[16,64,128]{2,1,0:T(8,128)(2,1)S(1)}, u32[]{:S(2)}, u32[]{:S(2)}) collective-permute-start(bf16[16,64,128]{2,1,0:T(8,128)(2,1)S(1)} %get-tuple-element.40), channel_id=1, source_target_pairs={{0,64},{64,0},{1,65},{65,1},{2,66},{66,2},{3,67},{67,3},{4,68},{68... | collective-permute-start | bytes 786440 | tf_op jit(solution)/shard_map/ppermute | solution.py:221
  102.7 5.8 %two_layers.9 = (bf16[5,4,64,128]{3,2,1,0:T(8,128)(2,1)S(1)}, bf16[16,64,128]{2,1,0:T(8,128)(2,1)S(1)}, bf16[16,64,128]{2,1,0:T(8,128)(2,1)S(1)}) custom-call(s32[2]{0:T(128)S(1)} %pad_add_fusion.refs_0_, bf16[16,64,128]{2,1,0:T(8,128)(2,1)S(1)} %collective-permute-done.10.refs_2_.refs_1_, bf16[16,64,128]{2,1,0:T(8,128)(2,1)S(1)} %collective-permute-done.12.refs_2_.refs_1_, ...), custom_call_target="tpu_custom_call" | custom-call | tf_op jit(solution)/shard_map/two_layers/pallas_call | solution.py:176
  108.6 8.0 %collective-permute-start.15 = (bf16[16,64,128]{2,1,0:T(8,128)(2,1)S(1)}, bf16[16,64,128]{2,1,0:T(8,128)(2,1)S(1)}, u32[]{:S(2)}, u32[]{:S(2)}) collective-permute-start(bf16[16,64,128]{2,1,0:T(8,128)(2,1)S(1)} %get-tuple-element.44), channel_id=1, source_target_pairs={{0,64},{64,0},{1,65},{65,1},{2,66},{66,2},{3,67},{67,3},{4,68},{68... | collective-permute-start | bytes 786440 | tf_op jit(solution)/shard_map/ppermute | solution.py:221
  117.7 5.7 %two_layers_last.1 = bf16[5,4,64,128]{3,2,1,0:T(8,128)(2,1)S(1)} custom-call(s32[2]{0:T(128)S(1)} %pad_add_fusion.refs_0_, bf16[16,64,128]{2,1,0:T(8,128)(2,1)S(1)} %collective-permute-done.12.refs_2_.refs_1_, bf16[16,64,128]{2,1,0:T(8,128)(2,1)S(1)} %collective-permute-done.14.refs_2_, bf16[16,64,128]{2,1,0:T(8,128)(2,1)S(1)} %collective-permute-done.13.refs_6_.refs_3_, ...), custom_call_target="tpu_custom_call" | custom-call | tf_op jit(solution)/shard_map/two_layers_last/pallas_call | solution.py:176
  123.5 3.6 %collective-permute-start.16 = (bf16[5,4,64,128]{3,2,1,0:T(8,128)(2,1)S(1)}, bf16[5,4,64,128]{3,2,1,0:T(8,128)(2,1)S(1)}, u32[]{:S(2)}, u32[]{:S(2)}) collective-permute-start(bf16[5,4,64,128]{3,2,1,0:T(8,128)(2,1)S(1)} %broadcast_select_fusion.10), channel_id=1, source_target_pairs={{0,64},{64,0},{1,65},{65,1},{2,66},{66,2},{3,67},{67,3},{4,68},{68... | collective-permute-start | bytes 983048 | tf_op jit(solution)/shard_map/ppermute | solution.py:221
  128.5 13.0 %all_to_all.10 = bf16[4,5,2,64,128]{4,3,2,1,0:T(8,128)(2,1)S(1)} all-to-all(bf16[4,5,2,64,128]{4,3,2,1,0:T(8,128)(2,1)S(1)} %bitcast.141), channel_id=1, replica_groups={{0,1,2,3},{4,5,6,7},{8,9,10,11},{12,13,14,15},{16,17,18,19},{20,21,22,2..., dimensions={0} | all-to-all | bytes 1310720 | tf_op jit(solution)/shard_map/all_to_all | solution.py:327
  (82 shorter events, 19.9 us)
Async XLA Ops:
  0.6 2.3 %copy-start.3 = (bf16[2,576,256]{2,1,0:T(8,128)(2,1)S(1)}, bf16[2,576,256]{2,1,0:T(8,128)(2,1)}, u32[]{:S(2)}) copy-start(bf16[2,576,256]{2,1,0:T(8,128)(2,1)} %param.16) | copy-start | bytes 1769476
  3.2 2.8 %copy-start = (bf16[2,576,192]{1,2,0:T(8,128)(2,1)S(1)}, bf16[2,576,192]{1,2,0:T(8,128)(2,1)}, u32[]{:S(2)}) copy-start(bf16[2,576,192]{1,2,0:T(8,128)(2,1)} %param.17) | copy-start | bytes 1327108
  4.7 2.6 %copy-start.4 = (bf16[2,1152,64]{1,2,0:T(8,128)(2,1)S(1)}, bf16[2,1152,64]{1,2,0:T(8,128)(2,1)}, u32[]{:S(2)}) copy-start(bf16[2,1152,64]{1,2,0:T(8,128)(2,1)} %param.18) | copy-start | bytes 884740
  4.7 28.6 %collective-permute-start.2 = (bf16[2,256,1152]{2,1,0:T(8,128)(2,1)}, bf16[2,256,1152]{2,1,0:T(8,128)(2,1)}, u32[]{:S(2)}, u32[]{:S(2)}) collective-permute-start(bf16[2,256,1152]{2,1,0:T(8,128)(2,1)} %pad_maximum_fusion), channel_id=1, source_target_pairs={{0,64},{64,0},{1,65},{65,1},{2,66},{66,2},{3,67},{67,3},{4,68},{68... | collective-permute-start | bytes 3538952 | tf_op jit(solution)/shard_map/ppermute | solution.py:221
  7.2 24.3 %collective-permute-start.3 = (bf16[2,192,1152]{2,1,0:T(8,128)(2,1)}, bf16[2,192,1152]{2,1,0:T(8,128)(2,1)}, u32[]{:S(2)}, u32[]{:S(2)}) collective-permute-start(bf16[2,192,1152]{2,1,0:T(8,128)(2,1)} %pad_maximum_fusion.1), channel_id=1, source_target_pairs={{0,64},{64,0},{1,65},{65,1},{2,66},{66,2},{3,67},{67,3},{4,68},{68... | collective-permute-start | bytes 2654216 | tf_op jit(solution)/shard_map/ppermute | solution.py:221
  8.4 1.5 %copy-start.5 = (bf16[2,4,2,64,128]{4,3,2,1,0:T(8,128)(2,1)S(1)}, bf16[2,4,2,64,128]{4,3,2,1,0:T(8,128)(2,1)}, u32[]{:S(2)}) copy-start(bf16[2,4,2,64,128]{4,3,2,1,0:T(8,128)(2,1)} %param.13) | copy-start | bytes 786436
  9.1 2.9 %copy-start.6 = (bf16[4,2,64,128]{3,2,1,0:T(8,128)(2,1)S(1)}, bf16[4,2,64,128]{3,2,1,0:T(8,128)(2,1)}, u32[]{:S(2)}) copy-start(bf16[4,2,64,128]{3,2,1,0:T(8,128)(2,1)} %param.14) | copy-start | bytes 393220
  9.3 8.9 %copy-start.2 = (bf16[2,256,384]{2,1,0:T(8,128)(2,1)}, bf16[2,256,384]{2,1,0:T(8,128)(2,1)S(1)}, u32[]{:S(2)}) copy-start(bf16[2,256,384]{2,1,0:T(8,128)(2,1)S(1)} %constant_dynamic-update-slice_fusion.6) | copy-start | bytes 1179652
  9.3 8.9 %collective-permute-start.4 = (bf16[2,256,384]{2,1,0:T(8,128)(2,1)S(1)}, bf16[2,256,384]{2,1,0:T(8,128)(2,1)}, u32[]{:S(2)}, u32[]{:S(2)}) collective-permute-start(bf16[2,256,384]{2,1,0:T(8,128)(2,1)S(1)} %constant_dynamic-update-slice_fusion.6), channel_id=1, source_target_pairs={{0,64},{64,0},{1,65},{65,1},{2,66},{66,2},{3,67},{67,3},{4,68},{68... | collective-permute-start | bytes 1179656 | tf_op jit(solution)/shard_map/ppermute | solution.py:221
  13.1 17.2 %all-to-all-start = ((bf16[4,6,2,64,128]{4,3,2,1,0:T(8,128)(2,1)}), bf16[4,6,2,64,128]{4,3,2,1,0:T(8,128)(2,1)S(1)}, u32[]{:S(2)}, u32[]{:S(2)}) async-start(bf16[4,6,2,64,128]{4,3,2,1,0:T(8,128)(2,1)} %pad_maximum_fusion.2), calls=%async_computation | async-start | bytes 1572864 | tf_op jit(solution)/shard_map/all_to_all | solution.py:239
  30.3 5.0 %collective-permute-start = (bf16[6,8,64,128]{3,2,1,0:T(8,128)(2,1)S(1)}, bf16[6,8,64,128]{3,2,1,0:T(8,128)(2,1)S(1)}, u32[]{:S(2)}, u32[]{:S(2)}) collective-permute-start(bf16[6,8,64,128]{3,2,1,0:T(8,128)(2,1)S(1)} %bitcast.136), channel_id=1, source_target_pairs={{0,64},{64,0},{1,65},{65,1},{2,66},{66,2},{3,67},{67,3},{4,68},{68... | collective-permute-start | bytes 2359304 | tf_op jit(solution)/shard_map/ppermute | solution.py:221
  35.7 6.5 %collective-permute-start.1 = (bf16[18,64,128]{2,1,0:T(8,128)(2,1)S(1)}, bf16[18,64,128]{2,1,0:T(8,128)(2,1)S(1)}, u32[]{:S(2)}, u32[]{:S(2)}) collective-permute-start(bf16[18,64,128]{2,1,0:T(8,128)(2,1)S(1)} %get-tuple-element.73), channel_id=1, source_target_pairs={{64,4},{0,124},{65,5},{1,125},{66,6},{2,126},{67,7},{3,127},{68,8}... | collective-permute-start | bytes 884744 | tf_op jit(solution)/shard_map/ppermute | solution.py:224
  38.0 18.6 %collective-permute-start.6 = (bf16[18,64,128]{2,1,0:T(8,128)(2,1)S(1)}, bf16[18,64,128]{2,1,0:T(8,128)(2,1)S(1)}, u32[]{:S(2)}, u32[]{:S(2)}) collective-permute-start(bf16[18,64,128]{2,1,0:T(8,128)(2,1)S(1)} %get-tuple-element.61), channel_id=1, source_target_pairs={{64,4},{0,124},{65,5},{1,125},{66,6},{2,126},{67,7},{3,127},{68,8}... | collective-permute-start | bytes 884744 | tf_op jit(solution)/shard_map/ppermute | solution.py:224
  48.0 8.5 %collective-permute-start.5 = (bf16[16,64,128]{2,1,0:T(8,128)(2,1)S(1)}, bf16[16,64,128]{2,1,0:T(8,128)(2,1)S(1)}, u32[]{:S(2)}, u32[]{:S(2)}) collective-permute-start(bf16[16,64,128]{2,1,0:T(8,128)(2,1)S(1)} %get-tuple-element.30), channel_id=1, source_target_pairs={{64,4},{0,124},{65,5},{1,125},{66,6},{2,126},{67,7},{3,127},{68,8}... | collective-permute-start | bytes 786440 | tf_op jit(solution)/shard_map/ppermute | solution.py:224
  49.8 7.8 %collective-permute-start.7 = (bf16[16,64,128]{2,1,0:T(8,128)(2,1)S(1)}, bf16[16,64,128]{2,1,0:T(8,128)(2,1)S(1)}, u32[]{:S(2)}, u32[]{:S(2)}) collective-permute-start(bf16[16,64,128]{2,1,0:T(8,128)(2,1)S(1)} %get-tuple-element.31), channel_id=1, source_target_pairs={{0,64},{64,0},{1,65},{65,1},{2,66},{66,2},{3,67},{67,3},{4,68},{68... | collective-permute-start | bytes 786440 | tf_op jit(solution)/shard_map/ppermute | solution.py:221
  63.5 8.0 %collective-permute-start.8 = (bf16[16,64,128]{2,1,0:T(8,128)(2,1)S(1)}, bf16[16,64,128]{2,1,0:T(8,128)(2,1)S(1)}, u32[]{:S(2)}, u32[]{:S(2)}) collective-permute-start(bf16[16,64,128]{2,1,0:T(8,128)(2,1)S(1)} %get-tuple-element.33), channel_id=1, source_target_pairs={{64,4},{0,124},{65,5},{1,125},{66,6},{2,126},{67,7},{3,127},{68,8}... | collective-permute-start | bytes 786440 | tf_op jit(solution)/shard_map/ppermute | solution.py:224
  63.6 9.1 %collective-permute-start.9 = (bf16[16,64,128]{2,1,0:T(8,128)(2,1)S(1)}, bf16[16,64,128]{2,1,0:T(8,128)(2,1)S(1)}, u32[]{:S(2)}, u32[]{:S(2)}) collective-permute-start(bf16[16,64,128]{2,1,0:T(8,128)(2,1)S(1)} %get-tuple-element.34), channel_id=1, source_target_pairs={{0,64},{64,0},{1,65},{65,1},{2,66},{66,2},{3,67},{67,3},{4,68},{68... | collective-permute-start | bytes 786440 | tf_op jit(solution)/shard_map/ppermute | solution.py:221
  78.5 8.0 %collective-permute-start.10 = (bf16[16,64,128]{2,1,0:T(8,128)(2,1)S(1)}, bf16[16,64,128]{2,1,0:T(8,128)(2,1)S(1)}, u32[]{:S(2)}, u32[]{:S(2)}) collective-permute-start(bf16[16,64,128]{2,1,0:T(8,128)(2,1)S(1)} %get-tuple-element.36), channel_id=1, source_target_pairs={{64,4},{0,124},{65,5},{1,125},{66,6},{2,126},{67,7},{3,127},{68,8}... | collective-permute-start | bytes 786440 | tf_op jit(solution)/shard_map/ppermute | solution.py:224
  78.6 9.1 %collective-permute-start.11 = (bf16[16,64,128]{2,1,0:T(8,128)(2,1)S(1)}, bf16[16,64,128]{2,1,0:T(8,128)(2,1)S(1)}, u32[]{:S(2)}, u32[]{:S(2)}) collective-permute-start(bf16[16,64,128]{2,1,0:T(8,128)(2,1)S(1)} %get-tuple-element.37), channel_id=1, source_target_pairs={{0,64},{64,0},{1,65},{65,1},{2,66},{66,2},{3,67},{67,3},{4,68},{68... | collective-permute-start | bytes 786440 | tf_op jit(solution)/shard_map/ppermute | solution.py:221
  93.5 8.0 %collective-permute-start.12 = (bf16[16,64,128]{2,1,0:T(8,128)(2,1)S(1)}, bf16[16,64,128]{2,1,0:T(8,128)(2,1)S(1)}, u32[]{:S(2)}, u32[]{:S(2)}) collective-permute-start(bf16[16,64,128]{2,1,0:T(8,128)(2,1)S(1)} %get-tuple-element.39), channel_id=1, source_target_pairs={{64,4},{0,124},{65,5},{1,125},{66,6},{2,126},{67,7},{3,127},{68,8}... | collective-permute-start | bytes 786440 | tf_op jit(solution)/shard_map/ppermute | solution.py:224
  93.6 9.1 %collective-permute-start.13 = (bf16[16,64,128]{2,1,0:T(8,128)(2,1)S(1)}, bf16[16,64,128]{2,1,0:T(8,128)(2,1)S(1)}, u32[]{:S(2)}, u32[]{:S(2)}) collective-permute-start(bf16[16,64,128]{2,1,0:T(8,128)(2,1)S(1)} %get-tuple-element.40), channel_id=1, source_target_pairs={{0,64},{64,0},{1,65},{65,1},{2,66},{66,2},{3,67},{67,3},{4,68},{68... | collective-permute-start | bytes 786440 | tf_op jit(solution)/shard_map/ppermute | solution.py:221
  108.5 8.0 %collective-permute-start.14 = (bf16[16,64,128]{2,1,0:T(8,128)(2,1)S(1)}, bf16[16,64,128]{2,1,0:T(8,128)(2,1)S(1)}, u32[]{:S(2)}, u32[]{:S(2)}) collective-permute-start(bf16[16,64,128]{2,1,0:T(8,128)(2,1)S(1)} %get-tuple-element.43), channel_id=1, source_target_pairs={{64,4},{0,124},{65,5},{1,125},{66,6},{2,126},{67,7},{3,127},{68,8}... | collective-permute-start | bytes 786440 | tf_op jit(solution)/shard_map/ppermute | solution.py:224
  108.6 9.1 %collective-permute-start.15 = (bf16[16,64,128]{2,1,0:T(8,128)(2,1)S(1)}, bf16[16,64,128]{2,1,0:T(8,128)(2,1)S(1)}, u32[]{:S(2)}, u32[]{:S(2)}) collective-permute-start(bf16[16,64,128]{2,1,0:T(8,128)(2,1)S(1)} %get-tuple-element.44), channel_id=1, source_target_pairs={{0,64},{64,0},{1,65},{65,1},{2,66},{66,2},{3,67},{67,3},{4,68},{68... | collective-permute-start | bytes 786440 | tf_op jit(solution)/shard_map/ppermute | solution.py:221
  123.5 4.8 %collective-permute-start.16 = (bf16[5,4,64,128]{3,2,1,0:T(8,128)(2,1)S(1)}, bf16[5,4,64,128]{3,2,1,0:T(8,128)(2,1)S(1)}, u32[]{:S(2)}, u32[]{:S(2)}) collective-permute-start(bf16[5,4,64,128]{3,2,1,0:T(8,128)(2,1)S(1)} %broadcast_select_fusion.10), channel_id=1, source_target_pairs={{0,64},{64,0},{1,65},{65,1},{2,66},{66,2},{3,67},{67,3},{4,68},{68... | collective-permute-start | bytes 983048 | tf_op jit(solution)/shard_map/ppermute | solution.py:221
  (2 other events, 2.1 us)

commit v2 on v0

v2 whole, which is shorter than its diff:
```python
import functools

import jax
import jax.numpy as jnp
from jax import lax
from jax.experimental import pallas as pl
from jax.experimental.pallas import tpu as pltpu
from jax.sharding import PartitionSpec as P


CH = 64
GW = 128
OWN = 4
BF = jnp.bfloat16
F32 = jnp.float32

FIRST_A = {"HT": (0, 2), "M": (2, 4), "HB": (6, 4), "CB": (10, 3), "CT": (13, 1), "F0": (14, 4)}
FIRST_B = {"HT": (0, 2), "HB": (2, 4), "CB": (6, 3), "CT": (9, 1), "F1": (10, 4), "F2": (14, 4)}
SOON = ({"HT": (0, 4), "M": (4, 4)}, {"M": (0, 4)})
LATE = (
    {"HB": (0, 4), "CB": (4, 3), "CT": (7, 1)},
    {"HT": (0, 2), "HB": (2, 4), "CB": (6, 3), "CT": (9, 1)},
)
SLOT = {"HB": 0, "HT": 1, "CB": 2, "CT": 3, "M": 4}
REACH = (3, 1)


def units(layout):
    return sum(count for _, count in layout.values())


def both(half):
    shift = units(SOON[half])
    near = dict(SOON[half])
    near.update({k: (o + shift, n) for k, (o, n) in LATE[half].items()})
    return near


def sigmoid(v):
    return 0.5 * jnp.tanh(0.5 * v) + 0.5


def taps_of(row):
    lane = lax.broadcasted_iota(jnp.int32, row.shape, 1)
    zero = jnp.zeros_like(row)
    before = jnp.where(lane == 0, zero, pltpu.roll(row, 1, 1))
    after = jnp.where(lane == GW - 1, zero, pltpu.roll(row, GW - 1, 1))
    return jnp.concatenate([before, row, after], axis=0)


def phase_kernel(plan, *refs):
    names = plan["names"]
    outs = plan["outs"]
    n_in = len(names)
    ref = dict(zip(names, refs[:n_in]))
    out = dict(zip(outs, refs[n_in : n_in + len(outs)]))
    tx, th, tm, tx2, th2, tm2, yb, ob, yb2, ob2, raw = refs[n_in + len(outs) :]
    state_out = out["state"]
    core = ref["sc"][0]
    top = ref["sc"][1]
    first_core = core == 0

    def keep(row, value):
        if 0 <= row < OWN:
            return value
        g = top + row
        return jnp.where(jnp.logical_and(g >= 0, g < 128), value, jnp.zeros_like(value))

    def fetch(field, row):
        (own, slot), (near, near_at, far, far_at, count) = plan["fields"][field]
        if 0 <= row < OWN:
            return ref[own][slot, row]
        if row < 0:
            unit = count + row
            value = jnp.where(first_core, ref[far][far_at + unit], ref[near][near_at + unit])
        else:
            unit = row - OWN
            value = jnp.where(first_core, ref[near][near_at + unit], ref[far][far_at + unit])
        return keep(row, value)

    rows_of = [list(range(-reach, OWN + reach)) for reach in REACH]
    bufs = ((tx, th, tm, yb, ob), (tx2, th2, tm2.at[1:9], yb2, ob2))
    filled = set()

    def fill(buf, key, field, reach, upto):
        for i in range(upto):
            if (key, i) not in filled:
                filled.add((key, i))
                buf[i] = taps_of(fetch(field, i - reach))

    def matmuls(index, q):
        bx, bh, bm, _, _ = bufs[index]
        if index == 0:
            fill(tx, "x", "X", 4, q + 4)
            fill(th, "h", "HB", 4, q + 4)
            fill(tm, "m", "M", 4, q + 4)
        else:
            fill(th2, "h2", "HT", 2, q + 4)
        cols = [
            jnp.concatenate([buf[i + a] for buf in (bx, bh, bm) for a in range(3)], axis=0)
            for i in (q, q + 1)
        ]
        rhs = jnp.concatenate(cols, axis=1)
        x, h, m = rhs[0:576], rhs[576:1152], rhs[1152:1728]
        layer = plan["layer"] + index
        shared = jnp.dot(
            ref["wb"][layer],
            jnp.concatenate([x, h[512:576], m[0:128]], axis=0),
            preferred_element_type=F32,
        )
        slot = (q // 2 + index) % 2
        raw[slot, 0:256] = shared[0:256] + jnp.dot(
            ref["wa"][layer], h[0:512], preferred_element_type=F32
        )
        raw[slot, 256:448] = shared[256:448] + jnp.dot(
            ref["wc"][layer], m[128:576], preferred_element_type=F32
        )
        return raw.at[slot, 0:256], raw.at[slot, 256:448]

    def gates(index, q, acc1, acc2):
        _, _, _, y_buf, o_buf = bufs[index]
        rows = rows_of[index]
        pair = (rows[q], rows[q + 1])
        c_field = "CT" if index else "CB"
        c_prev = jnp.concatenate([fetch(c_field, row) for row in pair], axis=1).astype(F32)
        if index:
            m_rows = [tm2[row + 3, 64:128] for row in pair]
        else:
            m_rows = [tm[row + 4, 64:128] for row in pair]
        m_prev = jnp.concatenate(m_rows, axis=1).astype(F32)
        c_new = sigmoid(acc1[64:128] + 1.0) * c_prev + sigmoid(acc1[0:64]) * jnp.tanh(acc1[128:192])
        m_new = sigmoid(acc2[64:128] + 1.0) * m_prev + sigmoid(acc2[0:64]) * jnp.tanh(acc2[128:192])
        c_new = c_new.astype(BF)
        m_new = m_new.astype(BF)
        lanes = slice(q * GW, (q + 2) * GW)
        o_buf[:, lanes] = acc1[192:256]
        blocks = []
        for j, row in enumerate(pair):
            c_row = keep(row, c_new[:, j * GW : (j + 1) * GW])
            m_row = keep(row, m_new[:, j * GW : (j + 1) * GW])
            if 0 <= row < OWN:
                state_out[SLOT[c_field], row] = c_row
                if index:
                    state_out[SLOT["M"], row] = m_row
            c_taps = taps_of(c_row)
            m_taps = taps_of(m_row)
            if not index:
                tm2[row + 3] = m_taps
            blocks.append(
                jnp.concatenate(
                    [t[64 * b : 64 * b + 64] for b in range(3) for t in (c_taps, m_taps)], axis=0
                )
            )
        y_buf[:, lanes] = jnp.dot(
            ref["wo"][plan["layer"] + index],
            jnp.concatenate(blocks, axis=1),
            preferred_element_type=F32,
        )

    def hidden(index, q):
        _, _, _, y_buf, o_buf = bufs[index]
        lanes = slice(q * GW, (q + 1) * GW)
        gate = (
            o_buf[:, lanes]
            + y_buf[0:64, (q - 1) * GW : q * GW]
            + y_buf[64:128, lanes]
            + y_buf[128:192, (q + 1) * GW : (q + 2) * GW]
        )
        h_new = (sigmoid(gate) * jnp.tanh(y_buf[192:256, lanes])).astype(BF)
        row = rows_of[index][q]
        h_new = keep(row, h_new)
        if 0 <= row < OWN:
            state_out[SLOT["HT" if index else "HB"], row] = h_new
        if not index:
            tx2[row + 2] = taps_of(h_new)

    def finish(index, q, accs):
        gates(index, q, *accs)
        for h in (q - 1, q):
            if h >= 1:
                hidden(index, h)

    tasks = [(i, q) for i in range(2) for q in range(0, len(rows_of[i]), 2)]
    waiting = None
    for task in tasks:
        accs = matmuls(*task)
        if waiting is not None:
            finish(*waiting)
        waiting = task + (accs,)
    finish(*waiting)

    def send(target, layout, last_rows_if):
        for field, (offset, count) in layout.items():
            for u in range(count):
                low = state_out[SLOT[field], u]
                high = state_out[SLOT[field], OWN - count + u]
                target[offset + u] = jnp.where(last_rows_if, high, low)

    half = plan["half"]
    if "near" in out:
        send(out["near"], both(half) if "late" in out else SOON[half], first_core)
    if "soon" in out:
        send(out["soon"], SOON[half], jnp.logical_not(first_core))
    if "late" in out:
        send(out["late"], LATE[half], jnp.logical_not(first_core))


def run_phase(operands, plan):
    names = list(operands)
    plan = dict(plan, names=names)
    unit = (CH, GW)
    half = plan["half"]
    sizes = {"state": (5, OWN) + unit}
    if plan["send"]:
        far = {"soon": units(SOON[half])}
        if plan["send"] > 1:
            far["late"] = units(LATE[half])
        sizes["near"] = (sum(far.values()),) + unit
        sizes.update({k: (n,) + unit for k, n in far.items()})
    plan["outs"] = list(sizes)
    in_specs = [
        pl.BlockSpec(memory_space=pltpu.SMEM if name == "sc" else pltpu.VMEM) for name in names
    ]
    results = pl.pallas_call(
        functools.partial(phase_kernel, plan),
        out_shape=[jax.ShapeDtypeStruct(s, BF) for s in sizes.values()],
        in_specs=in_specs,
        out_specs=[pl.BlockSpec(memory_space=pltpu.VMEM) for _ in sizes],
        scratch_shapes=[
            pltpu.VMEM((12, 3 * CH, GW), BF),
            pltpu.VMEM((12, 3 * CH, GW), BF),
            pltpu.VMEM((12, 3 * CH, GW), BF),
            pltpu.VMEM((8, 3 * CH, GW), BF),
            pltpu.VMEM((8, 3 * CH, GW), BF),
            pltpu.VMEM((10, 3 * CH, GW), BF),
            pltpu.VMEM((4 * CH, 10 * GW), F32),
            pltpu.VMEM((CH, 10 * GW), F32),
            pltpu.VMEM((4 * CH, 6 * GW), F32),
            pltpu.VMEM((CH, 6 * GW), F32),
            pltpu.VMEM((2, 7 * CH, 2 * GW), F32),
        ],
        compiler_params=pltpu.CompilerParams(vmem_limit_bytes=24 << 20),
        name="two_layers",
    )(*[operands[name] for name in names])
    return dict(zip(sizes, results))


def pack_weights_kernel(sc, *refs):
    inputs, (wa, wb, wc, wo) = refs[:10], refs[10:]
    core = sc[0]
    for group in range(2):
        x, h, m, o, last = inputs[5 * group : 5 * group + 5]
        first = 2 * core if group == 0 else 2 - 2 * core
        for l in range(2):
            at = first + l
            xt = x[l]
            ht = jnp.transpose(h[l])
            mt = m[l]
            ot = o[l]
            wa[at] = ht[:, 0:512]
            wc[at] = mt[:, 128:576]
            gate_rows = jnp.concatenate([xt[0:192], xt[384:448]], axis=0)
            wb[at, 0:256, 0:512] = gate_rows[:, 0:512]
            wb[at, 0:256, 512:640] = jnp.concatenate([gate_rows[:, 512:576], ht[:, 512:576]], axis=1)
            wb[at, 0:256, 640:768] = jnp.zeros((256, 128), BF)
            wb[at, 256:448, 0:512] = xt[192:384, 0:512]
            wb[at, 256:448, 512:640] = jnp.concatenate(
                [xt[192:384, 512:576], jnp.zeros((192, 64), BF)], axis=1
            )
            wb[at, 256:448, 640:768] = mt[:, 0:128]
            for a in range(3):
                wo[at, 64 * a : 64 * a + 64] = ot[:, 384 * a : 384 * a + 384]
            wo[at, 192:256, 0:128] = jnp.zeros((64, 128), BF)
            wo[at, 192:256, 128:256] = last[l]
            wo[at, 192:256, 256:384] = jnp.zeros((64, 128), BF)


def pack_weights(scalars, own, other):
    shapes = ((4, 256, 512), (4, 448, 768), (4, 192, 448), (4, 256, 384))
    vmem = pl.BlockSpec(memory_space=pltpu.VMEM)
    return pl.pallas_call(
        pack_weights_kernel,
        out_shape=[jax.ShapeDtypeStruct(s, BF) for s in shapes],
        in_specs=[pl.BlockSpec(memory_space=pltpu.SMEM)] + [vmem] * 10,
        out_specs=[vmem] * 4,
        compiler_params=pltpu.CompilerParams(vmem_limit_bytes=32 << 20),
        name="pack_weights",
    )(scalars, *own, *other)


def cut_state_kernel(sc, frames, hidden, cell, memory, *rest):
    pieces, sems = rest[:4], rest[4]
    core, z = sc[0], sc[2]
    shared = []
    for k in range(4):
        seq = lax.rem(z + k, 4)
        for l in range(2):
            shared.append(
                pltpu.make_async_copy(hidden.at[l, seq], pieces[k].at[l], sems.at[k, l])
            )
            shared.append(
                pltpu.make_async_copy(cell.at[l, seq], pieces[k].at[2 + l], sems.at[k, 2 + l])
            )
    for c in shared:
        c.start()

    def extras(sources):
        copies = []
        for k in range(4):
            seq = lax.rem(z + k, 4)
            for i, source in enumerate(sources(seq)):
                copies.append(
                    pltpu.make_async_copy(source, pieces[k].at[4 + i], sems.at[k, 4 + i])
                )
        for c in copies:
            c.start()
        for c in copies:
            c.wait()

    @pl.when(core == 0)
    def _():
        extras(lambda seq: (memory.at[seq], frames.at[0, seq]))

    @pl.when(core != 0)
    def _():
        extras(lambda seq: (frames.at[1, seq], frames.at[2, seq]))

    for c in shared:
        c.wait()


def cut_state(scalars, frames, hidden, cell, memory):
    anywhere = pl.BlockSpec(memory_space=pl.ANY)
    return pl.pallas_call(
        cut_state_kernel,
        out_shape=[jax.ShapeDtypeStruct((6, 2, CH, GW), BF)] * 4,
        in_specs=[pl.BlockSpec(memory_space=pltpu.SMEM)] + [anywhere] * 4,
        out_specs=[anywhere] * 4,
        scratch_shapes=[pltpu.SemaphoreType.DMA((4, 6))],
        name="cut_state",
    )(scalars, frames, hidden, cell, memory)


ORDER_A = ((1, "HT"), (4, "M"), (0, "HB"), (2, "CB"), (3, "CT"), (5, "F0"))
ORDER_B = ((1, "HT"), (0, "HB"), (2, "CB"), (3, "CT"), (4, "F1"), (5, "F2"))


def open_state_kernel(sc, *refs):
    mine, theirs = refs[:4], refs[4:8]
    low_own, high_own, near_a, near_b, far_a, far_b, rows = refs[8:]
    core, z = sc[0], sc[2]
    for k in range(4):
        at = 2 * lax.rem(z + 4 - k, 4)
        for i in range(2):
            for a in range(6):
                rows[0, a, at + i] = mine[k][a, i]
                rows[1, a, at + i] = theirs[k][a, i]
    other = 1 - core
    for a in range(6):
        for r in range(OWN):
            low_own[a, r] = rows[core, a, 4 * core + r]
            high_own[a, r] = rows[other, a, 4 * core + r]
    for group, order, layout, near, far in (
        (core, ORDER_A, FIRST_A, near_a, far_a),
        (other, ORDER_B, FIRST_B, near_b, far_b),
    ):
        for a, name in order:
            offset, count = layout[name]
            for u in range(count):
                turn = core * (OWN - count) + u
                far[offset + u] = rows[group, a, 4 * core + turn]
                near[offset + u] = rows[group, a, 4 * other + turn]


def open_state(scalars, mine, theirs):
    vmem = pl.BlockSpec(memory_space=pltpu.VMEM)
    shapes = [(6, OWN)] * 2 + [(18,)] * 4
    return pl.pallas_call(
        open_state_kernel,
        out_shape=[jax.ShapeDtypeStruct(s + (CH, GW), BF) for s in shapes],
        in_specs=[pl.BlockSpec(memory_space=pltpu.SMEM)] + [vmem] * 8,
        out_specs=[vmem] * 6,
        scratch_shapes=[pltpu.VMEM((2, 6, 8, CH, GW), BF)],
        compiler_params=pltpu.CompilerParams(vmem_limit_bytes=16 << 20),
        name="open_state",
    )(scalars, *mine, *theirs)


def cut_result_kernel(sc, own, taken, *pieces):
    core, z = sc[0], sc[2]
    for k in range(4):
        to = lax.rem(z + k, 4)
        here = (to // 2) == core
        row = 2 * lax.rem(to, 2)
        for a in range(5):
            for i in range(2):
                pieces[k][a, i] = jnp.where(here, own[a, row + i], taken[a, row + i])


def cut_result(scalars, own, taken):
    vmem = pl.BlockSpec(memory_space=pltpu.VMEM)
    return pl.pallas_call(
        cut_result_kernel,
        out_shape=[jax.ShapeDtypeStruct((5, 2, CH, GW), BF)] * 4,
        in_specs=[pl.BlockSpec(memory_space=pltpu.SMEM), vmem, vmem],
        out_specs=[vmem] * 4,
        compiler_params=pltpu.CompilerParams(vmem_limit_bytes=8 << 20),
        name="cut_result",
    )(scalars, own, taken)


def close_result_kernel(sc, *refs):
    low, high = refs[:4], refs[4:8]
    hidden, cell, memory = refs[8:]
    core, z = sc[0], sc[2]
    for k in range(4):
        seq = lax.rem(z + 4 - k, 4)
        for i in range(2):
            for a in range(5):
                value = jnp.where(core == 0, low[k][a, i], high[k][a, i])
                if a < 2:
                    hidden[a, seq, i] = value
                elif a < 4:
                    cell[a - 2, seq, i] = value
                else:
                    memory[0, seq, i] = value


def close_result(scalars, low, high):
    vmem = pl.BlockSpec(memory_space=pltpu.VMEM)
    shapes = ((2, 4, 2), (2, 4, 2), (1, 4, 2))
    return pl.pallas_call(
        close_result_kernel,
        out_shape=[jax.ShapeDtypeStruct(s + (CH, GW), BF) for s in shapes],
        in_specs=[pl.BlockSpec(memory_space=pltpu.SMEM)] + [vmem] * 8,
        out_specs=[vmem] * 3,
        compiler_params=pltpu.CompilerParams(vmem_limit_bytes=8 << 20),
        name="close_result",
    )(scalars, *low, *high)


def program(frames, hidden_in, cell_in, memory_in, w_x, w_h, w_m, w_o, w_last):
    core = lax.axis_index("layer")
    chip = lax.axis_index("rows")
    chips = lax.axis_size("rows")
    swap = [(0, 1), (1, 0)]
    across = []
    for i in range(chips):
        across.append((chips + i, (i + 4) % chips))
        across.append((i, chips + (i - 4) % chips))

    def to_partner(value):
        return lax.ppermute(value, "layer", swap)

    def to_neighbour(value):
        return lax.ppermute(value, ("layer", "rows"), across)

    def around(value, k, cores=None):
        turn = [(i, 4 * (i // 4) + (i + k) % 4) for i in range(chips)]
        if cores is None:
            return lax.ppermute(value, "rows", turn)
        pairs = [(cores * chips + i, cores * chips + j) for i, j in turn]
        return lax.ppermute(value, ("layer", "rows"), pairs)

    scalars = jnp.stack([core, 8 * (chip // 4) + 4 * core, chip % 4]).astype(jnp.int32)
    turned = [jnp.swapaxes(w, 1, 2) for w in (w_x, w_m, w_o, w_last)]
    own_w = [turned[0], w_h, turned[1], turned[2], turned[3]]
    other_w = [to_partner(w) for w in own_w]
    wa, wb, wc, wo = pack_weights(scalars, own_w, other_w)

    pieces = cut_state(scalars, frames, hidden_in, cell_in, memory_in)
    mine = [pieces[0]] + [around(pieces[k], k) for k in (1, 2, 3)]
    theirs = [to_partner(piece) for piece in mine]
    low_own, high_own, near_a, near_b, message_a, message_b = open_state(scalars, mine, theirs)
    far_a = to_neighbour(message_a)
    far_b = to_neighbour(message_b)

    base = {"sc": scalars, "wa": wa, "wb": wb, "wc": wc, "wo": wo}
    arrays = {"s00": low_own, "s01": high_own, "na": near_a, "fa": far_a, "nb": near_b, "fb": far_b}

    def first(letter, layout, field):
        offset, count = layout[field]
        return ("n" + letter, offset, "f" + letter, offset, count)

    kept = ("HB", "HT", "CB", "CT")
    halo = [{k: first("a", FIRST_A, k) for k in kept}, {k: first("b", FIRST_B, k) for k in kept}]
    states = ["s00", "s01"]
    own_m = ("s00", 4)
    halo_m = first("a", FIRST_A, "M")
    frame_field = (
        (("s00", 5), first("a", FIRST_A, "F0")),
        (("s01", 4), first("b", FIRST_B, "F1")),
        (("s01", 5), first("b", FIRST_B, "F2")),
    )
    steps = frames.shape[0]
    results = [None, None]
    for step in range(steps):
        x_field = frame_field[step]
        for half in range(2):
            send = 2 if step < steps - 1 else 1 - half
            fields = {k: ((states[half], SLOT[k]), halo[half][k]) for k in kept}
            fields["M"] = (own_m, halo_m)
            fields["X"] = x_field
            needed = {f[0][0] for f in fields.values()}
            needed |= {f[1][i] for f in fields.values() for i in (0, 2)}
            operands = dict(base)
            for name in sorted(needed):
                operands[name] = arrays[name]
            plan = {"fields": fields, "half": half, "layer": 2 * half, "send": send}
            tag = f"{step}{half}"
            outs = run_phase(operands, plan)
            results[half] = outs["state"]
            states[half] = "state" + tag
            arrays["state" + tag] = outs["state"]
            own_m = ("state" + tag, SLOT["M"])
            if send:
                arrays["soon" + tag] = to_neighbour(outs["soon"])
                arrays["near" + tag] = to_partner(outs["near"])
                near_at = both(half)
                for k, (o, n) in SOON[half].items():
                    spec = ("near" + tag, near_at[k][0], "soon" + tag, o, n)
                    if k == "M":
                        halo_m = spec
                    else:
                        x_field = (("state" + tag, SLOT["HT"]), spec)
                        halo[half][k] = spec
            if send > 1:
                arrays["late" + tag] = to_neighbour(outs["late"])
                for k, (o, n) in LATE[half].items():
                    halo[half][k] = ("near" + tag, near_at[k][0], "late" + tag, o, n)

    done = []
    for half in range(2):
        taken = lax.ppermute(results[half], "layer", [(1 - half, half)])
        pieces = cut_result(scalars, results[half], taken)
        done.append([pieces[0]] + [around(pieces[k], k, half) for k in (1, 2, 3)])
    return tuple(close_result(scalars, *done))


def solution(mesh):
    return jax.shard_map(
        program,
        mesh=mesh,
        in_specs=(
            P(None, None, "rows", None, None),
            P("layer", None, "rows", None, None),
            P("layer", None, "rows", None, None),
            P(None, "rows", None, None),
            P("layer", None, None),
            P("layer", None, None),
            P("layer", None, None),
            P("layer", None, None),
            P("layer", None, None),
        ),
        out_specs=(
            P("layer", None, "rows", None, None),
            P("layer", None, "rows", None, None),
            P("layer", None, "rows", None, None),
        ),
        check_vma=False,
    )
```

time: 458 us -> 159 us (0.35)
  the two profiles are of different devices: /device:TPU:25 before, /device:TPU:1 now
where the time goes in v2:
time: 159 us
  Pallas kernels  60.7 us (38%)
  starting transfers between devices  55.1 us (35%)
  waiting for transfers between devices  39.8 us (25%)
  local copies, waits for them, and re-layouts  1.62 us (1%)
    pallas_call x6, Pallas kernels, run_phase(): pl.pallas_call(functools.partial(phase_kernel, plan), out_shape=[jax.Shap...  29.6 us
    pallas_call x1, Pallas kernels, cut_state(): pl.pallas_call(cut_state_kernel, out_shape=[jax.ShapeDtypeStruct((6, 2, C...  26 us
    ppermute x14, starting transfers between devices, to_partner(): return lax.ppermute(value, 'layer', swap)  22.6 us
    ppermute x11, waiting for transfers between devices, to_neighbour(): return lax.ppermute(value, ('layer', 'rows'), across)  22.4 us
    ppermute x6, starting transfers between devices, around(): return lax.ppermute(value, ('layer', 'rows'), pairs)  10.7 us
    ppermute x2, starting transfers between devices, program(): taken = lax.ppermute(results[half], 'layer', [(1 - half, half)])  8.54 us
    ppermute x11, starting transfers between devices, to_neighbour(): return lax.ppermute(value, ('layer', 'rows'), across)  7.45 us
    ppermute x3, waiting for transfers between devices, around(): return lax.ppermute(value, 'rows', turn)  7.13 us
  transfers between devices with their start and end apart: 36, of which 16 were waited for; matrix products, arithmetic and copies ran while one was open for 0% of the time, Pallas kernels for 28%

profile of v2, /device:TPU:1, one launch (start us, length us, event | category | flops | bytes accessed | tf_op | source)
XLA Modules:
  0.0 158.8 jit_solution(3263883190064703402)
XLA Ops:
  2.8 26.0 %cut_state.1 = (bf16[6,2,64,128]{3,2,1,0:T(8,128)(2,1)}, bf16[6,2,64,128]{3,2,1,0:T(8,128)(2,1)}, bf16[6,2,64,128]{3,2,1,0:T(8,128)(2,1)}, bf16[6,2,64,128]{3,2,1,0:T(8,128)(2,1)}) custom-call(s32[3]{0:T(128)} %pad_add_fusion.sc.refs_0_, bf16[3,4,2,64,128]{4,3,2,1,0:T(8,128)(2,1)} %frames.1, bf16[2,4,2,64,128]{4,3,2,1,0:T(8,128)(2,1)} %hidden.1, ...), custom_call_target="tpu_custom_call" | custom-call | tf_op jit(solution)/shard_map/cut_state/pallas_call | solution.py:334
  30.6 3.3 %collective-permute-start.6 = (bf16[6,2,64,128]{3,2,1,0:T(8,128)(2,1)}, bf16[6,2,64,128]{3,2,1,0:T(8,128)(2,1)S(1)}, u32[]{:S(2)}, u32[]{:S(2)}) collective-permute-start(bf16[6,2,64,128]{3,2,1,0:T(8,128)(2,1)} %get-tuple-element.50), channel_id=1, source_target_pairs={{0,2},{1,3},{2,0},{3,1},{4,6},{5,7},{6,4},{7,5},{8,10},{9,11},{10,... | collective-permute-start | bytes 589832 | tf_op jit(solution)/shard_map/ppermute | solution.py:461
  35.5 2.6 %collective-permute-done.5.refs_1_ = bf16[6,2,64,128]{3,2,1,0:T(8,128)(2,1)S(1)} collective-permute-done((bf16[6,2,64,128]{3,2,1,0:T(8,128)(2,1)}, bf16[6,2,64,128]{3,2,1,0:T(8,128)(2,1)S(1)}, u32[]{:S(2)}, u32[]{:S(2)}) %collective-permute-start.5) | collective-permute-done | bytes 196640 | tf_op jit(solution)/shard_map/ppermute | solution.py:461
  38.7 4.5 %collective-permute-done.6.refs_2_ = bf16[6,2,64,128]{3,2,1,0:T(8,128)(2,1)S(1)} collective-permute-done((bf16[6,2,64,128]{3,2,1,0:T(8,128)(2,1)}, bf16[6,2,64,128]{3,2,1,0:T(8,128)(2,1)S(1)}, u32[]{:S(2)}, u32[]{:S(2)}) %collective-permute-start.6) | collective-permute-done | bytes 196640 | tf_op jit(solution)/shard_map/ppermute | solution.py:461
  52.6 3.3 %collective-permute-done.13.refs_5_ = bf16[18,64,128]{2,1,0:T(8,128)(2,1)S(1)} collective-permute-done((bf16[18,64,128]{2,1,0:T(8,128)(2,1)S(1)}, bf16[18,64,128]{2,1,0:T(8,128)(2,1)S(1)}, u32[]{:S(2)}, u32[]{:S(2)}) %collective-permute-start.13) | collective-permute-done | bytes 294944 | tf_op jit(solution)/shard_map/ppermute | solution.py:456
  55.8 4.9 %two_layers.6 = (bf16[5,4,64,128]{3,2,1,0:T(8,128)(2,1)S(1)}, bf16[16,64,128]{2,1,0:T(8,128)(2,1)S(1)}, bf16[8,64,128]{2,1,0:T(8,128)(2,1)S(1)}, bf16[8,64,128]{2,1,0:T(8,128)(2,1)S(1)}) custom-call(s32[3]{0:T(128)S(1)} %copy-done.5, bf16[4,256,512]{2,1,0:T(8,128)(2,1)S(1)} %get-tuple-element.44.refs_1_, bf16[4,448,768]{2,1,0:T(8,128)(2,1)S(1)} %get-tuple-element.45.refs_2_, ...), custom_call_target="tpu_custom_call" | custom-call | tf_op jit(solution)/shard_map/two_layers/pallas_call | solution.py:224
  60.8 3.4 %collective-permute-start.15 = (bf16[16,64,128]{2,1,0:T(8,128)(2,1)S(1)}, bf16[16,64,128]{2,1,0:T(8,128)(2,1)S(1)}, u32[]{:S(2)}, u32[]{:S(2)}) collective-permute-start(bf16[16,64,128]{2,1,0:T(8,128)(2,1)S(1)} %get-tuple-element.58), channel_id=1, source_target_pairs={{0,64},{64,0},{1,65},{65,1},{2,66},{66,2},{3,67},{67,3},{4,68},{68... | collective-permute-start | bytes 786440 | tf_op jit(solution)/shard_map/ppermute | solution.py:453
  64.2 4.4 %collective-permute-done.16.refs_9_.refs_11_ = bf16[8,64,128]{2,1,0:T(8,128)(2,1)S(1)} collective-permute-done((bf16[8,64,128]{2,1,0:T(8,128)(2,1)S(1)}, bf16[8,64,128]{2,1,0:T(8,128)(2,1)S(1)}, u32[]{:S(2)}, u32[]{:S(2)}) %collective-permute-start.16) | collective-permute-done | bytes 131104 | tf_op jit(solution)/shard_map/ppermute | solution.py:456
  68.6 4.9 %two_layers.7 = (bf16[5,4,64,128]{3,2,1,0:T(8,128)(2,1)S(1)}, bf16[14,64,128]{2,1,0:T(8,128)(2,1)S(1)}, bf16[4,64,128]{2,1,0:T(8,128)(2,1)S(1)}, bf16[10,64,128]{2,1,0:T(8,128)(2,1)S(1)}) custom-call(s32[3]{0:T(128)S(1)} %copy-done.5, bf16[4,256,512]{2,1,0:T(8,128)(2,1)S(1)} %get-tuple-element.44.refs_1_, ...), custom_call_target="tpu_custom_call" | custom-call | tf_op jit(solution)/shard_map/two_layers/pallas_call | solution.py:224
  73.5 3.7 %collective-permute-start.17 = (bf16[14,64,128]{2,1,0:T(8,128)(2,1)S(1)}, bf16[14,64,128]{2,1,0:T(8,128)(2,1)S(1)}, u32[]{:S(2)}, u32[]{:S(2)}) collective-permute-start(bf16[14,64,128]{2,1,0:T(8,128)(2,1)S(1)} %get-tuple-element.62), channel_id=1, source_target_pairs={{0,64},{64,0},{1,65},{65,1},{2,66},{66,2},{3,67},{67,3},{4,68},{68... | collective-permute-start | bytes 688136 | tf_op jit(solution)/shard_map/ppermute | solution.py:453
  78.9 2.6 %collective-permute-done.14.refs_6_ = bf16[8,64,128]{2,1,0:T(8,128)(2,1)S(1)} collective-permute-done((bf16[8,64,128]{2,1,0:T(8,128)(2,1)S(1)}, bf16[8,64,128]{2,1,0:T(8,128)(2,1)S(1)}, u32[]{:S(2)}, u32[]{:S(2)}) %collective-permute-start.14) | collective-permute-done | bytes 131104 | tf_op jit(solution)/shard_map/ppermute | solution.py:456
  82.3 4.9 %two_layers.8 = (bf16[5,4,64,128]{3,2,1,0:T(8,128)(2,1)S(1)}, bf16[16,64,128]{2,1,0:T(8,128)(2,1)S(1)}, bf16[8,64,128]{2,1,0:T(8,128)(2,1)S(1)}, bf16[8,64,128]{2,1,0:T(8,128)(2,1)S(1)}) custom-call(s32[3]{0:T(128)S(1)} %copy-done.5, bf16[4,256,512]{2,1,0:T(8,128)(2,1)S(1)} %get-tuple-element.44.refs_1_, bf16[4,448,768]{2,1,0:T(8,128)(2,1)S(1)} %get-tuple-element.45.refs_2_, ...), custom_call_target="tpu_custom_call" | custom-call | tf_op jit(solution)/shard_map/two_layers/pallas_call | solution.py:224
  87.2 7.1 %collective-permute-start.20 = (bf16[16,64,128]{2,1,0:T(8,128)(2,1)S(1)}, bf16[16,64,128]{2,1,0:T(8,128)(2,1)S(1)}, u32[]{:S(2)}, u32[]{:S(2)}) collective-permute-start(bf16[16,64,128]{2,1,0:T(8,128)(2,1)S(1)} %get-tuple-element.66), channel_id=1, source_target_pairs={{0,64},{64,0},{1,65},{65,1},{2,66},{66,2},{3,67},{67,3},{4,68},{68... | collective-permute-start | bytes 786440 | tf_op jit(solution)/shard_map/ppermute | solution.py:453
  96.1 3.0 %collective-permute-done.21.refs_5_ = bf16[10,64,128]{2,1,0:T(8,128)(2,1)S(1)} collective-permute-done((bf16[10,64,128]{2,1,0:T(8,128)(2,1)S(1)}, bf16[10,64,128]{2,1,0:T(8,128)(2,1)S(1)}, u32[]{:S(2)}, u32[]{:S(2)}) %collective-permute-start.21) | collective-permute-done | bytes 163872 | tf_op jit(solution)/shard_map/ppermute | solution.py:456
  100.8 4.9 %two_layers.9 = (bf16[5,4,64,128]{3,2,1,0:T(8,128)(2,1)S(1)}, bf16[14,64,128]{2,1,0:T(8,128)(2,1)S(1)}, bf16[4,64,128]{2,1,0:T(8,128)(2,1)S(1)}, bf16[10,64,128]{2,1,0:T(8,128)(2,1)S(1)}) custom-call(s32[3]{0:T(128)S(1)} %copy-done.5, bf16[4,256,512]{2,1,0:T(8,128)(2,1)S(1)} %get-tuple-element.44.refs_1_, ...), custom_call_target="tpu_custom_call" | custom-call | tf_op jit(solution)/shard_map/two_layers/pallas_call | solution.py:224
  105.8 3.2 %collective-permute-start.23 = (bf16[14,64,128]{2,1,0:T(8,128)(2,1)S(1)}, bf16[14,64,128]{2,1,0:T(8,128)(2,1)S(1)}, u32[]{:S(2)}, u32[]{:S(2)}) collective-permute-start(bf16[14,64,128]{2,1,0:T(8,128)(2,1)S(1)} %get-tuple-element.70), channel_id=1, source_target_pairs={{0,64},{64,0},{1,65},{65,1},{2,66},{66,2},{3,67},{67,3},{4,68},{68... | collective-permute-start | bytes 688136 | tf_op jit(solution)/shard_map/ppermute | solution.py:453
  114.0 4.9 %two_layers.10 = (bf16[5,4,64,128]{3,2,1,0:T(8,128)(2,1)S(1)}, bf16[8,64,128]{2,1,0:T(8,128)(2,1)S(1)}, bf16[8,64,128]{2,1,0:T(8,128)(2,1)S(1)}) custom-call(s32[3]{0:T(128)S(1)} %copy-done.5, bf16[4,256,512]{2,1,0:T(8,128)(2,1)S(1)} %get-tuple-element.44.refs_1_, bf16[4,448,768]{2,1,0:T(8,128)(2,1)S(1)} %get-tuple-element.45.refs_2_, ...), custom_call_target="tpu_custom_call" | custom-call | tf_op jit(solution)/shard_map/two_layers/pallas_call | solution.py:224
  119.0 7.2 %collective-permute-start.25 = (bf16[5,4,64,128]{3,2,1,0:T(8,128)(2,1)S(1)}, bf16[5,4,64,128]{3,2,1,0:T(8,128)(2,1)S(1)}, u32[]{:S(2)}, u32[]{:S(2)}) collective-permute-start(bf16[5,4,64,128]{3,2,1,0:T(8,128)(2,1)S(1)} %get-tuple-element.73.own.refs_10_), channel_id=1, source_target_pairs={{64,0},{65,1},{66,2},{67,3},{68,4},{69,5},{70,6},{71,7},{72,8},{73... | collective-permute-start | bytes 983048 | tf_op jit(solution)/shard_map/ppermute | solution.py:534
  127.6 3.4 %collective-permute-done.31.refs_8_ = bf16[8,64,128]{2,1,0:T(8,128)(2,1)S(1)} collective-permute-done((bf16[8,64,128]{2,1,0:T(8,128)(2,1)S(1)}, bf16[8,64,128]{2,1,0:T(8,128)(2,1)S(1)}, u32[]{:S(2)}, u32[]{:S(2)}) %collective-permute-start.31) | collective-permute-done | bytes 131104 | tf_op jit(solution)/shard_map/ppermute | solution.py:456
  131.0 4.9 %two_layers.11.own = bf16[5,4,64,128]{3,2,1,0:T(8,128)(2,1)S(1)} custom-call(s32[3]{0:T(128)S(1)} %copy-done.5, bf16[4,256,512]{2,1,0:T(8,128)(2,1)S(1)} %get-tuple-element.44.refs_1_, bf16[4,448,768]{2,1,0:T(8,128)(2,1)S(1)} %get-tuple-element.45.refs_2_, bf16[4,192,448]{2,1,0:T(8,128)(2,1)S(1)} %get-tuple-element.46.refs_3_, ...), custom_call_target="tpu_custom_call" | custom-call | tf_op jit(solution)/shard_map/two_layers/pallas_call | solution.py:224
  144.5 3.9 %collective-permute-start.34 = (bf16[5,2,64,128]{3,2,1,0:T(8,128)(2,1)S(1)}, bf16[5,2,64,128]{3,2,1,0:T(8,128)(2,1)S(1)}, u32[]{:S(2)}, u32[]{:S(2)}) collective-permute-start(bf16[5,2,64,128]{3,2,1,0:T(8,128)(2,1)S(1)} %get-tuple-element.83), channel_id=1, source_target_pairs={{64,66},{65,67},{66,64},{67,65},{68,70},{69,71},{70,68},{71,69},{7... | collective-permute-start | bytes 491528 | tf_op jit(solution)/shard_map/ppermute | solution.py:463
  148.4 2.9 %collective-permute-start.35 = (bf16[5,2,64,128]{3,2,1,0:T(8,128)(2,1)S(1)}, bf16[5,2,64,128]{3,2,1,0:T(8,128)(2,1)S(1)}, u32[]{:S(2)}, u32[]{:S(2)}) collective-permute-start(bf16[5,2,64,128]{3,2,1,0:T(8,128)(2,1)S(1)} %get-tuple-element.84), channel_id=1, source_target_pairs={{64,67},{65,64},{66,65},{67,66},{68,71},{69,68},{70,69},{71,70},{7... | collective-permute-start | bytes 491528 | tf_op jit(solution)/shard_map/ppermute | solution.py:463
  151.3 3.2 %collective-permute-done.33.refs_5_ = bf16[5,2,64,128]{3,2,1,0:T(8,128)(2,1)S(1)} collective-permute-done((bf16[5,2,64,128]{3,2,1,0:T(8,128)(2,1)S(1)}, bf16[5,2,64,128]{3,2,1,0:T(8,128)(2,1)S(1)}, u32[]{:S(2)}, u32[]{:S(2)}) %collective-permute-start.33) | collective-permute-done | bytes 163872 | tf_op jit(solution)/shard_map/ppermute | solution.py:463
  154.5 2.8 %collective-permute-done.35.refs_7_ = bf16[5,2,64,128]{3,2,1,0:T(8,128)(2,1)S(1)} collective-permute-done((bf16[5,2,64,128]{3,2,1,0:T(8,128)(2,1)S(1)}, bf16[5,2,64,128]{3,2,1,0:T(8,128)(2,1)S(1)}, u32[]{:S(2)}, u32[]{:S(2)}) %collective-permute-start.35) | collective-permute-done | bytes 163872 | tf_op jit(solution)/shard_map/ppermute | solution.py:463
  (75 shorter events, 37.9 us)
Async XLA Ops:
  0.6 50.5 %collective-permute-start = (bf16[2,448,576]{2,1,0:T(8,128)(2,1)}, bf16[2,448,576]{2,1,0:T(8,128)(2,1)S(1)}, u32[]{:S(2)}, u32[]{:S(2)}) collective-permute-start(bf16[2,448,576]{2,1,0:T(8,128)(2,1)} %bitcast.7), channel_id=1, source_target_pairs={{0,64},{64,0},{1,65},{65,1},{2,66},{66,2},{3,67},{67,3},{4,68},{68... | collective-permute-start | bytes 3096584 | tf_op jit(solution)/shard_map/ppermute | solution.py:453
  28.7 9.4 %collective-permute-start.5 = (bf16[6,2,64,128]{3,2,1,0:T(8,128)(2,1)}, bf16[6,2,64,128]{3,2,1,0:T(8,128)(2,1)S(1)}, u32[]{:S(2)}, u32[]{:S(2)}) collective-permute-start(bf16[6,2,64,128]{3,2,1,0:T(8,128)(2,1)} %get-tuple-element.49), channel_id=1, source_target_pairs={{0,1},{1,2},{2,3},{3,0},{4,5},{5,6},{6,7},{7,4},{8,9},{9,10},{10,1... | collective-permute-start | bytes 589832 | tf_op jit(solution)/shard_map/ppermute | solution.py:461
  30.6 12.7 %collective-permute-start.6 = (bf16[6,2,64,128]{3,2,1,0:T(8,128)(2,1)}, bf16[6,2,64,128]{3,2,1,0:T(8,128)(2,1)S(1)}, u32[]{:S(2)}, u32[]{:S(2)}) collective-permute-start(bf16[6,2,64,128]{3,2,1,0:T(8,128)(2,1)} %get-tuple-element.50), channel_id=1, source_target_pairs={{0,2},{1,3},{2,0},{3,1},{4,6},{5,7},{6,4},{7,5},{8,10},{9,11},{10,... | collective-permute-start | bytes 589832 | tf_op jit(solution)/shard_map/ppermute | solution.py:461
  33.9 10.3 %collective-permute-start.7 = (bf16[6,2,64,128]{3,2,1,0:T(8,128)(2,1)}, bf16[6,2,64,128]{3,2,1,0:T(8,128)(2,1)S(1)}, u32[]{:S(2)}, u32[]{:S(2)}) collective-permute-start(bf16[6,2,64,128]{3,2,1,0:T(8,128)(2,1)} %get-tuple-element.51), channel_id=1, source_target_pairs={{0,3},{1,0},{2,1},{3,2},{4,7},{5,4},{6,5},{7,6},{8,11},{9,8},{10,9... | collective-permute-start | bytes 589832 | tf_op jit(solution)/shard_map/ppermute | solution.py:461
  34.6 9.6 %collective-permute-start.8 = (bf16[6,2,64,128]{3,2,1,0:T(8,128)(2,1)}, bf16[6,2,64,128]{3,2,1,0:T(8,128)(2,1)S(1)}, u32[]{:S(2)}, u32[]{:S(2)}) collective-permute-start(bf16[6,2,64,128]{3,2,1,0:T(8,128)(2,1)} %get-tuple-element.48.refs_0_), channel_id=1, source_target_pairs={{0,64},{64,0},{1,65},{65,1},{2,66},{66,2},{3,67},{67,3},{4,68},{68... | collective-permute-start | bytes 589832 | tf_op jit(solution)/shard_map/ppermute | solution.py:453
  38.1 6.5 %collective-permute-start.9 = (bf16[6,2,64,128]{3,2,1,0:T(8,128)(2,1)S(1)}, bf16[6,2,64,128]{3,2,1,0:T(8,128)(2,1)S(1)}, u32[]{:S(2)}, u32[]{:S(2)}) collective-permute-start(bf16[6,2,64,128]{3,2,1,0:T(8,128)(2,1)S(1)} %collective-permute-done.5.refs_1_), channel_id=1, source_target_pairs={{0,64},{64,0},{1,65},{65,1},{2,66},{66,2},{3,67},{67,3},{4,68},{68... | collective-permute-start | bytes 589832 | tf_op jit(solution)/shard_map/ppermute | solution.py:453
  43.2 7.9 %collective-permute-start.1 = (bf16[2,576,256]{2,1,0:T(8,128)(2,1)}, bf16[2,576,256]{2,1,0:T(8,128)(2,1)S(1)}, u32[]{:S(2)}, u32[]{:S(2)}) collective-permute-start(bf16[2,576,256]{2,1,0:T(8,128)(2,1)} %refs_1_.1), channel_id=1, source_target_pairs={{0,64},{64,0},{1,65},{65,1},{2,66},{66,2},{3,67},{67,3},{4,68},{68... | collective-permute-start | bytes 1769480 | tf_op jit(solution)/shard_map/ppermute | solution.py:453
  44.7 6.5 %collective-permute-start.2 = (bf16[2,192,576]{2,1,0:T(8,128)(2,1)}, bf16[2,192,576]{2,1,0:T(8,128)(2,1)S(1)}, u32[]{:S(2)}, u32[]{:S(2)}) collective-permute-start(bf16[2,192,576]{2,1,0:T(8,128)(2,1)} %bitcast.9), channel_id=1, source_target_pairs={{0,64},{64,0},{1,65},{65,1},{2,66},{66,2},{3,67},{67,3},{4,68},{68... | collective-permute-start | bytes 1327112 | tf_op jit(solution)/shard_map/ppermute | solution.py:453
  49.3 6.5 %collective-permute-start.13 = (bf16[18,64,128]{2,1,0:T(8,128)(2,1)S(1)}, bf16[18,64,128]{2,1,0:T(8,128)(2,1)S(1)}, u32[]{:S(2)}, u32[]{:S(2)}) collective-permute-start(bf16[18,64,128]{2,1,0:T(8,128)(2,1)S(1)} %get-tuple-element.53), channel_id=1, source_target_pairs={{64,4},{0,124},{65,5},{1,125},{66,6},{2,126},{67,7},{3,127},{68,8}... | collective-permute-start | bytes 884744 | tf_op jit(solution)/shard_map/ppermute | solution.py:456
  50.7 13.4 %collective-permute-start.12 = (bf16[18,64,128]{2,1,0:T(8,128)(2,1)S(1)}, bf16[18,64,128]{2,1,0:T(8,128)(2,1)S(1)}, u32[]{:S(2)}, u32[]{:S(2)}) collective-permute-start(bf16[18,64,128]{2,1,0:T(8,128)(2,1)S(1)} %get-tuple-element.52), channel_id=1, source_target_pairs={{64,4},{0,124},{65,5},{1,125},{66,6},{2,126},{67,7},{3,127},{68,8}... | collective-permute-start | bytes 884744 | tf_op jit(solution)/shard_map/ppermute | solution.py:456
  60.8 7.8 %collective-permute-start.15 = (bf16[16,64,128]{2,1,0:T(8,128)(2,1)S(1)}, bf16[16,64,128]{2,1,0:T(8,128)(2,1)S(1)}, u32[]{:S(2)}, u32[]{:S(2)}) collective-permute-start(bf16[16,64,128]{2,1,0:T(8,128)(2,1)S(1)} %get-tuple-element.58), channel_id=1, source_target_pairs={{0,64},{64,0},{1,65},{65,1},{2,66},{66,2},{3,67},{67,3},{4,68},{68... | collective-permute-start | bytes 786440 | tf_op jit(solution)/shard_map/ppermute | solution.py:453
  73.5 8.8 %collective-permute-start.17 = (bf16[14,64,128]{2,1,0:T(8,128)(2,1)S(1)}, bf16[14,64,128]{2,1,0:T(8,128)(2,1)S(1)}, u32[]{:S(2)}, u32[]{:S(2)}) collective-permute-start(bf16[14,64,128]{2,1,0:T(8,128)(2,1)S(1)} %get-tuple-element.62), channel_id=1, source_target_pairs={{0,64},{64,0},{1,65},{65,1},{2,66},{66,2},{3,67},{67,3},{4,68},{68... | collective-permute-start | bytes 688136 | tf_op jit(solution)/shard_map/ppermute | solution.py:453
  87.2 13.6 %collective-permute-start.20 = (bf16[16,64,128]{2,1,0:T(8,128)(2,1)S(1)}, bf16[16,64,128]{2,1,0:T(8,128)(2,1)S(1)}, u32[]{:S(2)}, u32[]{:S(2)}) collective-permute-start(bf16[16,64,128]{2,1,0:T(8,128)(2,1)S(1)} %get-tuple-element.66), channel_id=1, source_target_pairs={{0,64},{64,0},{1,65},{65,1},{2,66},{66,2},{3,67},{67,3},{4,68},{68... | collective-permute-start | bytes 786440 | tf_op jit(solution)/shard_map/ppermute | solution.py:453
  94.4 6.4 %collective-permute-start.22 = (bf16[8,64,128]{2,1,0:T(8,128)(2,1)S(1)}, bf16[8,64,128]{2,1,0:T(8,128)(2,1)S(1)}, u32[]{:S(2)}, u32[]{:S(2)}) collective-permute-start(bf16[8,64,128]{2,1,0:T(8,128)(2,1)S(1)} %get-tuple-element.68), channel_id=1, source_target_pairs={{64,4},{0,124},{65,5},{1,125},{66,6},{2,126},{67,7},{3,127},{68,8}... | collective-permute-start | bytes 393224 | tf_op jit(solution)/shard_map/ppermute | solution.py:456
  105.8 8.3 %collective-permute-start.23 = (bf16[14,64,128]{2,1,0:T(8,128)(2,1)S(1)}, bf16[14,64,128]{2,1,0:T(8,128)(2,1)S(1)}, u32[]{:S(2)}, u32[]{:S(2)}) collective-permute-start(bf16[14,64,128]{2,1,0:T(8,128)(2,1)S(1)} %get-tuple-element.70), channel_id=1, source_target_pairs={{0,64},{64,0},{1,65},{65,1},{2,66},{66,2},{3,67},{67,3},{4,68},{68... | collective-permute-start | bytes 688136 | tf_op jit(solution)/shard_map/ppermute | solution.py:453
  110.7 16.0 %collective-permute-start.29 = (bf16[10,64,128]{2,1,0:T(8,128)(2,1)S(1)}, bf16[10,64,128]{2,1,0:T(8,128)(2,1)S(1)}, u32[]{:S(2)}, u32[]{:S(2)}) collective-permute-start(bf16[10,64,128]{2,1,0:T(8,128)(2,1)S(1)} %get-tuple-element.78), channel_id=1, source_target_pairs={{64,4},{0,124},{65,5},{1,125},{66,6},{2,126},{67,7},{3,127},{68,8}... | collective-permute-start | bytes 491528 | tf_op jit(solution)/shard_map/ppermute | solution.py:456
  119.0 18.3 %collective-permute-start.25 = (bf16[5,4,64,128]{3,2,1,0:T(8,128)(2,1)S(1)}, bf16[5,4,64,128]{3,2,1,0:T(8,128)(2,1)S(1)}, u32[]{:S(2)}, u32[]{:S(2)}) collective-permute-start(bf16[5,4,64,128]{3,2,1,0:T(8,128)(2,1)S(1)} %get-tuple-element.73.own.refs_10_), channel_id=1, source_target_pairs={{64,0},{65,1},{66,2},{67,3},{68,4},{69,5},{70,6},{71,7},{72,8},{73... | collective-permute-start | bytes 983048 | tf_op jit(solution)/shard_map/ppermute | solution.py:534
  135.9 5.9 %collective-permute-start.32 = (bf16[5,4,64,128]{3,2,1,0:T(8,128)(2,1)S(1)}, bf16[5,4,64,128]{3,2,1,0:T(8,128)(2,1)S(1)}, u32[]{:S(2)}, u32[]{:S(2)}) collective-permute-start(bf16[5,4,64,128]{3,2,1,0:T(8,128)(2,1)S(1)} %two_layers.11.own), channel_id=1, source_target_pairs={{0,64},{1,65},{2,66},{3,67},{4,68},{5,69},{6,70},{7,71},{8,72},{9,... | collective-permute-start | bytes 983048 | tf_op jit(solution)/shard_map/ppermute | solution.py:534
  138.0 10.4 %collective-permute-start.26 = (bf16[5,2,64,128]{3,2,1,0:T(8,128)(2,1)S(1)}, bf16[5,2,64,128]{3,2,1,0:T(8,128)(2,1)S(1)}, u32[]{:S(2)}, u32[]{:S(2)}) collective-permute-start(bf16[5,2,64,128]{3,2,1,0:T(8,128)(2,1)S(1)} %get-tuple-element.75), channel_id=1, source_target_pairs={{0,1},{1,2},{2,3},{3,0},{4,5},{5,6},{6,7},{7,4},{8,9},{9,10},{10,1... | collective-permute-start | bytes 491528 | tf_op jit(solution)/shard_map/ppermute | solution.py:463
  138.7 12.6 %collective-permute-start.27 = (bf16[5,2,64,128]{3,2,1,0:T(8,128)(2,1)S(1)}, bf16[5,2,64,128]{3,2,1,0:T(8,128)(2,1)S(1)}, u32[]{:S(2)}, u32[]{:S(2)}) collective-permute-start(bf16[5,2,64,128]{3,2,1,0:T(8,128)(2,1)S(1)} %get-tuple-element.76), channel_id=1, source_target_pairs={{0,2},{1,3},{2,0},{3,1},{4,6},{5,7},{6,4},{7,5},{8,10},{9,11},{10,... | collective-permute-start | bytes 491528 | tf_op jit(solution)/shard_map/ppermute | solution.py:463
  139.3 12.0 %collective-permute-start.28 = (bf16[5,2,64,128]{3,2,1,0:T(8,128)(2,1)S(1)}, bf16[5,2,64,128]{3,2,1,0:T(8,128)(2,1)S(1)}, u32[]{:S(2)}, u32[]{:S(2)}) collective-permute-start(bf16[5,2,64,128]{3,2,1,0:T(8,128)(2,1)S(1)} %get-tuple-element.77), channel_id=1, source_target_pairs={{0,3},{1,0},{2,1},{3,2},{4,7},{5,4},{6,5},{7,6},{8,11},{9,8},{10,9... | collective-permute-start | bytes 491528 | tf_op jit(solution)/shard_map/ppermute | solution.py:463
  142.5 11.9 %collective-permute-start.33 = (bf16[5,2,64,128]{3,2,1,0:T(8,128)(2,1)S(1)}, bf16[5,2,64,128]{3,2,1,0:T(8,128)(2,1)S(1)}, u32[]{:S(2)}, u32[]{:S(2)}) collective-permute-start(bf16[5,2,64,128]{3,2,1,0:T(8,128)(2,1)S(1)} %get-tuple-element.82), channel_id=1, source_target_pairs={{64,65},{65,66},{66,67},{67,64},{68,69},{69,70},{70,71},{71,68},{7... | collective-permute-start | bytes 491528 | tf_op jit(solution)/shard_map/ppermute | solution.py:463
  144.5 10.0 %collective-permute-start.34 = (bf16[5,2,64,128]{3,2,1,0:T(8,128)(2,1)S(1)}, bf16[5,2,64,128]{3,2,1,0:T(8,128)(2,1)S(1)}, u32[]{:S(2)}, u32[]{:S(2)}) collective-permute-start(bf16[5,2,64,128]{3,2,1,0:T(8,128)(2,1)S(1)} %get-tuple-element.83), channel_id=1, source_target_pairs={{64,66},{65,67},{66,64},{67,65},{68,70},{69,71},{70,68},{71,69},{7... | collective-permute-start | bytes 491528 | tf_op jit(solution)/shard_map/ppermute | solution.py:463
  148.4 8.8 %collective-permute-start.35 = (bf16[5,2,64,128]{3,2,1,0:T(8,128)(2,1)S(1)}, bf16[5,2,64,128]{3,2,1,0:T(8,128)(2,1)S(1)}, u32[]{:S(2)}, u32[]{:S(2)}) collective-permute-start(bf16[5,2,64,128]{3,2,1,0:T(8,128)(2,1)S(1)} %get-tuple-element.84), channel_id=1, source_target_pairs={{64,67},{65,64},{66,65},{67,66},{68,71},{69,68},{70,69},{71,70},{7... | collective-permute-start | bytes 491528 | tf_op jit(solution)/shard_map/ppermute | solution.py:463
  (19 other events, 264.4 us)

commit v3 on v2

--- a/solution.py
+++ b/solution.py
@@ -288,55 +288,26 @@
     )(scalars, *own, *other)
 
 
-def cut_state_kernel(sc, frames, hidden, cell, memory, *rest):
-    pieces, sems = rest[:4], rest[4]
-    core, z = sc[0], sc[2]
-    shared = []
+def cut_state_kernel(sc, frames, hidden, cell, memory, *pieces):
+    first_core, z = sc[0] == 0, sc[2]
     for k in range(4):
         seq = lax.rem(z + k, 4)
-        for l in range(2):
-            shared.append(
-                pltpu.make_async_copy(hidden.at[l, seq], pieces[k].at[l], sems.at[k, l])
-            )
-            shared.append(
-                pltpu.make_async_copy(cell.at[l, seq], pieces[k].at[2 + l], sems.at[k, 2 + l])
-            )
-    for c in shared:
-        c.start()
-
-    def extras(sources):
-        copies = []
-        for k in range(4):
-            seq = lax.rem(z + k, 4)
-            for i, source in enumerate(sources(seq)):
-                copies.append(
-                    pltpu.make_async_copy(source, pieces[k].at[4 + i], sems.at[k, 4 + i])
-                )
-        for c in copies:
-            c.start()
-        for c in copies:
-            c.wait()
-
-    @pl.when(core == 0)
-    def _():
-        extras(lambda seq: (memory.at[seq], frames.at[0, seq]))
-
-    @pl.when(core != 0)
-    def _():
-        extras(lambda seq: (frames.at[1, seq], frames.at[2, seq]))
-
-    for c in shared:
-        c.wait()
+        for i in range(2):
+            for l in range(2):
+                pieces[k][l, i] = hidden[l, seq, i]
+                pieces[k][2 + l, i] = cell[l, seq, i]
+            pieces[k][4, i] = jnp.where(first_core, memory[seq, i], frames[1, seq, i])
+            pieces[k][5, i] = jnp.where(first_core, frames[0, seq, i], frames[2, seq, i])
 
 
 def cut_state(scalars, frames, hidden, cell, memory):
-    anywhere = pl.BlockSpec(memory_space=pl.ANY)
+    vmem = pl.BlockSpec(memory_space=pltpu.VMEM)
     return pl.pallas_call(
         cut_state_kernel,
         out_shape=[jax.ShapeDtypeStruct((6, 2, CH, GW), BF)] * 4,
-        in_specs=[pl.BlockSpec(memory_space=pltpu.SMEM)] + [anywhere] * 4,
-        out_specs=[anywhere] * 4,
-        scratch_shapes=[pltpu.SemaphoreType.DMA((4, 6))],
+        in_specs=[pl.BlockSpec(memory_space=pltpu.SMEM)] + [vmem] * 4,
+        out_specs=[vmem] * 4,
+        compiler_params=pltpu.CompilerParams(vmem_limit_bytes=8 << 20),
         name="cut_state",
     )(scalars, frames, hidden, cell, memory)
 
@@ -386,7 +357,7 @@
     )(scalars, *mine, *theirs)
 
 
-def cut_result_kernel(sc, own, taken, *pieces):
+def cut_result_kernel(sc, low, high, taken, *pieces):
     core, z = sc[0], sc[2]
     for k in range(4):
         to = lax.rem(z + k, 4)
@@ -394,49 +365,46 @@
         row = 2 * lax.rem(to, 2)
         for a in range(5):
             for i in range(2):
-                pieces[k][a, i] = jnp.where(here, own[a, row + i], taken[a, row + i])
-
-
-def cut_result(scalars, own, taken):
+                own = jnp.where(core == 0, low[a, row + i], high[a, row + i])
+                pieces[k][a, i] = jnp.where(here, own, taken[a, row + i])
+
+
+def cut_result(scalars, low, high, taken):
     vmem = pl.BlockSpec(memory_space=pltpu.VMEM)
     return pl.pallas_call(
         cut_result_kernel,
         out_shape=[jax.ShapeDtypeStruct((5, 2, CH, GW), BF)] * 4,
-        in_specs=[pl.BlockSpec(memory_space=pltpu.SMEM), vmem, vmem],
+        in_specs=[pl.BlockSpec(memory_space=pltpu.SMEM)] + [vmem] * 3,
         out_specs=[vmem] * 4,
         compiler_params=pltpu.CompilerParams(vmem_limit_bytes=8 << 20),
         name="cut_result",
-    )(scalars, own, taken)
+    )(scalars, low, high, taken)
 
 
 def close_result_kernel(sc, *refs):
-    low, high = refs[:4], refs[4:8]
-    hidden, cell, memory = refs[8:]
-    core, z = sc[0], sc[2]
+    parts = refs[:4]
+    hidden, cell, memory = refs[4:]
+    z = sc[2]
     for k in range(4):
         seq = lax.rem(z + 4 - k, 4)
         for i in range(2):
-            for a in range(5):
-                value = jnp.where(core == 0, low[k][a, i], high[k][a, i])
-                if a < 2:
-                    hidden[a, seq, i] = value
-                elif a < 4:
-                    cell[a - 2, seq, i] = value
-                else:
-                    memory[0, seq, i] = value
-
-
-def close_result(scalars, low, high):
+            for a in range(2):
+                hidden[a, seq, i] = parts[k][a, i]
+                cell[a, seq, i] = parts[k][2 + a, i]
+            memory[0, seq, i] = parts[k][4, i]
+
+
+def close_result(scalars, parts):
     vmem = pl.BlockSpec(memory_space=pltpu.VMEM)
     shapes = ((2, 4, 2), (2, 4, 2), (1, 4, 2))
     return pl.pallas_call(
         close_result_kernel,
         out_shape=[jax.ShapeDtypeStruct(s + (CH, GW), BF) for s in shapes],
-        in_specs=[pl.BlockSpec(memory_space=pltpu.SMEM)] + [vmem] * 8,
+        in_specs=[pl.BlockSpec(memory_space=pltpu.SMEM)] + [vmem] * 4,
         out_specs=[vmem] * 3,
         compiler_params=pltpu.CompilerParams(vmem_limit_bytes=8 << 20),
         name="close_result",
-    )(scalars, *low, *high)
+    )(scalars, *parts)
 
 
 def program(frames, hidden_in, cell_in, memory_in, w_x, w_h, w_m, w_o, w_last):
@@ -455,12 +423,9 @@
     def to_neighbour(value):
         return lax.ppermute(value, ("layer", "rows"), across)
 
-    def around(value, k, cores=None):
+    def around(value, k):
         turn = [(i, 4 * (i // 4) + (i + k) % 4) for i in range(chips)]
-        if cores is None:
-            return lax.ppermute(value, "rows", turn)
-        pairs = [(cores * chips + i, cores * chips + j) for i, j in turn]
-        return lax.ppermute(value, ("layer", "rows"), pairs)
+        return lax.ppermute(value, "rows", turn)
 
     scalars = jnp.stack([core, 8 * (chip // 4) + 4 * core, chip % 4]).astype(jnp.int32)
     turned = [jnp.swapaxes(w, 1, 2) for w in (w_x, w_m, w_o, w_last)]
@@ -529,12 +494,11 @@
                 for k, (o, n) in LATE[half].items():
                     halo[half][k] = ("near" + tag, near_at[k][0], "late" + tag, o, n)
 
-    done = []
-    for half in range(2):
-        taken = lax.ppermute(results[half], "layer", [(1 - half, half)])
-        pieces = cut_result(scalars, results[half], taken)
-        done.append([pieces[0]] + [around(pieces[k], k, half) for k in (1, 2, 3)])
-    return tuple(close_result(scalars, *done))
+    give = jnp.where(core == 0, results[1], results[0])
+    taken = to_partner(give)
+    pieces = cut_result(scalars, results[0], results[1], taken)
+    done = [pieces[0]] + [around(pieces[k], k) for k in (1, 2, 3)]
+    return tuple(close_result(scalars, done))
 
 
 def solution(mesh):

time: 159 us -> 136 us (0.86)
  the two profiles are of different devices: /device:TPU:1 before, /device:TPU:0 now
where the time goes in v3:
time: 136 us; the launch traced here: 135 us
  starting transfers between devices  43.9 us (32%)
  waiting for transfers between devices  41.8 us (31%)
  Pallas kernels  36.3 us (27%)
  local copies, waits for them, and re-layouts  12.1 us (9%)
    ppermute x11, starting transfers between devices, to_neighbour(): return lax.ppermute(value, ('layer', 'rows'), across)  31.5 us
    pallas_call x6, Pallas kernels, run_phase(): pl.pallas_call(functools.partial(phase_kernel, plan), out_shape=[jax.Shap...  31.3 us
    ppermute x11, waiting for transfers between devices, to_neighbour(): return lax.ppermute(value, ('layer', 'rows'), across)  22.3 us
    ppermute x6, waiting for transfers between devices, around(): return lax.ppermute(value, 'rows', turn)  16.2 us
    unnamed x42, local copies, waits for them, and re-layouts  12.1 us
    ppermute x6, starting transfers between devices, around(): return lax.ppermute(value, 'rows', turn)  10.6 us
    ppermute x15, waiting for transfers between devices, to_partner(): return lax.ppermute(value, 'layer', swap)  3.36 us
  transfers between devices with their start and end apart: 32, of which 16 were waited for; matrix products, arithmetic and copies ran while one was open for 0% of the time, Pallas kernels for 10%

profile of v3, /device:TPU:0, one launch (start us, length us, event | category | flops | bytes accessed | tf_op | source)
XLA Modules:
  0.0 135.1 jit_solution(5843406780189862436)
XLA Ops:
  5.3 2.1 %collective-permute-start.5 = (bf16[6,2,64,128]{3,2,1,0:T(8,128)(2,1)S(1)}, bf16[6,2,64,128]{3,2,1,0:T(8,128)(2,1)S(1)}, u32[]{:S(2)}, u32[]{:S(2)}) collective-permute-start(bf16[6,2,64,128]{3,2,1,0:T(8,128)(2,1)S(1)} %get-tuple-element.45), channel_id=1, source_target_pairs={{0,1},{1,2},{2,3},{3,0},{4,5},{5,6},{6,7},{7,4},{8,9},{9,10},{10,1... | collective-permute-start | bytes 589832 | tf_op jit(solution)/shard_map/ppermute | solution.py:428
  7.4 3.6 %collective-permute-start.6 = (bf16[6,2,64,128]{3,2,1,0:T(8,128)(2,1)S(1)}, bf16[6,2,64,128]{3,2,1,0:T(8,128)(2,1)S(1)}, u32[]{:S(2)}, u32[]{:S(2)}) collective-permute-start(bf16[6,2,64,128]{3,2,1,0:T(8,128)(2,1)S(1)} %get-tuple-element.46), channel_id=1, source_target_pairs={{0,2},{1,3},{2,0},{3,1},{4,6},{5,7},{6,4},{7,5},{8,10},{9,11},{10,... | collective-permute-start | bytes 589832 | tf_op jit(solution)/shard_map/ppermute | solution.py:428
  12.0 3.1 %collective-permute-done.5.refs_1_ = bf16[6,2,64,128]{3,2,1,0:T(8,128)(2,1)S(1)} collective-permute-done((bf16[6,2,64,128]{3,2,1,0:T(8,128)(2,1)S(1)}, bf16[6,2,64,128]{3,2,1,0:T(8,128)(2,1)S(1)}, u32[]{:S(2)}, u32[]{:S(2)}) %collective-permute-start.5) | collective-permute-done | bytes 196640 | tf_op jit(solution)/shard_map/ppermute | solution.py:428
  15.1 5.4 %collective-permute-done.6.refs_2_ = bf16[6,2,64,128]{3,2,1,0:T(8,128)(2,1)S(1)} collective-permute-done((bf16[6,2,64,128]{3,2,1,0:T(8,128)(2,1)S(1)}, bf16[6,2,64,128]{3,2,1,0:T(8,128)(2,1)S(1)}, u32[]{:S(2)}, u32[]{:S(2)}) %collective-permute-start.6) | collective-permute-done | bytes 196640 | tf_op jit(solution)/shard_map/ppermute | solution.py:428
  24.4 5.1 %collective-permute-start.13 = (bf16[18,64,128]{2,1,0:T(8,128)(2,1)S(1)}, bf16[18,64,128]{2,1,0:T(8,128)(2,1)S(1)}, u32[]{:S(2)}, u32[]{:S(2)}) collective-permute-start(bf16[18,64,128]{2,1,0:T(8,128)(2,1)S(1)} %get-tuple-element.49), channel_id=1, source_target_pairs={{64,4},{0,124},{65,5},{1,125},{66,6},{2,126},{67,7},{3,127},{68,8}... | collective-permute-start | bytes 884744 | tf_op jit(solution)/shard_map/ppermute | solution.py:424
  33.8 4.9 %two_layers.6 = (bf16[5,4,64,128]{3,2,1,0:T(8,128)(2,1)S(1)}, bf16[16,64,128]{2,1,0:T(8,128)(2,1)S(1)}, bf16[8,64,128]{2,1,0:T(8,128)(2,1)S(1)}, bf16[8,64,128]{2,1,0:T(8,128)(2,1)S(1)}) custom-call(s32[3]{0:T(128)S(1)} %pad_add_fusion.sc.refs_0_, bf16[4,256,512]{2,1,0:T(8,128)(2,1)S(1)} %get-tuple-element.40.refs_1_, ...), custom_call_target="tpu_custom_call" | custom-call | tf_op jit(solution)/shard_map/two_layers/pallas_call | solution.py:224
  38.9 5.3 %collective-permute-start.16 = (bf16[8,64,128]{2,1,0:T(8,128)(2,1)S(1)}, bf16[8,64,128]{2,1,0:T(8,128)(2,1)S(1)}, u32[]{:S(2)}, u32[]{:S(2)}) collective-permute-start(bf16[8,64,128]{2,1,0:T(8,128)(2,1)S(1)} %get-tuple-element.56), channel_id=1, source_target_pairs={{64,4},{0,124},{65,5},{1,125},{66,6},{2,126},{67,7},{3,127},{68,8}... | collective-permute-start | bytes 393224 | tf_op jit(solution)/shard_map/ppermute | solution.py:424
  44.2 2.7 %collective-permute-done.16.refs_9_.refs_11_ = bf16[8,64,128]{2,1,0:T(8,128)(2,1)S(1)} collective-permute-done((bf16[8,64,128]{2,1,0:T(8,128)(2,1)S(1)}, bf16[8,64,128]{2,1,0:T(8,128)(2,1)S(1)}, u32[]{:S(2)}, u32[]{:S(2)}) %collective-permute-start.16) | collective-permute-done | bytes 131104 | tf_op jit(solution)/shard_map/ppermute | solution.py:424
  46.8 4.9 %two_layers.7 = (bf16[5,4,64,128]{3,2,1,0:T(8,128)(2,1)S(1)}, bf16[14,64,128]{2,1,0:T(8,128)(2,1)S(1)}, bf16[4,64,128]{2,1,0:T(8,128)(2,1)S(1)}, bf16[10,64,128]{2,1,0:T(8,128)(2,1)S(1)}) custom-call(s32[3]{0:T(128)S(1)} %pad_add_fusion.sc.refs_0_, bf16[4,256,512]{2,1,0:T(8,128)(2,1)S(1)} %get-tuple-element.40.refs_1_, ...), custom_call_target="tpu_custom_call" | custom-call | tf_op jit(solution)/shard_map/two_layers/pallas_call | solution.py:224
  51.8 5.1 %collective-permute-start.14 = (bf16[8,64,128]{2,1,0:T(8,128)(2,1)S(1)}, bf16[8,64,128]{2,1,0:T(8,128)(2,1)S(1)}, u32[]{:S(2)}, u32[]{:S(2)}) collective-permute-start(bf16[8,64,128]{2,1,0:T(8,128)(2,1)S(1)} %get-tuple-element.52), channel_id=1, source_target_pairs={{64,4},{0,124},{65,5},{1,125},{66,6},{2,126},{67,7},{3,127},{68,8}... | collective-permute-start | bytes 393224 | tf_op jit(solution)/shard_map/ppermute | solution.py:424
  57.1 2.6 %collective-permute-done.14.refs_6_ = bf16[8,64,128]{2,1,0:T(8,128)(2,1)S(1)} collective-permute-done((bf16[8,64,128]{2,1,0:T(8,128)(2,1)S(1)}, bf16[8,64,128]{2,1,0:T(8,128)(2,1)S(1)}, u32[]{:S(2)}, u32[]{:S(2)}) %collective-permute-start.14) | collective-permute-done | bytes 131104 | tf_op jit(solution)/shard_map/ppermute | solution.py:424
  59.6 4.4 %collective-permute-done.18.refs_12_ = bf16[4,64,128]{2,1,0:T(8,128)(2,1)S(1)} collective-permute-done((bf16[4,64,128]{2,1,0:T(8,128)(2,1)S(1)}, bf16[4,64,128]{2,1,0:T(8,128)(2,1)S(1)}, u32[]{:S(2)}, u32[]{:S(2)}) %collective-permute-start.18) | collective-permute-done | bytes 65568 | tf_op jit(solution)/shard_map/ppermute | solution.py:424
  64.0 4.9 %two_layers.8 = (bf16[5,4,64,128]{3,2,1,0:T(8,128)(2,1)S(1)}, bf16[16,64,128]{2,1,0:T(8,128)(2,1)S(1)}, bf16[8,64,128]{2,1,0:T(8,128)(2,1)S(1)}, bf16[8,64,128]{2,1,0:T(8,128)(2,1)S(1)}) custom-call(s32[3]{0:T(128)S(1)} %pad_add_fusion.sc.refs_0_, bf16[4,256,512]{2,1,0:T(8,128)(2,1)S(1)} %get-tuple-element.40.refs_1_, ...), custom_call_target="tpu_custom_call" | custom-call | tf_op jit(solution)/shard_map/two_layers/pallas_call | solution.py:224
  70.5 3.7 %collective-permute-start.22 = (bf16[8,64,128]{2,1,0:T(8,128)(2,1)S(1)}, bf16[8,64,128]{2,1,0:T(8,128)(2,1)S(1)}, u32[]{:S(2)}, u32[]{:S(2)}) collective-permute-start(bf16[8,64,128]{2,1,0:T(8,128)(2,1)S(1)} %get-tuple-element.64), channel_id=1, source_target_pairs={{64,4},{0,124},{65,5},{1,125},{66,6},{2,126},{67,7},{3,127},{68,8}... | collective-permute-start | bytes 393224 | tf_op jit(solution)/shard_map/ppermute | solution.py:424
  74.2 3.0 %collective-permute-done.21.refs_5_ = bf16[10,64,128]{2,1,0:T(8,128)(2,1)S(1)} collective-permute-done((bf16[10,64,128]{2,1,0:T(8,128)(2,1)S(1)}, bf16[10,64,128]{2,1,0:T(8,128)(2,1)S(1)}, u32[]{:S(2)}, u32[]{:S(2)}) %collective-permute-start.21) | collective-permute-done | bytes 163872 | tf_op jit(solution)/shard_map/ppermute | solution.py:424
  78.6 5.6 %two_layers.9 = (bf16[5,4,64,128]{3,2,1,0:T(8,128)(2,1)S(1)}, bf16[14,64,128]{2,1,0:T(8,128)(2,1)S(1)}, bf16[4,64,128]{2,1,0:T(8,128)(2,1)S(1)}, bf16[10,64,128]{2,1,0:T(8,128)(2,1)}) custom-call(s32[3]{0:T(128)S(1)} %pad_add_fusion.sc.refs_0_, bf16[4,256,512]{2,1,0:T(8,128)(2,1)S(1)} %get-tuple-element.40.refs_1_, ...), custom_call_target="tpu_custom_call" | custom-call | tf_op jit(solution)/shard_map/two_layers/pallas_call | solution.py:224
  84.2 3.3 %collective-permute-start.19 = (bf16[8,64,128]{2,1,0:T(8,128)(2,1)S(1)}, bf16[8,64,128]{2,1,0:T(8,128)(2,1)S(1)}, u32[]{:S(2)}, u32[]{:S(2)}) collective-permute-start(bf16[8,64,128]{2,1,0:T(8,128)(2,1)S(1)} %get-tuple-element.61), channel_id=1, source_target_pairs={{64,4},{0,124},{65,5},{1,125},{66,6},{2,126},{67,7},{3,127},{68,8}... | collective-permute-start | bytes 393224 | tf_op jit(solution)/shard_map/ppermute | solution.py:424
  89.2 3.3 %collective-permute-start.25 = (bf16[10,64,128]{2,1,0:T(8,128)(2,1)}, bf16[10,64,128]{2,1,0:T(8,128)(2,1)}, u32[]{:S(2)}, u32[]{:S(2)}) collective-permute-start(bf16[10,64,128]{2,1,0:T(8,128)(2,1)} %get-tuple-element.70), channel_id=1, source_target_pairs={{64,4},{0,124},{65,5},{1,125},{66,6},{2,126},{67,7},{3,127},{68,8}... | collective-permute-start | bytes 491528 | tf_op jit(solution)/shard_map/ppermute | solution.py:424
  92.5 1.9 %collective-permute-done.24.refs_12_ = bf16[4,64,128]{2,1,0:T(8,128)(2,1)S(1)} collective-permute-done((bf16[4,64,128]{2,1,0:T(8,128)(2,1)S(1)}, bf16[4,64,128]{2,1,0:T(8,128)(2,1)S(1)}, u32[]{:S(2)}, u32[]{:S(2)}) %collective-permute-start.24) | collective-permute-done | bytes 65568 | tf_op jit(solution)/shard_map/ppermute | solution.py:424
  94.5 5.6 %two_layers.10 = (bf16[5,4,64,128]{3,2,1,0:T(8,128)(2,1)S(1)}, bf16[8,64,128]{2,1,0:T(8,128)(2,1)}, bf16[8,64,128]{2,1,0:T(8,128)(2,1)}) custom-call(s32[3]{0:T(128)S(1)} %pad_add_fusion.sc.refs_0_, bf16[4,256,512]{2,1,0:T(8,128)(2,1)S(1)} %get-tuple-element.40.refs_1_, bf16[4,448,768]{2,1,0:T(8,128)(2,1)S(1)} %get-tuple-element.41.refs_2_, ...), custom_call_target="tpu_custom_call" | custom-call | tf_op jit(solution)/shard_map/two_layers/pallas_call | solution.py:224
  102.6 6.3 %collective-permute-done.27.refs_8_ = bf16[8,64,128]{2,1,0:T(8,128)(2,1)} collective-permute-done((bf16[8,64,128]{2,1,0:T(8,128)(2,1)}, bf16[8,64,128]{2,1,0:T(8,128)(2,1)}, u32[]{:S(2)}, u32[]{:S(2)}) %collective-permute-start.27) | collective-permute-done | bytes 131104 | tf_op jit(solution)/shard_map/ppermute | solution.py:424
  114.1 5.4 %two_layers.11.high = bf16[5,4,64,128]{3,2,1,0:T(8,128)(2,1)S(1)} custom-call(s32[3]{0:T(128)S(1)} %pad_add_fusion.sc.refs_0_, bf16[4,256,512]{2,1,0:T(8,128)(2,1)S(1)} %copy-done.1, bf16[4,448,768]{2,1,0:T(8,128)(2,1)S(1)} %get-tuple-element.41.refs_2_, bf16[4,192,448]{2,1,0:T(8,128)(2,1)S(1)} %get-tuple-element.42.refs_3_, ...), custom_call_target="tpu_custom_call" | custom-call | tf_op jit(solution)/shard_map/two_layers/pallas_call | solution.py:224
  122.3 2.4 %collective-permute-start.30 = (bf16[5,2,64,128]{3,2,1,0:T(8,128)(2,1)S(1)}, bf16[5,2,64,128]{3,2,1,0:T(8,128)(2,1)S(1)}, u32[]{:S(2)}, u32[]{:S(2)}) collective-permute-start(bf16[5,2,64,128]{3,2,1,0:T(8,128)(2,1)S(1)} %get-tuple-element.75), channel_id=1, source_target_pairs={{0,2},{1,3},{2,0},{3,1},{4,6},{5,7},{6,4},{7,5},{8,10},{9,11},{10,... | collective-permute-start | bytes 491528 | tf_op jit(solution)/shard_map/ppermute | solution.py:428
  125.9 7.1 %collective-permute-done.29.refs_1_ = bf16[5,2,64,128]{3,2,1,0:T(8,128)(2,1)S(1)} collective-permute-done((bf16[5,2,64,128]{3,2,1,0:T(8,128)(2,1)S(1)}, bf16[5,2,64,128]{3,2,1,0:T(8,128)(2,1)S(1)}, u32[]{:S(2)}, u32[]{:S(2)}) %collective-permute-start.29) | collective-permute-done | bytes 163872 | tf_op jit(solution)/shard_map/ppermute | solution.py:428
  (95 shorter events, 32.7 us)
Async XLA Ops:
  0.6 29.5 %collective-permute-start = (bf16[2,448,576]{2,1,0:T(8,128)(2,1)}, bf16[2,448,576]{2,1,0:T(8,128)(2,1)S(1)}, u32[]{:S(2)}, u32[]{:S(2)}) collective-permute-start(bf16[2,448,576]{2,1,0:T(8,128)(2,1)} %bitcast.7), channel_id=1, source_target_pairs={{0,64},{64,0},{1,65},{65,1},{2,66},{66,2},{3,67},{67,3},{4,68},{68... | collective-permute-start | bytes 3096584 | tf_op jit(solution)/shard_map/ppermute | solution.py:421
  5.3 9.8 %collective-permute-start.5 = (bf16[6,2,64,128]{3,2,1,0:T(8,128)(2,1)S(1)}, bf16[6,2,64,128]{3,2,1,0:T(8,128)(2,1)S(1)}, u32[]{:S(2)}, u32[]{:S(2)}) collective-permute-start(bf16[6,2,64,128]{3,2,1,0:T(8,128)(2,1)S(1)} %get-tuple-element.45), channel_id=1, source_target_pairs={{0,1},{1,2},{2,3},{3,0},{4,5},{5,6},{6,7},{7,4},{8,9},{9,10},{10,1... | collective-permute-start | bytes 589832 | tf_op jit(solution)/shard_map/ppermute | solution.py:428
  7.4 13.0 %collective-permute-start.6 = (bf16[6,2,64,128]{3,2,1,0:T(8,128)(2,1)S(1)}, bf16[6,2,64,128]{3,2,1,0:T(8,128)(2,1)S(1)}, u32[]{:S(2)}, u32[]{:S(2)}) collective-permute-start(bf16[6,2,64,128]{3,2,1,0:T(8,128)(2,1)S(1)} %get-tuple-element.46), channel_id=1, source_target_pairs={{0,2},{1,3},{2,0},{3,1},{4,6},{5,7},{6,4},{7,5},{8,10},{9,11},{10,... | collective-permute-start | bytes 589832 | tf_op jit(solution)/shard_map/ppermute | solution.py:428
  11.0 9.5 %collective-permute-start.7 = (bf16[6,2,64,128]{3,2,1,0:T(8,128)(2,1)S(1)}, bf16[6,2,64,128]{3,2,1,0:T(8,128)(2,1)S(1)}, u32[]{:S(2)}, u32[]{:S(2)}) collective-permute-start(bf16[6,2,64,128]{3,2,1,0:T(8,128)(2,1)S(1)} %get-tuple-element.47), channel_id=1, source_target_pairs={{0,3},{1,0},{2,1},{3,2},{4,7},{5,4},{6,5},{7,6},{8,11},{9,8},{10,9... | collective-permute-start | bytes 589832 | tf_op jit(solution)/shard_map/ppermute | solution.py:428
  12.0 9.0 %collective-permute-start.8 = (bf16[6,2,64,128]{3,2,1,0:T(8,128)(2,1)S(1)}, bf16[6,2,64,128]{3,2,1,0:T(8,128)(2,1)S(1)}, u32[]{:S(2)}, u32[]{:S(2)}) collective-permute-start(bf16[6,2,64,128]{3,2,1,0:T(8,128)(2,1)S(1)} %get-tuple-element.44.refs_0_), channel_id=1, source_target_pairs={{0,64},{64,0},{1,65},{65,1},{2,66},{66,2},{3,67},{67,3},{4,68},{68... | collective-permute-start | bytes 589832 | tf_op jit(solution)/shard_map/ppermute | solution.py:421
  20.5 9.6 %collective-permute-start.1 = (bf16[2,576,256]{2,1,0:T(8,128)(2,1)}, bf16[2,576,256]{2,1,0:T(8,128)(2,1)S(1)}, u32[]{:S(2)}, u32[]{:S(2)}) collective-permute-start(bf16[2,576,256]{2,1,0:T(8,128)(2,1)} %refs_1_.1), channel_id=1, source_target_pairs={{0,64},{64,0},{1,65},{65,1},{2,66},{66,2},{3,67},{67,3},{4,68},{68... | collective-permute-start | bytes 1769480 | tf_op jit(solution)/shard_map/ppermute | solution.py:421
  21.1 9.0 %collective-permute-start.2 = (bf16[2,192,576]{2,1,0:T(8,128)(2,1)}, bf16[2,192,576]{2,1,0:T(8,128)(2,1)S(1)}, u32[]{:S(2)}, u32[]{:S(2)}) collective-permute-start(bf16[2,192,576]{2,1,0:T(8,128)(2,1)} %bitcast.9), channel_id=1, source_target_pairs={{0,64},{64,0},{1,65},{65,1},{2,66},{66,2},{3,67},{67,3},{4,68},{68... | collective-permute-start | bytes 1327112 | tf_op jit(solution)/shard_map/ppermute | solution.py:421
  24.4 9.5 %collective-permute-start.13 = (bf16[18,64,128]{2,1,0:T(8,128)(2,1)S(1)}, bf16[18,64,128]{2,1,0:T(8,128)(2,1)S(1)}, u32[]{:S(2)}, u32[]{:S(2)}) collective-permute-start(bf16[18,64,128]{2,1,0:T(8,128)(2,1)S(1)} %get-tuple-element.49), channel_id=1, source_target_pairs={{64,4},{0,124},{65,5},{1,125},{66,6},{2,126},{67,7},{3,127},{68,8}... | collective-permute-start | bytes 884744 | tf_op jit(solution)/shard_map/ppermute | solution.py:424
  29.4 14.7 %collective-permute-start.12 = (bf16[18,64,128]{2,1,0:T(8,128)(2,1)S(1)}, bf16[18,64,128]{2,1,0:T(8,128)(2,1)S(1)}, u32[]{:S(2)}, u32[]{:S(2)}) collective-permute-start(bf16[18,64,128]{2,1,0:T(8,128)(2,1)S(1)} %get-tuple-element.48), channel_id=1, source_target_pairs={{64,4},{0,124},{65,5},{1,125},{66,6},{2,126},{67,7},{3,127},{68,8}... | collective-permute-start | bytes 884744 | tf_op jit(solution)/shard_map/ppermute | solution.py:424
  38.8 8.1 %collective-permute-start.15 = (bf16[16,64,128]{2,1,0:T(8,128)(2,1)S(1)}, bf16[16,64,128]{2,1,0:T(8,128)(2,1)S(1)}, u32[]{:S(2)}, u32[]{:S(2)}) collective-permute-start(bf16[16,64,128]{2,1,0:T(8,128)(2,1)S(1)} %get-tuple-element.54), channel_id=1, source_target_pairs={{0,64},{64,0},{1,65},{65,1},{2,66},{66,2},{3,67},{67,3},{4,68},{68... | collective-permute-start | bytes 786440 | tf_op jit(solution)/shard_map/ppermute | solution.py:421
  38.9 8.0 %collective-permute-start.16 = (bf16[8,64,128]{2,1,0:T(8,128)(2,1)S(1)}, bf16[8,64,128]{2,1,0:T(8,128)(2,1)S(1)}, u32[]{:S(2)}, u32[]{:S(2)}) collective-permute-start(bf16[8,64,128]{2,1,0:T(8,128)(2,1)S(1)} %get-tuple-element.56), channel_id=1, source_target_pairs={{64,4},{0,124},{65,5},{1,125},{66,6},{2,126},{67,7},{3,127},{68,8}... | collective-permute-start | bytes 393224 | tf_op jit(solution)/shard_map/ppermute | solution.py:424
  51.7 12.2 %collective-permute-start.17 = (bf16[14,64,128]{2,1,0:T(8,128)(2,1)S(1)}, bf16[14,64,128]{2,1,0:T(8,128)(2,1)S(1)}, u32[]{:S(2)}, u32[]{:S(2)}) collective-permute-start(bf16[14,64,128]{2,1,0:T(8,128)(2,1)S(1)} %get-tuple-element.58), channel_id=1, source_target_pairs={{0,64},{64,0},{1,65},{65,1},{2,66},{66,2},{3,67},{67,3},{4,68},{68... | collective-permute-start | bytes 688136 | tf_op jit(solution)/shard_map/ppermute | solution.py:421
  51.8 7.8 %collective-permute-start.14 = (bf16[8,64,128]{2,1,0:T(8,128)(2,1)S(1)}, bf16[8,64,128]{2,1,0:T(8,128)(2,1)S(1)}, u32[]{:S(2)}, u32[]{:S(2)}) collective-permute-start(bf16[8,64,128]{2,1,0:T(8,128)(2,1)S(1)} %get-tuple-element.52), channel_id=1, source_target_pairs={{64,4},{0,124},{65,5},{1,125},{66,6},{2,126},{67,7},{3,127},{68,8}... | collective-permute-start | bytes 393224 | tf_op jit(solution)/shard_map/ppermute | solution.py:424
  68.9 9.6 %collective-permute-start.20 = (bf16[16,64,128]{2,1,0:T(8,128)(2,1)S(1)}, bf16[16,64,128]{2,1,0:T(8,128)(2,1)S(1)}, u32[]{:S(2)}, u32[]{:S(2)}) collective-permute-start(bf16[16,64,128]{2,1,0:T(8,128)(2,1)S(1)} %get-tuple-element.62), channel_id=1, source_target_pairs={{0,64},{64,0},{1,65},{65,1},{2,66},{66,2},{3,67},{67,3},{4,68},{68... | collective-permute-start | bytes 786440 | tf_op jit(solution)/shard_map/ppermute | solution.py:421
  69.0 8.1 %collective-permute-start.21 = (bf16[10,64,128]{2,1,0:T(8,128)(2,1)S(1)}, bf16[10,64,128]{2,1,0:T(8,128)(2,1)S(1)}, u32[]{:S(2)}, u32[]{:S(2)}) collective-permute-start(bf16[10,64,128]{2,1,0:T(8,128)(2,1)S(1)} %get-tuple-element.63), channel_id=1, source_target_pairs={{64,4},{0,124},{65,5},{1,125},{66,6},{2,126},{67,7},{3,127},{68,8}... | collective-permute-start | bytes 491528 | tf_op jit(solution)/shard_map/ppermute | solution.py:424
  70.5 8.1 %collective-permute-start.22 = (bf16[8,64,128]{2,1,0:T(8,128)(2,1)S(1)}, bf16[8,64,128]{2,1,0:T(8,128)(2,1)S(1)}, u32[]{:S(2)}, u32[]{:S(2)}) collective-permute-start(bf16[8,64,128]{2,1,0:T(8,128)(2,1)S(1)} %get-tuple-element.64), channel_id=1, source_target_pairs={{64,4},{0,124},{65,5},{1,125},{66,6},{2,126},{67,7},{3,127},{68,8}... | collective-permute-start | bytes 393224 | tf_op jit(solution)/shard_map/ppermute | solution.py:424
  84.1 10.3 %collective-permute-start.23 = (bf16[14,64,128]{2,1,0:T(8,128)(2,1)S(1)}, bf16[14,64,128]{2,1,0:T(8,128)(2,1)S(1)}, u32[]{:S(2)}, u32[]{:S(2)}) collective-permute-start(bf16[14,64,128]{2,1,0:T(8,128)(2,1)S(1)} %get-tuple-element.66), channel_id=1, source_target_pairs={{0,64},{64,0},{1,65},{65,1},{2,66},{66,2},{3,67},{67,3},{4,68},{68... | collective-permute-start | bytes 688136 | tf_op jit(solution)/shard_map/ppermute | solution.py:421
  84.2 8.4 %collective-permute-start.19 = (bf16[8,64,128]{2,1,0:T(8,128)(2,1)S(1)}, bf16[8,64,128]{2,1,0:T(8,128)(2,1)S(1)}, u32[]{:S(2)}, u32[]{:S(2)}) collective-permute-start(bf16[8,64,128]{2,1,0:T(8,128)(2,1)S(1)} %get-tuple-element.61), channel_id=1, source_target_pairs={{64,4},{0,124},{65,5},{1,125},{66,6},{2,126},{67,7},{3,127},{68,8}... | collective-permute-start | bytes 393224 | tf_op jit(solution)/shard_map/ppermute | solution.py:424
  87.5 7.0 %collective-permute-start.24 = (bf16[4,64,128]{2,1,0:T(8,128)(2,1)S(1)}, bf16[4,64,128]{2,1,0:T(8,128)(2,1)S(1)}, u32[]{:S(2)}, u32[]{:S(2)}) collective-permute-start(bf16[4,64,128]{2,1,0:T(8,128)(2,1)S(1)} %get-tuple-element.67), channel_id=1, source_target_pairs={{64,4},{0,124},{65,5},{1,125},{66,6},{2,126},{67,7},{3,127},{68,8}... | collective-permute-start | bytes 196616 | tf_op jit(solution)/shard_map/ppermute | solution.py:424
  89.2 13.4 %collective-permute-start.25 = (bf16[10,64,128]{2,1,0:T(8,128)(2,1)}, bf16[10,64,128]{2,1,0:T(8,128)(2,1)}, u32[]{:S(2)}, u32[]{:S(2)}) collective-permute-start(bf16[10,64,128]{2,1,0:T(8,128)(2,1)} %get-tuple-element.70), channel_id=1, source_target_pairs={{64,4},{0,124},{65,5},{1,125},{66,6},{2,126},{67,7},{3,127},{68,8}... | collective-permute-start | bytes 491528 | tf_op jit(solution)/shard_map/ppermute | solution.py:424
  100.8 8.0 %collective-permute-start.27 = (bf16[8,64,128]{2,1,0:T(8,128)(2,1)}, bf16[8,64,128]{2,1,0:T(8,128)(2,1)}, u32[]{:S(2)}, u32[]{:S(2)}) collective-permute-start(bf16[8,64,128]{2,1,0:T(8,128)(2,1)} %get-tuple-element.72), channel_id=1, source_target_pairs={{64,4},{0,124},{65,5},{1,125},{66,6},{2,126},{67,7},{3,127},{68,8}... | collective-permute-start | bytes 393224 | tf_op jit(solution)/shard_map/ppermute | solution.py:424
  122.0 11.0 %collective-permute-start.29 = (bf16[5,2,64,128]{3,2,1,0:T(8,128)(2,1)S(1)}, bf16[5,2,64,128]{3,2,1,0:T(8,128)(2,1)S(1)}, u32[]{:S(2)}, u32[]{:S(2)}) collective-permute-start(bf16[5,2,64,128]{3,2,1,0:T(8,128)(2,1)S(1)} %get-tuple-element.74), channel_id=1, source_target_pairs={{0,1},{1,2},{2,3},{3,0},{4,5},{5,6},{6,7},{7,4},{8,9},{9,10},{10,1... | collective-permute-start | bytes 491528 | tf_op jit(solution)/shard_map/ppermute | solution.py:428
  122.3 10.8 %collective-permute-start.30 = (bf16[5,2,64,128]{3,2,1,0:T(8,128)(2,1)S(1)}, bf16[5,2,64,128]{3,2,1,0:T(8,128)(2,1)S(1)}, u32[]{:S(2)}, u32[]{:S(2)}) collective-permute-start(bf16[5,2,64,128]{3,2,1,0:T(8,128)(2,1)S(1)} %get-tuple-element.75), channel_id=1, source_target_pairs={{0,2},{1,3},{2,0},{3,1},{4,6},{5,7},{6,4},{7,5},{8,10},{9,11},{10,... | collective-permute-start | bytes 491528 | tf_op jit(solution)/shard_map/ppermute | solution.py:428
  124.7 9.0 %collective-permute-start.31 = (bf16[5,2,64,128]{3,2,1,0:T(8,128)(2,1)S(1)}, bf16[5,2,64,128]{3,2,1,0:T(8,128)(2,1)S(1)}, u32[]{:S(2)}, u32[]{:S(2)}) collective-permute-start(bf16[5,2,64,128]{3,2,1,0:T(8,128)(2,1)S(1)} %get-tuple-element.76), channel_id=1, source_target_pairs={{0,3},{1,0},{2,1},{3,2},{4,7},{5,4},{6,5},{7,6},{8,11},{9,8},{10,9... | collective-permute-start | bytes 491528 | tf_op jit(solution)/shard_map/ppermute | solution.py:428
  (29 other events, 316.5 us)

commit v4 on v3

--- a/solution.py
+++ b/solution.py
@@ -197,6 +197,13 @@
                 target[offset + u] = jnp.where(last_rows_if, high, low)
 
     half = plan["half"]
+    if "give" in out:
+        lower, slots = ref[plan["lower"]], out["give"].shape[0]
+        for slot in range(slots):
+            for row in range(OWN):
+                out["give"][slot, row] = jnp.where(
+                    first_core, state_out[slot, row], lower[slot, row]
+                )
     if "near" in out:
         send(out["near"], both(half) if "late" in out else SOON[half], first_core)
     if "soon" in out:
@@ -217,6 +224,8 @@
             far["late"] = units(LATE[half])
         sizes["near"] = (sum(far.values()),) + unit
         sizes.update({k: (n,) + unit for k, n in far.items()})
+    else:
+        sizes["give"] = sizes["state"]
     plan["outs"] = list(sizes)
     in_specs = [
         pl.BlockSpec(memory_space=pltpu.SMEM if name == "sc" else pltpu.VMEM) for name in names
@@ -246,9 +255,15 @@
 
 
 def pack_weights_kernel(sc, *refs):
-    inputs, (wa, wb, wc, wo) = refs[:10], refs[10:]
+    sources, (wa, wb, wc, wo) = refs[:10], refs[10:14]
+    inputs, sems = refs[14:24], refs[24]
     core = sc[0]
+    copies = [pltpu.make_async_copy(s, t, sems.at[i]) for i, (s, t) in enumerate(zip(sources, inputs))]
+    for c in copies:
+        c.start()
     for group in range(2):
+        for c in copies[5 * group : 5 * group + 5]:
+            c.wait()
         x, h, m, o, last = inputs[5 * group : 5 * group + 5]
         first = 2 * core if group == 0 else 2 - 2 * core
         for l in range(2):
@@ -281,14 +296,24 @@
     return pl.pallas_call(
         pack_weights_kernel,
         out_shape=[jax.ShapeDtypeStruct(s, BF) for s in shapes],
-        in_specs=[pl.BlockSpec(memory_space=pltpu.SMEM)] + [vmem] * 10,
+        in_specs=[pl.BlockSpec(memory_space=pltpu.SMEM)]
+        + [pl.BlockSpec(memory_space=pltpu.HBM)] * 10,
         out_specs=[vmem] * 4,
+        scratch_shapes=[pltpu.VMEM(w.shape, BF) for w in (*own, *other)]
+        + [pltpu.SemaphoreType.DMA((10,))],
         compiler_params=pltpu.CompilerParams(vmem_limit_bytes=32 << 20),
         name="pack_weights",
     )(scalars, *own, *other)
 
 
-def cut_state_kernel(sc, frames, hidden, cell, memory, *pieces):
+def cut_state_kernel(sc, *refs):
+    sources, pieces, copied, sems = refs[:4], refs[4:8], refs[8:12], refs[12]
+    copies = [pltpu.make_async_copy(s, t, sems.at[i]) for i, (s, t) in enumerate(zip(sources, copied))]
+    for c in copies:
+        c.start()
+    for c in copies:
+        c.wait()
+    frames, hidden, cell, memory = copied
     first_core, z = sc[0] == 0, sc[2]
     for k in range(4):
         seq = lax.rem(z + k, 4)
@@ -305,8 +330,11 @@
     return pl.pallas_call(
         cut_state_kernel,
         out_shape=[jax.ShapeDtypeStruct((6, 2, CH, GW), BF)] * 4,
-        in_specs=[pl.BlockSpec(memory_space=pltpu.SMEM)] + [vmem] * 4,
+        in_specs=[pl.BlockSpec(memory_space=pltpu.SMEM)]
+        + [pl.BlockSpec(memory_space=pltpu.HBM)] * 4,
         out_specs=[vmem] * 4,
+        scratch_shapes=[pltpu.VMEM(v.shape, BF) for v in (frames, hidden, cell, memory)]
+        + [pltpu.SemaphoreType.DMA((4,))],
         compiler_params=pltpu.CompilerParams(vmem_limit_bytes=8 << 20),
         name="cut_state",
     )(scalars, frames, hidden, cell, memory)
@@ -429,7 +457,9 @@
 
     scalars = jnp.stack([core, 8 * (chip // 4) + 4 * core, chip % 4]).astype(jnp.int32)
     turned = [jnp.swapaxes(w, 1, 2) for w in (w_x, w_m, w_o, w_last)]
-    own_w = [turned[0], w_h, turned[1], turned[2], turned[3]]
+    scalars, own_w = lax.optimization_barrier(
+        (scalars, [turned[0], w_h, turned[1], turned[2], turned[3]])
+    )
     other_w = [to_partner(w) for w in own_w]
     wa, wb, wc, wo = pack_weights(scalars, own_w, other_w)
 
@@ -472,6 +502,9 @@
             for name in sorted(needed):
                 operands[name] = arrays[name]
             plan = {"fields": fields, "half": half, "layer": 2 * half, "send": send}
+            if not send:
+                plan["lower"] = states[0]
+                operands[states[0]] = arrays[states[0]]
             tag = f"{step}{half}"
             outs = run_phase(operands, plan)
             results[half] = outs["state"]
@@ -494,8 +527,7 @@
                 for k, (o, n) in LATE[half].items():
                     halo[half][k] = ("near" + tag, near_at[k][0], "late" + tag, o, n)
 
-    give = jnp.where(core == 0, results[1], results[0])
-    taken = to_partner(give)
+    taken = to_partner(outs["give"])
     pieces = cut_result(scalars, results[0], results[1], taken)
     done = [pieces[0]] + [around(pieces[k], k) for k in (1, 2, 3)]
     return tuple(close_result(scalars, done))

time: 136 us -> 128 us (0.941)
  local copies, waits for them, and re-layouts: 12.1 us -> 3.95 us
    unnamed x42 -> x18, local copies, waits for them, and re-layouts: 12.1 us -> 3.95 us
    pallas_call x1, Pallas kernels: 1.34 us -> 3.13 us  [pack_weights(): pl.pallas_call(pack_weights_kernel, out_shape=[jax.ShapeDtypeStruct(s, BF...]
    pallas_call x6, Pallas kernels: 31.3 us -> 29.6 us  [run_phase(): pl.pallas_call(functools.partial(phase_kernel, plan), out_shape=[jax.Shap...]
  transfers between devices with their start and end apart: 32 -> 32, of which waited for: 16 -> 16; matrix products, arithmetic and copies ran while one was open for 0% -> 0% of each run, Pallas kernels for 10% -> 12%
where the time goes in v4:
time: 128 us
  starting transfers between devices  44.5 us (35%)
  waiting for transfers between devices  41.9 us (33%)
  Pallas kernels  36.9 us (29%)
  local copies, waits for them, and re-layouts  3.95 us (3%)
    ppermute x11, starting transfers between devices, to_neighbour(): return lax.ppermute(value, ('layer', 'rows'), across)  31.9 us
    pallas_call x6, Pallas kernels, run_phase(): pl.pallas_call(functools.partial(phase_kernel, plan), out_shape=[jax.Shap...  29.6 us
    ppermute x11, waiting for transfers between devices, to_neighbour(): return lax.ppermute(value, ('layer', 'rows'), across)  22.4 us
    ppermute x6, waiting for transfers between devices, around(): return lax.ppermute(value, 'rows', turn)  16.1 us
    ppermute x6, starting transfers between devices, around(): return lax.ppermute(value, 'rows', turn)  10.6 us
    unnamed x18, local copies, waits for them, and re-layouts  3.95 us
    ppermute x15, waiting for transfers between devices, to_partner(): return lax.ppermute(value, 'layer', swap)  3.36 us
    pallas_call x1, Pallas kernels, pack_weights(): pl.pallas_call(pack_weights_kernel, out_shape=[jax.ShapeDtypeStruct(s, BF...  3.13 us
  transfers between devices with their start and end apart: 32, of which 16 were waited for; matrix products, arithmetic and copies ran while one was open for 0% of the time, Pallas kernels for 12%

profile of v4, /device:TPU:0, one launch (start us, length us, event | category | flops | bytes accessed | tf_op | source)
XLA Modules:
  0.0 128.1 jit_solution(883125165178676011)
XLA Ops:
  5.9 2.1 %collective-permute-start.5 = (bf16[6,2,64,128]{3,2,1,0:T(8,128)(2,1)S(1)}, bf16[6,2,64,128]{3,2,1,0:T(8,128)(2,1)S(1)}, u32[]{:S(2)}, u32[]{:S(2)}) collective-permute-start(bf16[6,2,64,128]{3,2,1,0:T(8,128)(2,1)S(1)} %get-tuple-element.59), channel_id=1, source_target_pairs={{0,1},{1,2},{2,3},{3,0},{4,5},{5,6},{6,7},{7,4},{8,9},{9,10},{10,1... | collective-permute-start | bytes 589832 | tf_op jit(solution)/shard_map/ppermute | solution.py:456
  8.0 3.6 %collective-permute-start.6 = (bf16[6,2,64,128]{3,2,1,0:T(8,128)(2,1)S(1)}, bf16[6,2,64,128]{3,2,1,0:T(8,128)(2,1)S(1)}, u32[]{:S(2)}, u32[]{:S(2)}) collective-permute-start(bf16[6,2,64,128]{3,2,1,0:T(8,128)(2,1)S(1)} %get-tuple-element.60), channel_id=1, source_target_pairs={{0,2},{1,3},{2,0},{3,1},{4,6},{5,7},{6,4},{7,5},{8,10},{9,11},{10,... | collective-permute-start | bytes 589832 | tf_op jit(solution)/shard_map/ppermute | solution.py:456
  12.5 2.9 %collective-permute-done.5.refs_1_ = bf16[6,2,64,128]{3,2,1,0:T(8,128)(2,1)S(1)} collective-permute-done((bf16[6,2,64,128]{3,2,1,0:T(8,128)(2,1)S(1)}, bf16[6,2,64,128]{3,2,1,0:T(8,128)(2,1)S(1)}, u32[]{:S(2)}, u32[]{:S(2)}) %collective-permute-start.5) | collective-permute-done | bytes 196640 | tf_op jit(solution)/shard_map/ppermute | solution.py:456
  15.5 5.4 %collective-permute-done.6.refs_2_ = bf16[6,2,64,128]{3,2,1,0:T(8,128)(2,1)S(1)} collective-permute-done((bf16[6,2,64,128]{3,2,1,0:T(8,128)(2,1)S(1)}, bf16[6,2,64,128]{3,2,1,0:T(8,128)(2,1)S(1)}, u32[]{:S(2)}, u32[]{:S(2)}) %collective-permute-start.6) | collective-permute-done | bytes 196640 | tf_op jit(solution)/shard_map/ppermute | solution.py:456
  24.8 5.1 %collective-permute-start.13 = (bf16[18,64,128]{2,1,0:T(8,128)(2,1)S(1)}, bf16[18,64,128]{2,1,0:T(8,128)(2,1)S(1)}, u32[]{:S(2)}, u32[]{:S(2)}) collective-permute-start(bf16[18,64,128]{2,1,0:T(8,128)(2,1)S(1)} %get-tuple-element.63), channel_id=1, source_target_pairs={{64,4},{0,124},{65,5},{1,125},{66,6},{2,126},{67,7},{3,127},{68,8}... | collective-permute-start | bytes 884744 | tf_op jit(solution)/shard_map/ppermute | solution.py:452
  30.6 3.1 %pack_weights.1 = (bf16[4,256,512]{2,1,0:T(8,128)(2,1)S(1)}, bf16[4,448,768]{2,1,0:T(8,128)(2,1)S(1)}, bf16[4,192,448]{2,1,0:T(8,128)(2,1)S(1)}, bf16[4,256,384]{2,1,0:T(8,128)(2,1)S(1)}) custom-call(s32[3]{0:T(128)S(1)} %pad_add_fusion.sc.refs_0_, bf16[2,448,576]{2,1,0:T(8,128)(2,1)S(1)} %bitcast.8, bf16[2,576,256]{2,1,0:T(8,128)(2,1)S(1)} %copy-done.1, ...), custom_call_target="tpu_custom_call" | custom-call | tf_op jit(solution)/shard_map/pack_weights/pallas_call | solution.py:296
  34.3 4.9 %two_layers.6 = (bf16[5,4,64,128]{3,2,1,0:T(8,128)(2,1)S(1)}, bf16[16,64,128]{2,1,0:T(8,128)(2,1)S(1)}, bf16[8,64,128]{2,1,0:T(8,128)(2,1)S(1)}, bf16[8,64,128]{2,1,0:T(8,128)(2,1)S(1)}) custom-call(s32[3]{0:T(128)S(1)} %pad_add_fusion.sc.refs_0_, bf16[4,256,512]{2,1,0:T(8,128)(2,1)S(1)} %get-tuple-element.54.refs_1_, ...), custom_call_target="tpu_custom_call" | custom-call | tf_op jit(solution)/shard_map/two_layers/pallas_call | solution.py:233
  39.3 5.3 %collective-permute-start.16 = (bf16[8,64,128]{2,1,0:T(8,128)(2,1)S(1)}, bf16[8,64,128]{2,1,0:T(8,128)(2,1)S(1)}, u32[]{:S(2)}, u32[]{:S(2)}) collective-permute-start(bf16[8,64,128]{2,1,0:T(8,128)(2,1)S(1)} %get-tuple-element.70), channel_id=1, source_target_pairs={{64,4},{0,124},{65,5},{1,125},{66,6},{2,126},{67,7},{3,127},{68,8}... | collective-permute-start | bytes 393224 | tf_op jit(solution)/shard_map/ppermute | solution.py:452
  44.6 2.6 %collective-permute-done.16.refs_9_.refs_11_ = bf16[8,64,128]{2,1,0:T(8,128)(2,1)S(1)} collective-permute-done((bf16[8,64,128]{2,1,0:T(8,128)(2,1)S(1)}, bf16[8,64,128]{2,1,0:T(8,128)(2,1)S(1)}, u32[]{:S(2)}, u32[]{:S(2)}) %collective-permute-start.16) | collective-permute-done | bytes 131104 | tf_op jit(solution)/shard_map/ppermute | solution.py:452
  47.3 4.9 %two_layers.7 = (bf16[5,4,64,128]{3,2,1,0:T(8,128)(2,1)S(1)}, bf16[14,64,128]{2,1,0:T(8,128)(2,1)S(1)}, bf16[4,64,128]{2,1,0:T(8,128)(2,1)S(1)}, bf16[10,64,128]{2,1,0:T(8,128)(2,1)S(1)}) custom-call(s32[3]{0:T(128)S(1)} %pad_add_fusion.sc.refs_0_, bf16[4,256,512]{2,1,0:T(8,128)(2,1)S(1)} %get-tuple-element.54.refs_1_, ...), custom_call_target="tpu_custom_call" | custom-call | tf_op jit(solution)/shard_map/two_layers/pallas_call | solution.py:233
  52.3 5.1 %collective-permute-start.14 = (bf16[8,64,128]{2,1,0:T(8,128)(2,1)S(1)}, bf16[8,64,128]{2,1,0:T(8,128)(2,1)S(1)}, u32[]{:S(2)}, u32[]{:S(2)}) collective-permute-start(bf16[8,64,128]{2,1,0:T(8,128)(2,1)S(1)} %get-tuple-element.66), channel_id=1, source_target_pairs={{64,4},{0,124},{65,5},{1,125},{66,6},{2,126},{67,7},{3,127},{68,8}... | collective-permute-start | bytes 393224 | tf_op jit(solution)/shard_map/ppermute | solution.py:452
  57.6 2.6 %collective-permute-done.14.refs_6_ = bf16[8,64,128]{2,1,0:T(8,128)(2,1)S(1)} collective-permute-done((bf16[8,64,128]{2,1,0:T(8,128)(2,1)S(1)}, bf16[8,64,128]{2,1,0:T(8,128)(2,1)S(1)}, u32[]{:S(2)}, u32[]{:S(2)}) %collective-permute-start.14) | collective-permute-done | bytes 131104 | tf_op jit(solution)/shard_map/ppermute | solution.py:452
  60.1 4.4 %collective-permute-done.18.refs_12_ = bf16[4,64,128]{2,1,0:T(8,128)(2,1)S(1)} collective-permute-done((bf16[4,64,128]{2,1,0:T(8,128)(2,1)S(1)}, bf16[4,64,128]{2,1,0:T(8,128)(2,1)S(1)}, u32[]{:S(2)}, u32[]{:S(2)}) %collective-permute-start.18) | collective-permute-done | bytes 65568 | tf_op jit(solution)/shard_map/ppermute | solution.py:452
  64.5 4.9 %two_layers.8 = (bf16[5,4,64,128]{3,2,1,0:T(8,128)(2,1)S(1)}, bf16[16,64,128]{2,1,0:T(8,128)(2,1)S(1)}, bf16[8,64,128]{2,1,0:T(8,128)(2,1)S(1)}, bf16[8,64,128]{2,1,0:T(8,128)(2,1)S(1)}) custom-call(s32[3]{0:T(128)S(1)} %pad_add_fusion.sc.refs_0_, bf16[4,256,512]{2,1,0:T(8,128)(2,1)S(1)} %get-tuple-element.54.refs_1_, ...), custom_call_target="tpu_custom_call" | custom-call | tf_op jit(solution)/shard_map/two_layers/pallas_call | solution.py:233
  71.0 3.7 %collective-permute-start.22 = (bf16[8,64,128]{2,1,0:T(8,128)(2,1)S(1)}, bf16[8,64,128]{2,1,0:T(8,128)(2,1)S(1)}, u32[]{:S(2)}, u32[]{:S(2)}) collective-permute-start(bf16[8,64,128]{2,1,0:T(8,128)(2,1)S(1)} %get-tuple-element.78), channel_id=1, source_target_pairs={{64,4},{0,124},{65,5},{1,125},{66,6},{2,126},{67,7},{3,127},{68,8}... | collective-permute-start | bytes 393224 | tf_op jit(solution)/shard_map/ppermute | solution.py:452
  74.7 3.0 %collective-permute-done.21.refs_5_ = bf16[10,64,128]{2,1,0:T(8,128)(2,1)S(1)} collective-permute-done((bf16[10,64,128]{2,1,0:T(8,128)(2,1)S(1)}, bf16[10,64,128]{2,1,0:T(8,128)(2,1)S(1)}, u32[]{:S(2)}, u32[]{:S(2)}) %collective-permute-start.21) | collective-permute-done | bytes 163872 | tf_op jit(solution)/shard_map/ppermute | solution.py:452
  79.1 4.9 %two_layers.9 = (bf16[5,4,64,128]{3,2,1,0:T(8,128)(2,1)S(1)}, bf16[14,64,128]{2,1,0:T(8,128)(2,1)S(1)}, bf16[4,64,128]{2,1,0:T(8,128)(2,1)S(1)}, bf16[10,64,128]{2,1,0:T(8,128)(2,1)S(1)}) custom-call(s32[3]{0:T(128)S(1)} %pad_add_fusion.sc.refs_0_, bf16[4,256,512]{2,1,0:T(8,128)(2,1)S(1)} %get-tuple-element.54.refs_1_, ...), custom_call_target="tpu_custom_call" | custom-call | tf_op jit(solution)/shard_map/two_layers/pallas_call | solution.py:233
  84.1 3.4 %collective-permute-start.19 = (bf16[8,64,128]{2,1,0:T(8,128)(2,1)S(1)}, bf16[8,64,128]{2,1,0:T(8,128)(2,1)S(1)}, u32[]{:S(2)}, u32[]{:S(2)}) collective-permute-start(bf16[8,64,128]{2,1,0:T(8,128)(2,1)S(1)} %get-tuple-element.75), channel_id=1, source_target_pairs={{64,4},{0,124},{65,5},{1,125},{66,6},{2,126},{67,7},{3,127},{68,8}... | collective-permute-start | bytes 393224 | tf_op jit(solution)/shard_map/ppermute | solution.py:452
  89.2 3.3 %collective-permute-start.25 = (bf16[10,64,128]{2,1,0:T(8,128)(2,1)S(1)}, bf16[10,64,128]{2,1,0:T(8,128)(2,1)S(1)}, u32[]{:S(2)}, u32[]{:S(2)}) collective-permute-start(bf16[10,64,128]{2,1,0:T(8,128)(2,1)S(1)} %get-tuple-element.84), channel_id=1, source_target_pairs={{64,4},{0,124},{65,5},{1,125},{66,6},{2,126},{67,7},{3,127},{68,8}... | collective-permute-start | bytes 491528 | tf_op jit(solution)/shard_map/ppermute | solution.py:452
  94.5 4.9 %two_layers.10 = (bf16[5,4,64,128]{3,2,1,0:T(8,128)(2,1)S(1)}, bf16[8,64,128]{2,1,0:T(8,128)(2,1)S(1)}, bf16[8,64,128]{2,1,0:T(8,128)(2,1)S(1)}) custom-call(s32[3]{0:T(128)S(1)} %pad_add_fusion.sc.refs_0_, bf16[4,256,512]{2,1,0:T(8,128)(2,1)S(1)} %get-tuple-element.54.refs_1_, bf16[4,448,768]{2,1,0:T(8,128)(2,1)S(1)} %get-tuple-element.55.refs_2_, ...), custom_call_target="tpu_custom_call" | custom-call | tf_op jit(solution)/shard_map/two_layers/pallas_call | solution.py:233
  101.6 6.0 %collective-permute-done.27.refs_8_ = bf16[8,64,128]{2,1,0:T(8,128)(2,1)S(1)} collective-permute-done((bf16[8,64,128]{2,1,0:T(8,128)(2,1)S(1)}, bf16[8,64,128]{2,1,0:T(8,128)(2,1)S(1)}, u32[]{:S(2)}, u32[]{:S(2)}) %collective-permute-start.27) | collective-permute-done | bytes 131104 | tf_op jit(solution)/shard_map/ppermute | solution.py:452
  107.6 5.0 %two_layers.11 = (bf16[5,4,64,128]{3,2,1,0:T(8,128)(2,1)S(1)}, bf16[5,4,64,128]{3,2,1,0:T(8,128)(2,1)S(1)}) custom-call(s32[3]{0:T(128)S(1)} %pad_add_fusion.sc.refs_0_, bf16[4,256,512]{2,1,0:T(8,128)(2,1)S(1)} %get-tuple-element.54.refs_1_, bf16[4,448,768]{2,1,0:T(8,128)(2,1)S(1)} %get-tuple-element.55.refs_2_, ...), custom_call_target="tpu_custom_call" | custom-call | tf_op jit(solution)/shard_map/two_layers/pallas_call | solution.py:233
  115.3 2.4 %collective-permute-start.30 = (bf16[5,2,64,128]{3,2,1,0:T(8,128)(2,1)S(1)}, bf16[5,2,64,128]{3,2,1,0:T(8,128)(2,1)S(1)}, u32[]{:S(2)}, u32[]{:S(2)}) collective-permute-start(bf16[5,2,64,128]{3,2,1,0:T(8,128)(2,1)S(1)} %get-tuple-element.91), channel_id=1, source_target_pairs={{0,2},{1,3},{2,0},{3,1},{4,6},{5,7},{6,4},{7,5},{8,10},{9,11},{10,... | collective-permute-start | bytes 491528 | tf_op jit(solution)/shard_map/ppermute | solution.py:456
  118.9 7.1 %collective-permute-done.29.refs_1_ = bf16[5,2,64,128]{3,2,1,0:T(8,128)(2,1)S(1)} collective-permute-done((bf16[5,2,64,128]{3,2,1,0:T(8,128)(2,1)S(1)}, bf16[5,2,64,128]{3,2,1,0:T(8,128)(2,1)S(1)}, u32[]{:S(2)}, u32[]{:S(2)}) %collective-permute-start.29) | collective-permute-done | bytes 163872 | tf_op jit(solution)/shard_map/ppermute | solution.py:456
  (70 shorter events, 26.5 us)
Async XLA Ops:
  0.7 29.8 %collective-permute-start = (bf16[2,448,576]{2,1,0:T(8,128)(2,1)}, bf16[2,448,576]{2,1,0:T(8,128)(2,1)S(1)}, u32[]{:S(2)}, u32[]{:S(2)}) collective-permute-start(bf16[2,448,576]{2,1,0:T(8,128)(2,1)} %bitcast.7), channel_id=1, source_target_pairs={{0,64},{64,0},{1,65},{65,1},{2,66},{66,2},{3,67},{67,3},{4,68},{68... | collective-permute-start | bytes 3096584 | tf_op jit(solution)/shard_map/ppermute | solution.py:449
  5.9 9.6 %collective-permute-start.5 = (bf16[6,2,64,128]{3,2,1,0:T(8,128)(2,1)S(1)}, bf16[6,2,64,128]{3,2,1,0:T(8,128)(2,1)S(1)}, u32[]{:S(2)}, u32[]{:S(2)}) collective-permute-start(bf16[6,2,64,128]{3,2,1,0:T(8,128)(2,1)S(1)} %get-tuple-element.59), channel_id=1, source_target_pairs={{0,1},{1,2},{2,3},{3,0},{4,5},{5,6},{6,7},{7,4},{8,9},{9,10},{10,1... | collective-permute-start | bytes 589832 | tf_op jit(solution)/shard_map/ppermute | solution.py:456
  8.0 12.9 %collective-permute-start.6 = (bf16[6,2,64,128]{3,2,1,0:T(8,128)(2,1)S(1)}, bf16[6,2,64,128]{3,2,1,0:T(8,128)(2,1)S(1)}, u32[]{:S(2)}, u32[]{:S(2)}) collective-permute-start(bf16[6,2,64,128]{3,2,1,0:T(8,128)(2,1)S(1)} %get-tuple-element.60), channel_id=1, source_target_pairs={{0,2},{1,3},{2,0},{3,1},{4,6},{5,7},{6,4},{7,5},{8,10},{9,11},{10,... | collective-permute-start | bytes 589832 | tf_op jit(solution)/shard_map/ppermute | solution.py:456
  11.5 9.4 %collective-permute-start.7 = (bf16[6,2,64,128]{3,2,1,0:T(8,128)(2,1)S(1)}, bf16[6,2,64,128]{3,2,1,0:T(8,128)(2,1)S(1)}, u32[]{:S(2)}, u32[]{:S(2)}) collective-permute-start(bf16[6,2,64,128]{3,2,1,0:T(8,128)(2,1)S(1)} %get-tuple-element.61), channel_id=1, source_target_pairs={{0,3},{1,0},{2,1},{3,2},{4,7},{5,4},{6,5},{7,6},{8,11},{9,8},{10,9... | collective-permute-start | bytes 589832 | tf_op jit(solution)/shard_map/ppermute | solution.py:456
  12.5 8.9 %collective-permute-start.8 = (bf16[6,2,64,128]{3,2,1,0:T(8,128)(2,1)S(1)}, bf16[6,2,64,128]{3,2,1,0:T(8,128)(2,1)S(1)}, u32[]{:S(2)}, u32[]{:S(2)}) collective-permute-start(bf16[6,2,64,128]{3,2,1,0:T(8,128)(2,1)S(1)} %get-tuple-element.58.refs_0_), channel_id=1, source_target_pairs={{0,64},{64,0},{1,65},{65,1},{2,66},{66,2},{3,67},{67,3},{4,68},{68... | collective-permute-start | bytes 589832 | tf_op jit(solution)/shard_map/ppermute | solution.py:449
  20.9 9.6 %collective-permute-start.1 = (bf16[2,576,256]{2,1,0:T(8,128)(2,1)}, bf16[2,576,256]{2,1,0:T(8,128)(2,1)S(1)}, u32[]{:S(2)}, u32[]{:S(2)}) collective-permute-start(bf16[2,576,256]{2,1,0:T(8,128)(2,1)} %refs_1_.1), channel_id=1, source_target_pairs={{0,64},{64,0},{1,65},{65,1},{2,66},{66,2},{3,67},{67,3},{4,68},{68... | collective-permute-start | bytes 1769480 | tf_op jit(solution)/shard_map/ppermute | solution.py:449
  21.5 9.0 %collective-permute-start.2 = (bf16[2,192,576]{2,1,0:T(8,128)(2,1)}, bf16[2,192,576]{2,1,0:T(8,128)(2,1)S(1)}, u32[]{:S(2)}, u32[]{:S(2)}) collective-permute-start(bf16[2,192,576]{2,1,0:T(8,128)(2,1)} %bitcast.9), channel_id=1, source_target_pairs={{0,64},{64,0},{1,65},{65,1},{2,66},{66,2},{3,67},{67,3},{4,68},{68... | collective-permute-start | bytes 1327112 | tf_op jit(solution)/shard_map/ppermute | solution.py:449
  24.8 9.5 %collective-permute-start.13 = (bf16[18,64,128]{2,1,0:T(8,128)(2,1)S(1)}, bf16[18,64,128]{2,1,0:T(8,128)(2,1)S(1)}, u32[]{:S(2)}, u32[]{:S(2)}) collective-permute-start(bf16[18,64,128]{2,1,0:T(8,128)(2,1)S(1)} %get-tuple-element.63), channel_id=1, source_target_pairs={{64,4},{0,124},{65,5},{1,125},{66,6},{2,126},{67,7},{3,127},{68,8}... | collective-permute-start | bytes 884744 | tf_op jit(solution)/shard_map/ppermute | solution.py:452
  29.9 14.8 %collective-permute-start.12 = (bf16[18,64,128]{2,1,0:T(8,128)(2,1)S(1)}, bf16[18,64,128]{2,1,0:T(8,128)(2,1)S(1)}, u32[]{:S(2)}, u32[]{:S(2)}) collective-permute-start(bf16[18,64,128]{2,1,0:T(8,128)(2,1)S(1)} %get-tuple-element.62), channel_id=1, source_target_pairs={{64,4},{0,124},{65,5},{1,125},{66,6},{2,126},{67,7},{3,127},{68,8}... | collective-permute-start | bytes 884744 | tf_op jit(solution)/shard_map/ppermute | solution.py:452
  39.2 8.1 %collective-permute-start.15 = (bf16[16,64,128]{2,1,0:T(8,128)(2,1)S(1)}, bf16[16,64,128]{2,1,0:T(8,128)(2,1)S(1)}, u32[]{:S(2)}, u32[]{:S(2)}) collective-permute-start(bf16[16,64,128]{2,1,0:T(8,128)(2,1)S(1)} %get-tuple-element.68), channel_id=1, source_target_pairs={{0,64},{64,0},{1,65},{65,1},{2,66},{66,2},{3,67},{67,3},{4,68},{68... | collective-permute-start | bytes 786440 | tf_op jit(solution)/shard_map/ppermute | solution.py:449
  39.3 8.0 %collective-permute-start.16 = (bf16[8,64,128]{2,1,0:T(8,128)(2,1)S(1)}, bf16[8,64,128]{2,1,0:T(8,128)(2,1)S(1)}, u32[]{:S(2)}, u32[]{:S(2)}) collective-permute-start(bf16[8,64,128]{2,1,0:T(8,128)(2,1)S(1)} %get-tuple-element.70), channel_id=1, source_target_pairs={{64,4},{0,124},{65,5},{1,125},{66,6},{2,126},{67,7},{3,127},{68,8}... | collective-permute-start | bytes 393224 | tf_op jit(solution)/shard_map/ppermute | solution.py:452
  52.2 12.2 %collective-permute-start.17 = (bf16[14,64,128]{2,1,0:T(8,128)(2,1)S(1)}, bf16[14,64,128]{2,1,0:T(8,128)(2,1)S(1)}, u32[]{:S(2)}, u32[]{:S(2)}) collective-permute-start(bf16[14,64,128]{2,1,0:T(8,128)(2,1)S(1)} %get-tuple-element.72), channel_id=1, source_target_pairs={{0,64},{64,0},{1,65},{65,1},{2,66},{66,2},{3,67},{67,3},{4,68},{68... | collective-permute-start | bytes 688136 | tf_op jit(solution)/shard_map/ppermute | solution.py:449
  52.3 7.8 %collective-permute-start.14 = (bf16[8,64,128]{2,1,0:T(8,128)(2,1)S(1)}, bf16[8,64,128]{2,1,0:T(8,128)(2,1)S(1)}, u32[]{:S(2)}, u32[]{:S(2)}) collective-permute-start(bf16[8,64,128]{2,1,0:T(8,128)(2,1)S(1)} %get-tuple-element.66), channel_id=1, source_target_pairs={{64,4},{0,124},{65,5},{1,125},{66,6},{2,126},{67,7},{3,127},{68,8}... | collective-permute-start | bytes 393224 | tf_op jit(solution)/shard_map/ppermute | solution.py:452
  57.5 7.0 %collective-permute-start.18 = (bf16[4,64,128]{2,1,0:T(8,128)(2,1)S(1)}, bf16[4,64,128]{2,1,0:T(8,128)(2,1)S(1)}, u32[]{:S(2)}, u32[]{:S(2)}) collective-permute-start(bf16[4,64,128]{2,1,0:T(8,128)(2,1)S(1)} %get-tuple-element.73), channel_id=1, source_target_pairs={{64,4},{0,124},{65,5},{1,125},{66,6},{2,126},{67,7},{3,127},{68,8}... | collective-permute-start | bytes 196616 | tf_op jit(solution)/shard_map/ppermute | solution.py:452
  69.4 9.6 %collective-permute-start.20 = (bf16[16,64,128]{2,1,0:T(8,128)(2,1)S(1)}, bf16[16,64,128]{2,1,0:T(8,128)(2,1)S(1)}, u32[]{:S(2)}, u32[]{:S(2)}) collective-permute-start(bf16[16,64,128]{2,1,0:T(8,128)(2,1)S(1)} %get-tuple-element.76), channel_id=1, source_target_pairs={{0,64},{64,0},{1,65},{65,1},{2,66},{66,2},{3,67},{67,3},{4,68},{68... | collective-permute-start | bytes 786440 | tf_op jit(solution)/shard_map/ppermute | solution.py:449
  69.5 8.1 %collective-permute-start.21 = (bf16[10,64,128]{2,1,0:T(8,128)(2,1)S(1)}, bf16[10,64,128]{2,1,0:T(8,128)(2,1)S(1)}, u32[]{:S(2)}, u32[]{:S(2)}) collective-permute-start(bf16[10,64,128]{2,1,0:T(8,128)(2,1)S(1)} %get-tuple-element.77), channel_id=1, source_target_pairs={{64,4},{0,124},{65,5},{1,125},{66,6},{2,126},{67,7},{3,127},{68,8}... | collective-permute-start | bytes 491528 | tf_op jit(solution)/shard_map/ppermute | solution.py:452
  71.0 8.1 %collective-permute-start.22 = (bf16[8,64,128]{2,1,0:T(8,128)(2,1)S(1)}, bf16[8,64,128]{2,1,0:T(8,128)(2,1)S(1)}, u32[]{:S(2)}, u32[]{:S(2)}) collective-permute-start(bf16[8,64,128]{2,1,0:T(8,128)(2,1)S(1)} %get-tuple-element.78), channel_id=1, source_target_pairs={{64,4},{0,124},{65,5},{1,125},{66,6},{2,126},{67,7},{3,127},{68,8}... | collective-permute-start | bytes 393224 | tf_op jit(solution)/shard_map/ppermute | solution.py:452
  84.0 10.5 %collective-permute-start.23 = (bf16[14,64,128]{2,1,0:T(8,128)(2,1)S(1)}, bf16[14,64,128]{2,1,0:T(8,128)(2,1)S(1)}, u32[]{:S(2)}, u32[]{:S(2)}) collective-permute-start(bf16[14,64,128]{2,1,0:T(8,128)(2,1)S(1)} %get-tuple-element.80), channel_id=1, source_target_pairs={{0,64},{64,0},{1,65},{65,1},{2,66},{66,2},{3,67},{67,3},{4,68},{68... | collective-permute-start | bytes 688136 | tf_op jit(solution)/shard_map/ppermute | solution.py:449
  84.1 8.5 %collective-permute-start.19 = (bf16[8,64,128]{2,1,0:T(8,128)(2,1)S(1)}, bf16[8,64,128]{2,1,0:T(8,128)(2,1)S(1)}, u32[]{:S(2)}, u32[]{:S(2)}) collective-permute-start(bf16[8,64,128]{2,1,0:T(8,128)(2,1)S(1)} %get-tuple-element.75), channel_id=1, source_target_pairs={{64,4},{0,124},{65,5},{1,125},{66,6},{2,126},{67,7},{3,127},{68,8}... | collective-permute-start | bytes 393224 | tf_op jit(solution)/shard_map/ppermute | solution.py:452
  89.2 12.4 %collective-permute-start.25 = (bf16[10,64,128]{2,1,0:T(8,128)(2,1)S(1)}, bf16[10,64,128]{2,1,0:T(8,128)(2,1)S(1)}, u32[]{:S(2)}, u32[]{:S(2)}) collective-permute-start(bf16[10,64,128]{2,1,0:T(8,128)(2,1)S(1)} %get-tuple-element.84), channel_id=1, source_target_pairs={{64,4},{0,124},{65,5},{1,125},{66,6},{2,126},{67,7},{3,127},{68,8}... | collective-permute-start | bytes 491528 | tf_op jit(solution)/shard_map/ppermute | solution.py:452
  99.5 8.1 %collective-permute-start.27 = (bf16[8,64,128]{2,1,0:T(8,128)(2,1)S(1)}, bf16[8,64,128]{2,1,0:T(8,128)(2,1)S(1)}, u32[]{:S(2)}, u32[]{:S(2)}) collective-permute-start(bf16[8,64,128]{2,1,0:T(8,128)(2,1)S(1)} %get-tuple-element.86), channel_id=1, source_target_pairs={{64,4},{0,124},{65,5},{1,125},{66,6},{2,126},{67,7},{3,127},{68,8}... | collective-permute-start | bytes 393224 | tf_op jit(solution)/shard_map/ppermute | solution.py:452
  115.0 11.0 %collective-permute-start.29 = (bf16[5,2,64,128]{3,2,1,0:T(8,128)(2,1)S(1)}, bf16[5,2,64,128]{3,2,1,0:T(8,128)(2,1)S(1)}, u32[]{:S(2)}, u32[]{:S(2)}) collective-permute-start(bf16[5,2,64,128]{3,2,1,0:T(8,128)(2,1)S(1)} %get-tuple-element.90), channel_id=1, source_target_pairs={{0,1},{1,2},{2,3},{3,0},{4,5},{5,6},{6,7},{7,4},{8,9},{9,10},{10,1... | collective-permute-start | bytes 491528 | tf_op jit(solution)/shard_map/ppermute | solution.py:456
  115.3 10.8 %collective-permute-start.30 = (bf16[5,2,64,128]{3,2,1,0:T(8,128)(2,1)S(1)}, bf16[5,2,64,128]{3,2,1,0:T(8,128)(2,1)S(1)}, u32[]{:S(2)}, u32[]{:S(2)}) collective-permute-start(bf16[5,2,64,128]{3,2,1,0:T(8,128)(2,1)S(1)} %get-tuple-element.91), channel_id=1, source_target_pairs={{0,2},{1,3},{2,0},{3,1},{4,6},{5,7},{6,4},{7,5},{8,10},{9,11},{10,... | collective-permute-start | bytes 491528 | tf_op jit(solution)/shard_map/ppermute | solution.py:456
  117.7 9.0 %collective-permute-start.31 = (bf16[5,2,64,128]{3,2,1,0:T(8,128)(2,1)S(1)}, bf16[5,2,64,128]{3,2,1,0:T(8,128)(2,1)S(1)}, u32[]{:S(2)}, u32[]{:S(2)}) collective-permute-start(bf16[5,2,64,128]{3,2,1,0:T(8,128)(2,1)S(1)} %get-tuple-element.92), channel_id=1, source_target_pairs={{0,3},{1,0},{2,1},{3,2},{4,7},{5,4},{6,5},{7,6},{8,11},{9,8},{10,9... | collective-permute-start | bytes 491528 | tf_op jit(solution)/shard_map/ppermute | solution.py:456
  (17 other events, 174.2 us)

commit v5 on v4

--- a/solution.py
+++ b/solution.py
@@ -254,6 +254,10 @@
     return dict(zip(sizes, results))
 
 
+def in_hbm(*values):
+    return [pltpu.with_memory_space_constraint(v, pltpu.HBM) for v in values]
+
+
 def pack_weights_kernel(sc, *refs):
     sources, (wa, wb, wc, wo) = refs[:10], refs[10:14]
     inputs, sems = refs[14:24], refs[24]
@@ -303,7 +307,7 @@
         + [pltpu.SemaphoreType.DMA((10,))],
         compiler_params=pltpu.CompilerParams(vmem_limit_bytes=32 << 20),
         name="pack_weights",
-    )(scalars, *own, *other)
+    )(scalars, *in_hbm(*own), *other)
 
 
 def cut_state_kernel(sc, *refs):
@@ -337,7 +341,7 @@
         + [pltpu.SemaphoreType.DMA((4,))],
         compiler_params=pltpu.CompilerParams(vmem_limit_bytes=8 << 20),
         name="cut_state",
-    )(scalars, frames, hidden, cell, memory)
+    )(scalars, *in_hbm(frames, hidden, cell, memory))
 
 
 ORDER_A = ((1, "HT"), (4, "M"), (0, "HB"), (2, "CB"), (3, "CT"), (5, "F0"))
@@ -442,8 +446,8 @@
     swap = [(0, 1), (1, 0)]
     across = []
     for i in range(chips):
-        across.append((chips + i, (i + 4) % chips))
-        across.append((i, chips + (i - 4) % chips))
+        across.append((chips + i, i + 4 if i + 4 < chips else chips + (i ^ 1)))
+        across.append((i, chips + i - 4 if i >= 4 else i ^ 1))
 
     def to_partner(value):
         return lax.ppermute(value, "layer", swap)

time: 128 us -> 114 us (0.89)
  the two profiles are of different devices: /device:TPU:0 before, /device:TPU:25 now
where the time goes in v5:
time: 114 us; the launch traced here: 113 us
  waiting for transfers between devices  39.1 us (34%)
  Pallas kernels  37.8 us (33%)
  starting transfers between devices  35.6 us (31%)
    pallas_call x6, Pallas kernels, run_phase(): pl.pallas_call(functools.partial(phase_kernel, plan), out_shape=[jax.Shap...  29.6 us
    ppermute x11, waiting for transfers between devices, to_neighbour(): return lax.ppermute(value, ('layer', 'rows'), across)  20.9 us
    ppermute x15, starting transfers between devices, to_partner(): return lax.ppermute(value, 'layer', swap)  19.5 us
    ppermute x6, waiting for transfers between devices, around(): return lax.ppermute(value, 'rows', turn)  14.5 us
    ppermute x6, starting transfers between devices, around(): return lax.ppermute(value, 'rows', turn)  8.78 us
    ppermute x11, starting transfers between devices, to_neighbour(): return lax.ppermute(value, ('layer', 'rows'), across)  7.36 us
    ppermute x15, waiting for transfers between devices, to_partner(): return lax.ppermute(value, 'layer', swap)  3.78 us
    pallas_call x1, Pallas kernels, pack_weights(): pl.pallas_call(pack_weights_kernel, out_shape=[jax.ShapeDtypeStruct(s, BF...  3.3 us
  transfers between devices with their start and end apart: 32, of which 17 were waited for; matrix products, arithmetic and copies ran while one was open for 0% of the time, Pallas kernels for 14%

profile of v5, /device:TPU:25, one launch (start us, length us, event | category | flops | bytes accessed | tf_op | source)
XLA Modules:
  0.0 113.3 jit_solution(624628888495800863)
XLA Ops:
  5.0 3.3 %collective-permute-start.6 = (bf16[6,2,64,128]{3,2,1,0:T(8,128)(2,1)S(1)}, bf16[6,2,64,128]{3,2,1,0:T(8,128)(2,1)S(1)}, u32[]{:S(2)}, u32[]{:S(2)}) collective-permute-start(bf16[6,2,64,128]{3,2,1,0:T(8,128)(2,1)S(1)} %get-tuple-element.60), channel_id=1, source_target_pairs={{0,2},{1,3},{2,0},{3,1},{4,6},{5,7},{6,4},{7,5},{8,10},{9,11},{10,... | collective-permute-start | bytes 589832 | tf_op jit(solution)/shard_map/ppermute | solution.py:460
  9.9 2.5 %collective-permute-done.5.refs_1_ = bf16[6,2,64,128]{3,2,1,0:T(8,128)(2,1)S(1)} collective-permute-done((bf16[6,2,64,128]{3,2,1,0:T(8,128)(2,1)S(1)}, bf16[6,2,64,128]{3,2,1,0:T(8,128)(2,1)S(1)}, u32[]{:S(2)}, u32[]{:S(2)}) %collective-permute-start.5) | collective-permute-done | bytes 196640 | tf_op jit(solution)/shard_map/ppermute | solution.py:460
  13.0 4.5 %collective-permute-done.6.refs_2_ = bf16[6,2,64,128]{3,2,1,0:T(8,128)(2,1)S(1)} collective-permute-done((bf16[6,2,64,128]{3,2,1,0:T(8,128)(2,1)S(1)}, bf16[6,2,64,128]{3,2,1,0:T(8,128)(2,1)S(1)}, u32[]{:S(2)}, u32[]{:S(2)}) %collective-permute-start.6) | collective-permute-done | bytes 196640 | tf_op jit(solution)/shard_map/ppermute | solution.py:460
  24.0 3.3 %pack_weights.1 = (bf16[4,256,512]{2,1,0:T(8,128)(2,1)S(1)}, bf16[4,448,768]{2,1,0:T(8,128)(2,1)S(1)}, bf16[4,192,448]{2,1,0:T(8,128)(2,1)S(1)}, bf16[4,256,384]{2,1,0:T(8,128)(2,1)S(1)}) custom-call(s32[3]{0:T(128)S(1)} %pad_add_fusion.sc.refs_0_, bf16[2,448,576]{2,1,0:T(8,128)(2,1)} %bitcast.8, bf16[2,576,256]{2,1,0:T(8,128)(2,1)} %refs_1_.1, ...), custom_call_target="tpu_custom_call" | custom-call | tf_op jit(solution)/shard_map/pack_weights/pallas_call | solution.py:300
  28.5 4.9 %two_layers.6 = (bf16[5,4,64,128]{3,2,1,0:T(8,128)(2,1)S(1)}, bf16[16,64,128]{2,1,0:T(8,128)(2,1)S(1)}, bf16[8,64,128]{2,1,0:T(8,128)(2,1)S(1)}, bf16[8,64,128]{2,1,0:T(8,128)(2,1)S(1)}) custom-call(s32[3]{0:T(128)S(1)} %pad_add_fusion.sc.refs_0_, bf16[4,256,512]{2,1,0:T(8,128)(2,1)S(1)} %get-tuple-element.54.refs_1_, ...), custom_call_target="tpu_custom_call" | custom-call | tf_op jit(solution)/shard_map/two_layers/pallas_call | solution.py:233
  33.4 2.1 %collective-permute-start.15 = (bf16[16,64,128]{2,1,0:T(8,128)(2,1)S(1)}, bf16[16,64,128]{2,1,0:T(8,128)(2,1)S(1)}, u32[]{:S(2)}, u32[]{:S(2)}) collective-permute-start(bf16[16,64,128]{2,1,0:T(8,128)(2,1)S(1)} %get-tuple-element.68), channel_id=1, source_target_pairs={{0,64},{64,0},{1,65},{65,1},{2,66},{66,2},{3,67},{67,3},{4,68},{68... | collective-permute-start | bytes 786440 | tf_op jit(solution)/shard_map/ppermute | solution.py:453
  35.6 4.4 %collective-permute-done.16.refs_9_.refs_11_ = bf16[8,64,128]{2,1,0:T(8,128)(2,1)S(1)} collective-permute-done((bf16[8,64,128]{2,1,0:T(8,128)(2,1)S(1)}, bf16[8,64,128]{2,1,0:T(8,128)(2,1)S(1)}, u32[]{:S(2)}, u32[]{:S(2)}) %collective-permute-start.16) | collective-permute-done | bytes 131104 | tf_op jit(solution)/shard_map/ppermute | solution.py:456
  40.0 4.9 %two_layers.7 = (bf16[5,4,64,128]{3,2,1,0:T(8,128)(2,1)S(1)}, bf16[14,64,128]{2,1,0:T(8,128)(2,1)S(1)}, bf16[4,64,128]{2,1,0:T(8,128)(2,1)S(1)}, bf16[10,64,128]{2,1,0:T(8,128)(2,1)S(1)}) custom-call(s32[3]{0:T(128)S(1)} %pad_add_fusion.sc.refs_0_, bf16[4,256,512]{2,1,0:T(8,128)(2,1)S(1)} %get-tuple-element.54.refs_1_, ...), custom_call_target="tpu_custom_call" | custom-call | tf_op jit(solution)/shard_map/two_layers/pallas_call | solution.py:233
  44.9 2.5 %collective-permute-start.17 = (bf16[14,64,128]{2,1,0:T(8,128)(2,1)S(1)}, bf16[14,64,128]{2,1,0:T(8,128)(2,1)S(1)}, u32[]{:S(2)}, u32[]{:S(2)}) collective-permute-start(bf16[14,64,128]{2,1,0:T(8,128)(2,1)S(1)} %get-tuple-element.72), channel_id=1, source_target_pairs={{0,64},{64,0},{1,65},{65,1},{2,66},{66,2},{3,67},{67,3},{4,68},{68... | collective-permute-start | bytes 688136 | tf_op jit(solution)/shard_map/ppermute | solution.py:453
  49.1 2.6 %collective-permute-done.14.refs_6_ = bf16[8,64,128]{2,1,0:T(8,128)(2,1)S(1)} collective-permute-done((bf16[8,64,128]{2,1,0:T(8,128)(2,1)S(1)}, bf16[8,64,128]{2,1,0:T(8,128)(2,1)S(1)}, u32[]{:S(2)}, u32[]{:S(2)}) %collective-permute-start.14) | collective-permute-done | bytes 131104 | tf_op jit(solution)/shard_map/ppermute | solution.py:456
  52.7 4.9 %two_layers.8 = (bf16[5,4,64,128]{3,2,1,0:T(8,128)(2,1)S(1)}, bf16[16,64,128]{2,1,0:T(8,128)(2,1)S(1)}, bf16[8,64,128]{2,1,0:T(8,128)(2,1)S(1)}, bf16[8,64,128]{2,1,0:T(8,128)(2,1)S(1)}) custom-call(s32[3]{0:T(128)S(1)} %pad_add_fusion.sc.refs_0_, bf16[4,256,512]{2,1,0:T(8,128)(2,1)S(1)} %get-tuple-element.54.refs_1_, ...), custom_call_target="tpu_custom_call" | custom-call | tf_op jit(solution)/shard_map/two_layers/pallas_call | solution.py:233
  57.7 3.4 %collective-permute-start.20 = (bf16[16,64,128]{2,1,0:T(8,128)(2,1)S(1)}, bf16[16,64,128]{2,1,0:T(8,128)(2,1)S(1)}, u32[]{:S(2)}, u32[]{:S(2)}) collective-permute-start(bf16[16,64,128]{2,1,0:T(8,128)(2,1)S(1)} %get-tuple-element.76), channel_id=1, source_target_pairs={{0,64},{64,0},{1,65},{65,1},{2,66},{66,2},{3,67},{67,3},{4,68},{68... | collective-permute-start | bytes 786440 | tf_op jit(solution)/shard_map/ppermute | solution.py:453
  62.8 3.3 %collective-permute-done.21.refs_5_ = bf16[10,64,128]{2,1,0:T(8,128)(2,1)S(1)} collective-permute-done((bf16[10,64,128]{2,1,0:T(8,128)(2,1)S(1)}, bf16[10,64,128]{2,1,0:T(8,128)(2,1)S(1)}, u32[]{:S(2)}, u32[]{:S(2)}) %collective-permute-start.21) | collective-permute-done | bytes 163872 | tf_op jit(solution)/shard_map/ppermute | solution.py:456
  67.5 4.9 %two_layers.9 = (bf16[5,4,64,128]{3,2,1,0:T(8,128)(2,1)S(1)}, bf16[14,64,128]{2,1,0:T(8,128)(2,1)S(1)}, bf16[4,64,128]{2,1,0:T(8,128)(2,1)S(1)}, bf16[10,64,128]{2,1,0:T(8,128)(2,1)S(1)}) custom-call(s32[3]{0:T(128)S(1)} %pad_add_fusion.sc.refs_0_, bf16[4,256,512]{2,1,0:T(8,128)(2,1)S(1)} %get-tuple-element.54.refs_1_, ...), custom_call_target="tpu_custom_call" | custom-call | tf_op jit(solution)/shard_map/two_layers/pallas_call | solution.py:233
  72.5 2.0 %collective-permute-start.23 = (bf16[14,64,128]{2,1,0:T(8,128)(2,1)S(1)}, bf16[14,64,128]{2,1,0:T(8,128)(2,1)S(1)}, u32[]{:S(2)}, u32[]{:S(2)}) collective-permute-start(bf16[14,64,128]{2,1,0:T(8,128)(2,1)S(1)} %get-tuple-element.80), channel_id=1, source_target_pairs={{0,64},{64,0},{1,65},{65,1},{2,66},{66,2},{3,67},{67,3},{4,68},{68... | collective-permute-start | bytes 688136 | tf_op jit(solution)/shard_map/ppermute | solution.py:453
  76.2 2.6 %collective-permute-done.19.refs_6_ = bf16[8,64,128]{2,1,0:T(8,128)(2,1)S(1)} collective-permute-done((bf16[8,64,128]{2,1,0:T(8,128)(2,1)S(1)}, bf16[8,64,128]{2,1,0:T(8,128)(2,1)S(1)}, u32[]{:S(2)}, u32[]{:S(2)}) %collective-permute-start.19) | collective-permute-done | bytes 131104 | tf_op jit(solution)/shard_map/ppermute | solution.py:456
  79.8 4.9 %two_layers.10 = (bf16[5,4,64,128]{3,2,1,0:T(8,128)(2,1)S(1)}, bf16[8,64,128]{2,1,0:T(8,128)(2,1)S(1)}, bf16[8,64,128]{2,1,0:T(8,128)(2,1)S(1)}) custom-call(s32[3]{0:T(128)S(1)} %pad_add_fusion.sc.refs_0_, bf16[4,256,512]{2,1,0:T(8,128)(2,1)S(1)} %get-tuple-element.54.refs_1_, bf16[4,448,768]{2,1,0:T(8,128)(2,1)S(1)} %get-tuple-element.55.refs_2_, ...), custom_call_target="tpu_custom_call" | custom-call | tf_op jit(solution)/shard_map/two_layers/pallas_call | solution.py:233
  84.8 2.7 %collective-permute-start.26 = (bf16[8,64,128]{2,1,0:T(8,128)(2,1)S(1)}, bf16[8,64,128]{2,1,0:T(8,128)(2,1)S(1)}, u32[]{:S(2)}, u32[]{:S(2)}) collective-permute-start(bf16[8,64,128]{2,1,0:T(8,128)(2,1)S(1)} %get-tuple-element.85), channel_id=1, source_target_pairs={{0,64},{64,0},{1,65},{65,1},{2,66},{66,2},{3,67},{67,3},{4,68},{68... | collective-permute-start | bytes 393224 | tf_op jit(solution)/shard_map/ppermute | solution.py:453
  88.4 3.4 %collective-permute-done.27.refs_8_ = bf16[8,64,128]{2,1,0:T(8,128)(2,1)S(1)} collective-permute-done((bf16[8,64,128]{2,1,0:T(8,128)(2,1)S(1)}, bf16[8,64,128]{2,1,0:T(8,128)(2,1)S(1)}, u32[]{:S(2)}, u32[]{:S(2)}) %collective-permute-start.27) | collective-permute-done | bytes 131104 | tf_op jit(solution)/shard_map/ppermute | solution.py:456
  91.8 5.0 %two_layers.11 = (bf16[5,4,64,128]{3,2,1,0:T(8,128)(2,1)S(1)}, bf16[5,4,64,128]{3,2,1,0:T(8,128)(2,1)S(1)}) custom-call(s32[3]{0:T(128)S(1)} %pad_add_fusion.sc.refs_0_, bf16[4,256,512]{2,1,0:T(8,128)(2,1)S(1)} %get-tuple-element.54.refs_1_, bf16[4,448,768]{2,1,0:T(8,128)(2,1)S(1)} %get-tuple-element.55.refs_2_, ...), custom_call_target="tpu_custom_call" | custom-call | tf_op jit(solution)/shard_map/two_layers/pallas_call | solution.py:233
  96.8 2.5 %collective-permute-start.28 = (bf16[5,4,64,128]{3,2,1,0:T(8,128)(2,1)S(1)}, bf16[5,4,64,128]{3,2,1,0:T(8,128)(2,1)S(1)}, u32[]{:S(2)}, u32[]{:S(2)}) collective-permute-start(bf16[5,4,64,128]{3,2,1,0:T(8,128)(2,1)S(1)} %get-tuple-element.88), channel_id=1, source_target_pairs={{0,64},{64,0},{1,65},{65,1},{2,66},{66,2},{3,67},{67,3},{4,68},{68... | collective-permute-start | bytes 983048 | tf_op jit(solution)/shard_map/ppermute | solution.py:453
  101.5 2.0 %collective-permute-start.30 = (bf16[5,2,64,128]{3,2,1,0:T(8,128)(2,1)S(1)}, bf16[5,2,64,128]{3,2,1,0:T(8,128)(2,1)S(1)}, u32[]{:S(2)}, u32[]{:S(2)}) collective-permute-start(bf16[5,2,64,128]{3,2,1,0:T(8,128)(2,1)S(1)} %get-tuple-element.91), channel_id=1, source_target_pairs={{0,2},{1,3},{2,0},{3,1},{4,6},{5,7},{6,4},{7,5},{8,10},{9,11},{10,... | collective-permute-start | bytes 491528 | tf_op jit(solution)/shard_map/ppermute | solution.py:460
  104.5 4.3 %collective-permute-done.29.refs_1_ = bf16[5,2,64,128]{3,2,1,0:T(8,128)(2,1)S(1)} collective-permute-done((bf16[5,2,64,128]{3,2,1,0:T(8,128)(2,1)S(1)}, bf16[5,2,64,128]{3,2,1,0:T(8,128)(2,1)S(1)}, u32[]{:S(2)}, u32[]{:S(2)}) %collective-permute-start.29) | collective-permute-done | bytes 163872 | tf_op jit(solution)/shard_map/ppermute | solution.py:460
  108.7 2.2 %collective-permute-done.30.refs_2_ = bf16[5,2,64,128]{3,2,1,0:T(8,128)(2,1)S(1)} collective-permute-done((bf16[5,2,64,128]{3,2,1,0:T(8,128)(2,1)S(1)}, bf16[5,2,64,128]{3,2,1,0:T(8,128)(2,1)S(1)}, u32[]{:S(2)}, u32[]{:S(2)}) %collective-permute-start.30) | collective-permute-done | bytes 163872 | tf_op jit(solution)/shard_map/ppermute | solution.py:460
  (52 shorter events, 29.3 us)
Async XLA Ops:
  0.7 23.3 %collective-permute-start = (bf16[2,448,576]{2,1,0:T(8,128)(2,1)}, bf16[2,448,576]{2,1,0:T(8,128)(2,1)S(1)}, u32[]{:S(2)}, u32[]{:S(2)}) collective-permute-start(bf16[2,448,576]{2,1,0:T(8,128)(2,1)} %bitcast.7), channel_id=1, source_target_pairs={{0,64},{64,0},{1,65},{65,1},{2,66},{66,2},{3,67},{67,3},{4,68},{68... | collective-permute-start | bytes 3096584 | tf_op jit(solution)/shard_map/ppermute | solution.py:453
  3.3 9.1 %collective-permute-start.5 = (bf16[6,2,64,128]{3,2,1,0:T(8,128)(2,1)S(1)}, bf16[6,2,64,128]{3,2,1,0:T(8,128)(2,1)S(1)}, u32[]{:S(2)}, u32[]{:S(2)}) collective-permute-start(bf16[6,2,64,128]{3,2,1,0:T(8,128)(2,1)S(1)} %get-tuple-element.59), channel_id=1, source_target_pairs={{0,1},{1,2},{2,3},{3,0},{4,5},{5,6},{6,7},{7,4},{8,9},{9,10},{10,1... | collective-permute-start | bytes 589832 | tf_op jit(solution)/shard_map/ppermute | solution.py:460
  5.0 12.5 %collective-permute-start.6 = (bf16[6,2,64,128]{3,2,1,0:T(8,128)(2,1)S(1)}, bf16[6,2,64,128]{3,2,1,0:T(8,128)(2,1)S(1)}, u32[]{:S(2)}, u32[]{:S(2)}) collective-permute-start(bf16[6,2,64,128]{3,2,1,0:T(8,128)(2,1)S(1)} %get-tuple-element.60), channel_id=1, source_target_pairs={{0,2},{1,3},{2,0},{3,1},{4,6},{5,7},{6,4},{7,5},{8,10},{9,11},{10,... | collective-permute-start | bytes 589832 | tf_op jit(solution)/shard_map/ppermute | solution.py:460
  8.3 10.1 %collective-permute-start.7 = (bf16[6,2,64,128]{3,2,1,0:T(8,128)(2,1)S(1)}, bf16[6,2,64,128]{3,2,1,0:T(8,128)(2,1)S(1)}, u32[]{:S(2)}, u32[]{:S(2)}) collective-permute-start(bf16[6,2,64,128]{3,2,1,0:T(8,128)(2,1)S(1)} %get-tuple-element.61), channel_id=1, source_target_pairs={{0,3},{1,0},{2,1},{3,2},{4,7},{5,4},{6,5},{7,6},{8,11},{9,8},{10,9... | collective-permute-start | bytes 589832 | tf_op jit(solution)/shard_map/ppermute | solution.py:460
  9.0 9.3 %collective-permute-start.8 = (bf16[6,2,64,128]{3,2,1,0:T(8,128)(2,1)S(1)}, bf16[6,2,64,128]{3,2,1,0:T(8,128)(2,1)S(1)}, u32[]{:S(2)}, u32[]{:S(2)}) collective-permute-start(bf16[6,2,64,128]{3,2,1,0:T(8,128)(2,1)S(1)} %get-tuple-element.58.refs_0_), channel_id=1, source_target_pairs={{0,64},{64,0},{1,65},{65,1},{2,66},{66,2},{3,67},{67,3},{4,68},{68... | collective-permute-start | bytes 589832 | tf_op jit(solution)/shard_map/ppermute | solution.py:453
  12.4 6.5 %collective-permute-start.9 = (bf16[6,2,64,128]{3,2,1,0:T(8,128)(2,1)S(1)}, bf16[6,2,64,128]{3,2,1,0:T(8,128)(2,1)S(1)}, u32[]{:S(2)}, u32[]{:S(2)}) collective-permute-start(bf16[6,2,64,128]{3,2,1,0:T(8,128)(2,1)S(1)} %collective-permute-done.5.refs_1_), channel_id=1, source_target_pairs={{0,64},{64,0},{1,65},{65,1},{2,66},{66,2},{3,67},{67,3},{4,68},{68... | collective-permute-start | bytes 589832 | tf_op jit(solution)/shard_map/ppermute | solution.py:453
  17.5 6.6 %collective-permute-start.1 = (bf16[2,576,256]{2,1,0:T(8,128)(2,1)}, bf16[2,576,256]{2,1,0:T(8,128)(2,1)S(1)}, u32[]{:S(2)}, u32[]{:S(2)}) collective-permute-start(bf16[2,576,256]{2,1,0:T(8,128)(2,1)} %refs_1_.1), channel_id=1, source_target_pairs={{0,64},{64,0},{1,65},{65,1},{2,66},{66,2},{3,67},{67,3},{4,68},{68... | collective-permute-start | bytes 1769480 | tf_op jit(solution)/shard_map/ppermute | solution.py:453
  18.9 5.1 %collective-permute-start.2 = (bf16[2,192,576]{2,1,0:T(8,128)(2,1)}, bf16[2,192,576]{2,1,0:T(8,128)(2,1)S(1)}, u32[]{:S(2)}, u32[]{:S(2)}) collective-permute-start(bf16[2,192,576]{2,1,0:T(8,128)(2,1)} %bitcast.9), channel_id=1, source_target_pairs={{0,64},{64,0},{1,65},{65,1},{2,66},{66,2},{3,67},{67,3},{4,68},{68... | collective-permute-start | bytes 1327112 | tf_op jit(solution)/shard_map/ppermute | solution.py:453
  21.9 6.5 %collective-permute-start.13 = (bf16[18,64,128]{2,1,0:T(8,128)(2,1)S(1)}, bf16[18,64,128]{2,1,0:T(8,128)(2,1)S(1)}, u32[]{:S(2)}, u32[]{:S(2)}) collective-permute-start(bf16[18,64,128]{2,1,0:T(8,128)(2,1)S(1)} %get-tuple-element.63), channel_id=1, source_target_pairs={{64,4},{0,1},{65,5},{1,0},{66,6},{2,3},{67,7},{3,2},{68,8},{4,64},... | collective-permute-start | bytes 884744 | tf_op jit(solution)/shard_map/ppermute | solution.py:456
  23.4 12.2 %collective-permute-start.12 = (bf16[18,64,128]{2,1,0:T(8,128)(2,1)S(1)}, bf16[18,64,128]{2,1,0:T(8,128)(2,1)S(1)}, u32[]{:S(2)}, u32[]{:S(2)}) collective-permute-start(bf16[18,64,128]{2,1,0:T(8,128)(2,1)S(1)} %get-tuple-element.62), channel_id=1, source_target_pairs={{64,4},{0,1},{65,5},{1,0},{66,6},{2,3},{67,7},{3,2},{68,8},{4,64},... | collective-permute-start | bytes 884744 | tf_op jit(solution)/shard_map/ppermute | solution.py:456
  33.4 6.5 %collective-permute-start.15 = (bf16[16,64,128]{2,1,0:T(8,128)(2,1)S(1)}, bf16[16,64,128]{2,1,0:T(8,128)(2,1)S(1)}, u32[]{:S(2)}, u32[]{:S(2)}) collective-permute-start(bf16[16,64,128]{2,1,0:T(8,128)(2,1)S(1)} %get-tuple-element.68), channel_id=1, source_target_pairs={{0,64},{64,0},{1,65},{65,1},{2,66},{66,2},{3,67},{67,3},{4,68},{68... | collective-permute-start | bytes 786440 | tf_op jit(solution)/shard_map/ppermute | solution.py:453
  35.6 4.4 %collective-permute-start.16 = (bf16[8,64,128]{2,1,0:T(8,128)(2,1)S(1)}, bf16[8,64,128]{2,1,0:T(8,128)(2,1)S(1)}, u32[]{:S(2)}, u32[]{:S(2)}) collective-permute-start(bf16[8,64,128]{2,1,0:T(8,128)(2,1)S(1)} %get-tuple-element.70), channel_id=1, source_target_pairs={{64,4},{0,1},{65,5},{1,0},{66,6},{2,3},{67,7},{3,2},{68,8},{4,64},... | collective-permute-start | bytes 393224 | tf_op jit(solution)/shard_map/ppermute | solution.py:456
  44.9 7.9 %collective-permute-start.17 = (bf16[14,64,128]{2,1,0:T(8,128)(2,1)S(1)}, bf16[14,64,128]{2,1,0:T(8,128)(2,1)S(1)}, u32[]{:S(2)}, u32[]{:S(2)}) collective-permute-start(bf16[14,64,128]{2,1,0:T(8,128)(2,1)S(1)} %get-tuple-element.72), channel_id=1, source_target_pairs={{0,64},{64,0},{1,65},{65,1},{2,66},{66,2},{3,67},{67,3},{4,68},{68... | collective-permute-start | bytes 688136 | tf_op jit(solution)/shard_map/ppermute | solution.py:453
  47.4 5.4 %collective-permute-start.18 = (bf16[4,64,128]{2,1,0:T(8,128)(2,1)S(1)}, bf16[4,64,128]{2,1,0:T(8,128)(2,1)S(1)}, u32[]{:S(2)}, u32[]{:S(2)}) collective-permute-start(bf16[4,64,128]{2,1,0:T(8,128)(2,1)S(1)} %get-tuple-element.73), channel_id=1, source_target_pairs={{64,4},{0,1},{65,5},{1,0},{66,6},{2,3},{67,7},{3,2},{68,8},{4,64},... | collective-permute-start | bytes 196616 | tf_op jit(solution)/shard_map/ppermute | solution.py:456
  57.7 9.8 %collective-permute-start.20 = (bf16[16,64,128]{2,1,0:T(8,128)(2,1)S(1)}, bf16[16,64,128]{2,1,0:T(8,128)(2,1)S(1)}, u32[]{:S(2)}, u32[]{:S(2)}) collective-permute-start(bf16[16,64,128]{2,1,0:T(8,128)(2,1)S(1)} %get-tuple-element.76), channel_id=1, source_target_pairs={{0,64},{64,0},{1,65},{65,1},{2,66},{66,2},{3,67},{67,3},{4,68},{68... | collective-permute-start | bytes 786440 | tf_op jit(solution)/shard_map/ppermute | solution.py:453
  61.1 5.0 %collective-permute-start.21 = (bf16[10,64,128]{2,1,0:T(8,128)(2,1)S(1)}, bf16[10,64,128]{2,1,0:T(8,128)(2,1)S(1)}, u32[]{:S(2)}, u32[]{:S(2)}) collective-permute-start(bf16[10,64,128]{2,1,0:T(8,128)(2,1)S(1)} %get-tuple-element.77), channel_id=1, source_target_pairs={{64,4},{0,1},{65,5},{1,0},{66,6},{2,3},{67,7},{3,2},{68,8},{4,64},... | collective-permute-start | bytes 491528 | tf_op jit(solution)/shard_map/ppermute | solution.py:456
  61.1 6.4 %collective-permute-start.22 = (bf16[8,64,128]{2,1,0:T(8,128)(2,1)S(1)}, bf16[8,64,128]{2,1,0:T(8,128)(2,1)S(1)}, u32[]{:S(2)}, u32[]{:S(2)}) collective-permute-start(bf16[8,64,128]{2,1,0:T(8,128)(2,1)S(1)} %get-tuple-element.78), channel_id=1, source_target_pairs={{64,4},{0,1},{65,5},{1,0},{66,6},{2,3},{67,7},{3,2},{68,8},{4,64},... | collective-permute-start | bytes 393224 | tf_op jit(solution)/shard_map/ppermute | solution.py:456
  72.5 7.4 %collective-permute-start.23 = (bf16[14,64,128]{2,1,0:T(8,128)(2,1)S(1)}, bf16[14,64,128]{2,1,0:T(8,128)(2,1)S(1)}, u32[]{:S(2)}, u32[]{:S(2)}) collective-permute-start(bf16[14,64,128]{2,1,0:T(8,128)(2,1)S(1)} %get-tuple-element.80), channel_id=1, source_target_pairs={{0,64},{64,0},{1,65},{65,1},{2,66},{66,2},{3,67},{67,3},{4,68},{68... | collective-permute-start | bytes 688136 | tf_op jit(solution)/shard_map/ppermute | solution.py:453
  74.5 5.4 %collective-permute-start.24 = (bf16[4,64,128]{2,1,0:T(8,128)(2,1)S(1)}, bf16[4,64,128]{2,1,0:T(8,128)(2,1)S(1)}, u32[]{:S(2)}, u32[]{:S(2)}) collective-permute-start(bf16[4,64,128]{2,1,0:T(8,128)(2,1)S(1)} %get-tuple-element.81), channel_id=1, source_target_pairs={{64,4},{0,1},{65,5},{1,0},{66,6},{2,3},{67,7},{3,2},{68,8},{4,64},... | collective-permute-start | bytes 196616 | tf_op jit(solution)/shard_map/ppermute | solution.py:456
  76.2 11.3 %collective-permute-start.25 = (bf16[10,64,128]{2,1,0:T(8,128)(2,1)S(1)}, bf16[10,64,128]{2,1,0:T(8,128)(2,1)S(1)}, u32[]{:S(2)}, u32[]{:S(2)}) collective-permute-start(bf16[10,64,128]{2,1,0:T(8,128)(2,1)S(1)} %get-tuple-element.84), channel_id=1, source_target_pairs={{64,4},{0,1},{65,5},{1,0},{66,6},{2,3},{67,7},{3,2},{68,8},{4,64},... | collective-permute-start | bytes 491528 | tf_op jit(solution)/shard_map/ppermute | solution.py:456
  87.5 4.4 %collective-permute-start.27 = (bf16[8,64,128]{2,1,0:T(8,128)(2,1)S(1)}, bf16[8,64,128]{2,1,0:T(8,128)(2,1)S(1)}, u32[]{:S(2)}, u32[]{:S(2)}) collective-permute-start(bf16[8,64,128]{2,1,0:T(8,128)(2,1)S(1)} %get-tuple-element.86), channel_id=1, source_target_pairs={{64,4},{0,1},{65,5},{1,0},{66,6},{2,3},{67,7},{3,2},{68,8},{4,64},... | collective-permute-start | bytes 393224 | tf_op jit(solution)/shard_map/ppermute | solution.py:456
  101.4 7.3 %collective-permute-start.29 = (bf16[5,2,64,128]{3,2,1,0:T(8,128)(2,1)S(1)}, bf16[5,2,64,128]{3,2,1,0:T(8,128)(2,1)S(1)}, u32[]{:S(2)}, u32[]{:S(2)}) collective-permute-start(bf16[5,2,64,128]{3,2,1,0:T(8,128)(2,1)S(1)} %get-tuple-element.90), channel_id=1, source_target_pairs={{0,1},{1,2},{2,3},{3,0},{4,5},{5,6},{6,7},{7,4},{8,9},{9,10},{10,1... | collective-permute-start | bytes 491528 | tf_op jit(solution)/shard_map/ppermute | solution.py:460
  101.5 9.5 %collective-permute-start.30 = (bf16[5,2,64,128]{3,2,1,0:T(8,128)(2,1)S(1)}, bf16[5,2,64,128]{3,2,1,0:T(8,128)(2,1)S(1)}, u32[]{:S(2)}, u32[]{:S(2)}) collective-permute-start(bf16[5,2,64,128]{3,2,1,0:T(8,128)(2,1)S(1)} %get-tuple-element.91), channel_id=1, source_target_pairs={{0,2},{1,3},{2,0},{3,1},{4,6},{5,7},{6,4},{7,5},{8,10},{9,11},{10,... | collective-permute-start | bytes 491528 | tf_op jit(solution)/shard_map/ppermute | solution.py:460
  103.5 8.4 %collective-permute-start.31 = (bf16[5,2,64,128]{3,2,1,0:T(8,128)(2,1)S(1)}, bf16[5,2,64,128]{3,2,1,0:T(8,128)(2,1)S(1)}, u32[]{:S(2)}, u32[]{:S(2)}) collective-permute-start(bf16[5,2,64,128]{3,2,1,0:T(8,128)(2,1)S(1)} %get-tuple-element.92), channel_id=1, source_target_pairs={{0,3},{1,0},{2,1},{3,2},{4,7},{5,4},{6,5},{7,6},{8,11},{9,8},{10,9... | collective-permute-start | bytes 491528 | tf_op jit(solution)/shard_map/ppermute | solution.py:460
  (8 other events, 24.8 us)

commit v6 on v5

--- a/solution.py
+++ b/solution.py
@@ -48,14 +48,7 @@
     return jnp.concatenate([before, row, after], axis=0)
 
 
-def phase_kernel(plan, *refs):
-    names = plan["names"]
-    outs = plan["outs"]
-    n_in = len(names)
-    ref = dict(zip(names, refs[:n_in]))
-    out = dict(zip(outs, refs[n_in : n_in + len(outs)]))
-    tx, th, tm, tx2, th2, tm2, yb, ob, yb2, ob2, raw = refs[n_in + len(outs) :]
-    state_out = out["state"]
+def accessors(ref, fields):
     core = ref["sc"][0]
     top = ref["sc"][1]
     first_core = core == 0
@@ -67,7 +60,7 @@
         return jnp.where(jnp.logical_and(g >= 0, g < 128), value, jnp.zeros_like(value))
 
     def fetch(field, row):
-        (own, slot), (near, near_at, far, far_at, count) = plan["fields"][field]
+        (own, slot), (near, near_at, far, far_at, count) = fields[field]
         if 0 <= row < OWN:
             return ref[own][slot, row]
         if row < 0:
@@ -78,6 +71,63 @@
             value = jnp.where(first_core, ref[near][near_at + unit], ref[far][far_at + unit])
         return keep(row, value)
 
+    return first_core, keep, fetch
+
+
+def stacked(bufs, q):
+    cols = [
+        jnp.concatenate([buf[i + a] for buf in bufs for a in range(3)], axis=0) for i in (q, q + 1)
+    ]
+    return jnp.concatenate(cols, axis=1)
+
+
+def early_kernel(plan, *refs):
+    names, half = plan["names"], plan["half"]
+    ref = dict(zip(names, refs))
+    sums, tx, th, th2 = refs[len(names) : len(names) + 2], *refs[len(names) + 2 :]
+    _, _, fetch = accessors(ref, plan["fields"])
+    filled = set()
+
+    def fill(buf, field, reach, upto):
+        for i in range(upto):
+            if (field, i) not in filled:
+                filled.add((field, i))
+                buf[i] = taps_of(fetch(field, i - reach))
+
+    for index in range(2):
+        layer = plan["layer"] + index
+        for q in range(0, OWN + 2 * REACH[index], 2):
+            with_x = half == 0 and index == 0
+            fill((th, th2)[index], ("HB", "HT")[index], REACH[index] + 1, q + 4)
+            h = stacked([(th, th2)[index]], q)
+            own = jnp.dot(ref["wa"][layer], h[0:512], preferred_element_type=F32)
+            if with_x:
+                fill(tx, "X", 4, q + 4)
+                x = stacked([tx], q)
+                shared = jnp.dot(
+                    ref["wb"][layer, :, 0:640],
+                    jnp.concatenate([x, h[512:576]], axis=0),
+                    preferred_element_type=F32,
+                )
+                sums[index][q // 2, 0:256] = own + shared[0:256]
+                sums[index][q // 2, 256:448] = shared[256:448]
+            else:
+                rest = jnp.concatenate([jnp.zeros((64, 2 * GW), BF), h[512:576]], axis=0)
+                sums[index][q // 2] = own + jnp.dot(
+                    ref["wb"][layer, 0:256, 512:640], rest, preferred_element_type=F32
+                )
+
+
+def phase_kernel(plan, *refs):
+    names = plan["names"]
+    outs = plan["outs"]
+    n_in = len(names)
+    ref = dict(zip(names, refs[:n_in]))
+    out = dict(zip(outs, refs[n_in : n_in + len(outs)]))
+    tx, th, tm, tx2, th2, tm2, yb, ob, yb2, ob2 = refs[n_in + len(outs) :]
+    state_out = out["state"]
+    first_core, keep, fetch = accessors(ref, plan["fields"])
+
     rows_of = [list(range(-reach, OWN + reach)) for reach in REACH]
     bufs = ((tx, th, tm, yb, ob), (tx2, th2, tm2.at[1:9], yb2, ob2))
     filled = set()
@@ -88,34 +138,36 @@
                 filled.add((key, i))
                 buf[i] = taps_of(fetch(field, i - reach))
 
+    early = plan["early"]
+
     def matmuls(index, q):
         bx, bh, bm, _, _ = bufs[index]
+        layer = plan["layer"] + index
+        add = lambda w, rhs: jnp.dot(w, rhs, preferred_element_type=F32)
         if index == 0:
-            fill(tx, "x", "X", 4, q + 4)
-            fill(th, "h", "HB", 4, q + 4)
             fill(tm, "m", "M", 4, q + 4)
+            if not (early and plan["half"] == 0):
+                fill(tx, "x", "X", 4, q + 4)
+        m = stacked([bm], q)
+        rest = add(ref["wc"][layer], m[128:576])
+        if early and plan["half"] == 0 and index == 0:
+            acc2 = rest + add(ref["wb"][layer, 256:448, 640:768], m[0:128])
+            return ref["sums0"][q // 2, 0:256], acc2 + ref["sums0"][q // 2, 256:448]
+        if early:
+            h_rest = jnp.zeros((64, 2 * GW), BF)
+            own = ref[f"sums{index}"][q // 2]
         else:
-            fill(th2, "h2", "HT", 2, q + 4)
-        cols = [
-            jnp.concatenate([buf[i + a] for buf in (bx, bh, bm) for a in range(3)], axis=0)
-            for i in (q, q + 1)
-        ]
-        rhs = jnp.concatenate(cols, axis=1)
-        x, h, m = rhs[0:576], rhs[576:1152], rhs[1152:1728]
-        layer = plan["layer"] + index
-        shared = jnp.dot(
-            ref["wb"][layer],
-            jnp.concatenate([x, h[512:576], m[0:128]], axis=0),
-            preferred_element_type=F32,
+            if index == 0:
+                fill(th, "h", "HB", 4, q + 4)
+            else:
+                fill(th2, "h2", "HT", 2, q + 4)
+            h = stacked([bh], q)
+            h_rest = h[512:576]
+            own = add(ref["wa"][layer], h[0:512])
+        shared = add(
+            ref["wb"][layer], jnp.concatenate([stacked([bx], q), h_rest, m[0:128]], axis=0)
         )
-        slot = (q // 2 + index) % 2
-        raw[slot, 0:256] = shared[0:256] + jnp.dot(
-            ref["wa"][layer], h[0:512], preferred_element_type=F32
-        )
-        raw[slot, 256:448] = shared[256:448] + jnp.dot(
-            ref["wc"][layer], m[128:576], preferred_element_type=F32
-        )
-        return raw.at[slot, 0:256], raw.at[slot, 256:448]
+        return shared[0:256] + own, shared[256:448] + rest
 
     def gates(index, q, acc1, acc2):
         _, _, _, y_buf, o_buf = bufs[index]
@@ -212,6 +264,29 @@
         send(out["late"], LATE[half], jnp.logical_not(first_core))
 
 
+def run_early(operands, plan):
+    names = list(operands)
+    plan = dict(plan, names=names)
+    height = 448 if plan["half"] == 0 else 256
+    taps = (3 * CH, GW)
+    return pl.pallas_call(
+        functools.partial(early_kernel, plan),
+        out_shape=[
+            jax.ShapeDtypeStruct((5, height, 2 * GW), F32),
+            jax.ShapeDtypeStruct((3, 256, 2 * GW), F32),
+        ],
+        in_specs=[
+            pl.BlockSpec(memory_space=pltpu.SMEM if name == "sc" else pltpu.VMEM) for name in names
+        ],
+        out_specs=[pl.BlockSpec(memory_space=pltpu.VMEM)] * 2,
+        scratch_shapes=[
+            pltpu.VMEM((12,) + taps, BF), pltpu.VMEM((12,) + taps, BF), pltpu.VMEM((8,) + taps, BF)
+        ],
+        compiler_params=pltpu.CompilerParams(vmem_limit_bytes=12 << 20),
+        name="early_sums",
+    )(*[operands[name] for name in names])
+
+
 def run_phase(operands, plan):
     names = list(operands)
     plan = dict(plan, names=names)
@@ -246,7 +321,6 @@
             pltpu.VMEM((CH, 10 * GW), F32),
             pltpu.VMEM((4 * CH, 6 * GW), F32),
             pltpu.VMEM((CH, 6 * GW), F32),
-            pltpu.VMEM((2, 7 * CH, 2 * GW), F32),
         ],
         compiler_params=pltpu.CompilerParams(vmem_limit_bytes=24 << 20),
         name="two_layers",
@@ -500,16 +574,32 @@
             fields = {k: ((states[half], SLOT[k]), halo[half][k]) for k in kept}
             fields["M"] = (own_m, halo_m)
             fields["X"] = x_field
-            needed = {f[0][0] for f in fields.values()}
-            needed |= {f[1][i] for f in fields.values() for i in (0, 2)}
-            operands = dict(base)
-            for name in sorted(needed):
-                operands[name] = arrays[name]
-            plan = {"fields": fields, "half": half, "layer": 2 * half, "send": send}
+            tag = f"{step}{half}"
+            early = tag != "00"
+            ahead = ("HB", "HT", "X") if half == 0 else ("HB", "HT")
+
+            def gather(wanted, weights):
+                used = {k: fields[k] for k in wanted}
+                needed = {f[0][0] for f in used.values()}
+                needed |= {f[1][i] for f in used.values() for i in (0, 2)}
+                operands = {k: base[k] for k in ("sc",) + weights}
+                operands.update({name: arrays[name] for name in sorted(needed)})
+                return used, operands
+
+            plan = {"half": half, "layer": 2 * half, "send": send, "early": early}
+            if early:
+                used, operands = gather(ahead, ("wa", "wb"))
+                sums = run_early(operands, dict(plan, fields=used))
+                used, operands = gather(
+                    [k for k in fields if k not in ahead], ("wb", "wc", "wo")
+                )
+                operands.update(sums0=sums[0], sums1=sums[1])
+            else:
+                used, operands = gather(fields, ("wa", "wb", "wc", "wo"))
+            plan["fields"] = used
             if not send:
                 plan["lower"] = states[0]
                 operands[states[0]] = arrays[states[0]]
-            tag = f"{step}{half}"
             outs = run_phase(operands, plan)
             results[half] = outs["state"]
             states[half] = "state" + tag

time: 114 us -> 112 us (0.982)
  waiting for transfers between devices: 39.1 us -> 32.5 us
  Pallas kernels: 37.8 us -> 42.7 us
    pallas_call x0 -> x5, Pallas kernels: none -> 9.71 us  [run_early(): pl.pallas_call(functools.partial(early_kernel, plan), out_shape=[jax.Shap...]
    ppermute x11, waiting for transfers between devices: 20.9 us -> 15.2 us  [to_neighbour(): return lax.ppermute(value, ('layer', 'rows'), across)]
    pallas_call x6, Pallas kernels: 29.6 us -> 24.8 us  [run_phase(): pl.pallas_call(functools.partial(phase_kernel, plan), out_shape=[jax.Shap...]
  transfers between devices with their start and end apart: 32 -> 32, of which waited for: 17 -> 13; matrix products, arithmetic and copies ran while one was open for 0% -> 0% of each run, Pallas kernels for 14% -> 22%
where the time goes in v6:
time: 112 us; the launch traced here: 111 us
  Pallas kernels  42.7 us (38%)
  starting transfers between devices  34.9 us (31%)
  waiting for transfers between devices  32.5 us (29%)
    pallas_call x6, Pallas kernels, run_phase(): pl.pallas_call(functools.partial(phase_kernel, plan), out_shape=[jax.Shap...  24.8 us
    ppermute x15, starting transfers between devices, to_partner(): return lax.ppermute(value, 'layer', swap)  18.8 us
    ppermute x11, waiting for transfers between devices, to_neighbour(): return lax.ppermute(value, ('layer', 'rows'), across)  15.2 us
    ppermute x6, waiting for transfers between devices, around(): return lax.ppermute(value, 'rows', turn)  14.5 us
    pallas_call x5, Pallas kernels, run_early(): pl.pallas_call(functools.partial(early_kernel, plan), out_shape=[jax.Shap...  9.71 us
    ppermute x6, starting transfers between devices, around(): return lax.ppermute(value, 'rows', turn)  8.78 us
    ppermute x11, starting transfers between devices, to_neighbour(): return lax.ppermute(value, ('layer', 'rows'), across)  7.36 us
    pallas_call x1, Pallas kernels, pack_weights(): pl.pallas_call(pack_weights_kernel, out_shape=[jax.ShapeDtypeStruct(s, BF...  3.3 us
  transfers between devices with their start and end apart: 32, of which 13 were waited for; matrix products, arithmetic and copies ran while one was open for 0% of the time, Pallas kernels for 22%

profile of v6, /device:TPU:25, one launch (start us, length us, event | category | flops | bytes accessed | tf_op | source)
XLA Modules:
  0.0 111.0 jit_solution(7517043178185530377)
XLA Ops:
  5.0 3.3 %collective-permute-start.6 = (bf16[6,2,64,128]{3,2,1,0:T(8,128)(2,1)S(1)}, bf16[6,2,64,128]{3,2,1,0:T(8,128)(2,1)S(1)}, u32[]{:S(2)}, u32[]{:S(2)}) collective-permute-start(bf16[6,2,64,128]{3,2,1,0:T(8,128)(2,1)S(1)} %get-tuple-element.70), channel_id=1, source_target_pairs={{0,2},{1,3},{2,0},{3,1},{4,6},{5,7},{6,4},{7,5},{8,10},{9,11},{10,... | collective-permute-start | bytes 589832 | tf_op jit(solution)/shard_map/ppermute | solution.py:534
  9.9 2.5 %collective-permute-done.5.refs_1_ = bf16[6,2,64,128]{3,2,1,0:T(8,128)(2,1)S(1)} collective-permute-done((bf16[6,2,64,128]{3,2,1,0:T(8,128)(2,1)S(1)}, bf16[6,2,64,128]{3,2,1,0:T(8,128)(2,1)S(1)}, u32[]{:S(2)}, u32[]{:S(2)}) %collective-permute-start.5) | collective-permute-done | bytes 196640 | tf_op jit(solution)/shard_map/ppermute | solution.py:534
  13.0 4.5 %collective-permute-done.6.refs_2_ = bf16[6,2,64,128]{3,2,1,0:T(8,128)(2,1)S(1)} collective-permute-done((bf16[6,2,64,128]{3,2,1,0:T(8,128)(2,1)S(1)}, bf16[6,2,64,128]{3,2,1,0:T(8,128)(2,1)S(1)}, u32[]{:S(2)}, u32[]{:S(2)}) %collective-permute-start.6) | collective-permute-done | bytes 196640 | tf_op jit(solution)/shard_map/ppermute | solution.py:534
  24.0 3.3 %pack_weights.1 = (bf16[4,256,512]{2,1,0:T(8,128)(2,1)S(1)}, bf16[4,448,768]{2,1,0:T(8,128)(2,1)S(1)}, bf16[4,192,448]{2,1,0:T(8,128)(2,1)S(1)}, bf16[4,256,384]{2,1,0:T(8,128)(2,1)S(1)}) custom-call(s32[3]{0:T(128)S(1)} %pad_add_fusion.sc.refs_0_, bf16[2,448,576]{2,1,0:T(8,128)(2,1)} %bitcast.8, bf16[2,576,256]{2,1,0:T(8,128)(2,1)} %refs_1_.1, ...), custom_call_target="tpu_custom_call" | custom-call | tf_op jit(solution)/shard_map/pack_weights/pallas_call | solution.py:374
  28.5 4.9 %two_layers.6 = (bf16[5,4,64,128]{3,2,1,0:T(8,128)(2,1)S(1)}, bf16[16,64,128]{2,1,0:T(8,128)(2,1)S(1)}, bf16[8,64,128]{2,1,0:T(8,128)(2,1)S(1)}, bf16[8,64,128]{2,1,0:T(8,128)(2,1)S(1)}) custom-call(s32[3]{0:T(128)S(1)} %pad_add_fusion.sc.refs_0_, bf16[4,256,512]{2,1,0:T(8,128)(2,1)S(1)} %get-tuple-element.67.refs_1_, ...), custom_call_target="tpu_custom_call" | custom-call | tf_op jit(solution)/shard_map/two_layers/pallas_call | solution.py:308
  37.2 2.8 %collective-permute-done.16.refs_8_ = bf16[8,64,128]{2,1,0:T(8,128)(2,1)S(1)} collective-permute-done((bf16[8,64,128]{2,1,0:T(8,128)(2,1)S(1)}, bf16[8,64,128]{2,1,0:T(8,128)(2,1)S(1)}, u32[]{:S(2)}, u32[]{:S(2)}) %collective-permute-start.16) | collective-permute-done | bytes 131104 | tf_op jit(solution)/shard_map/ppermute | solution.py:530
  39.9 4.3 %two_layers.7 = (bf16[5,4,64,128]{3,2,1,0:T(8,128)(2,1)S(1)}, bf16[14,64,128]{2,1,0:T(8,128)(2,1)S(1)}, bf16[4,64,128]{2,1,0:T(8,128)(2,1)S(1)}, bf16[10,64,128]{2,1,0:T(8,128)(2,1)S(1)}) custom-call(s32[3]{0:T(128)S(1)} %pad_add_fusion.sc.refs_0_, bf16[4,448,768]{2,1,0:T(8,128)(2,1)S(1)} %get-tuple-element.64.refs_2_.refs_1_, ...), custom_call_target="tpu_custom_call" | custom-call | tf_op jit(solution)/shard_map/two_layers/pallas_call | solution.py:308
  44.2 2.5 %collective-permute-start.17 = (bf16[14,64,128]{2,1,0:T(8,128)(2,1)S(1)}, bf16[14,64,128]{2,1,0:T(8,128)(2,1)S(1)}, u32[]{:S(2)}, u32[]{:S(2)}) collective-permute-start(bf16[14,64,128]{2,1,0:T(8,128)(2,1)S(1)} %get-tuple-element.84), channel_id=1, source_target_pairs={{0,64},{64,0},{1,65},{65,1},{2,66},{66,2},{3,67},{67,3},{4,68},{68... | collective-permute-start | bytes 688136 | tf_op jit(solution)/shard_map/ppermute | solution.py:527
  48.4 2.6 %collective-permute-done.13.refs_4_ = bf16[8,64,128]{2,1,0:T(8,128)(2,1)S(1)} collective-permute-done((bf16[8,64,128]{2,1,0:T(8,128)(2,1)S(1)}, bf16[8,64,128]{2,1,0:T(8,128)(2,1)S(1)}, u32[]{:S(2)}, u32[]{:S(2)}) %collective-permute-start.13) | collective-permute-done | bytes 131104 | tf_op jit(solution)/shard_map/ppermute | solution.py:530
  51.1 2.4 %early_sums.6 = (f32[5,448,256]{2,1,0:T(8,128)S(1)}, f32[3,256,256]{2,1,0:T(8,128)S(1)}) custom-call(s32[3]{0:T(128)S(1)} %pad_add_fusion.sc.refs_0_, bf16[4,256,512]{2,1,0:T(8,128)(2,1)S(1)} %get-tuple-element.67.refs_1_, bf16[4,448,768]{2,1,0:T(8,128)(2,1)S(1)} %get-tuple-element.64.refs_2_.refs_1_, ...), custom_call_target="tpu_custom_call" | custom-call | tf_op jit(solution)/shard_map/early_sums/pallas_call | solution.py:272
  53.5 3.5 %two_layers.8 = (bf16[5,4,64,128]{3,2,1,0:T(8,128)(2,1)S(1)}, bf16[16,64,128]{2,1,0:T(8,128)(2,1)S(1)}, bf16[8,64,128]{2,1,0:T(8,128)(2,1)S(1)}, bf16[8,64,128]{2,1,0:T(8,128)(2,1)S(1)}) custom-call(s32[3]{0:T(128)S(1)} %pad_add_fusion.sc.refs_0_, bf16[4,448,768]{2,1,0:T(8,128)(2,1)S(1)} %get-tuple-element.64.refs_2_.refs_1_, ...), custom_call_target="tpu_custom_call" | custom-call | tf_op jit(solution)/shard_map/two_layers/pallas_call | solution.py:308
  57.0 2.3 %collective-permute-start.20 = (bf16[16,64,128]{2,1,0:T(8,128)(2,1)S(1)}, bf16[16,64,128]{2,1,0:T(8,128)(2,1)S(1)}, u32[]{:S(2)}, u32[]{:S(2)}) collective-permute-start(bf16[16,64,128]{2,1,0:T(8,128)(2,1)S(1)} %get-tuple-element.90), channel_id=1, source_target_pairs={{0,64},{64,0},{1,65},{65,1},{2,66},{66,2},{3,67},{67,3},{4,68},{68... | collective-permute-start | bytes 786440 | tf_op jit(solution)/shard_map/ppermute | solution.py:527
  61.1 3.3 %collective-permute-done.21.refs_3_.refs_4_ = bf16[10,64,128]{2,1,0:T(8,128)(2,1)S(1)} collective-permute-done((bf16[10,64,128]{2,1,0:T(8,128)(2,1)S(1)}, bf16[10,64,128]{2,1,0:T(8,128)(2,1)S(1)}, u32[]{:S(2)}, u32[]{:S(2)}) %collective-permute-start.21) | collective-permute-done | bytes 163872 | tf_op jit(solution)/shard_map/ppermute | solution.py:530
  66.0 4.3 %two_layers.9 = (bf16[5,4,64,128]{3,2,1,0:T(8,128)(2,1)S(1)}, bf16[14,64,128]{2,1,0:T(8,128)(2,1)S(1)}, bf16[4,64,128]{2,1,0:T(8,128)(2,1)S(1)}, bf16[10,64,128]{2,1,0:T(8,128)(2,1)S(1)}) custom-call(s32[3]{0:T(128)S(1)} %pad_add_fusion.sc.refs_0_, bf16[4,448,768]{2,1,0:T(8,128)(2,1)S(1)} %get-tuple-element.64.refs_2_.refs_1_, ...), custom_call_target="tpu_custom_call" | custom-call | tf_op jit(solution)/shard_map/two_layers/pallas_call | solution.py:308
  70.3 2.8 %collective-permute-start.23 = (bf16[14,64,128]{2,1,0:T(8,128)(2,1)S(1)}, bf16[14,64,128]{2,1,0:T(8,128)(2,1)S(1)}, u32[]{:S(2)}, u32[]{:S(2)}) collective-permute-start(bf16[14,64,128]{2,1,0:T(8,128)(2,1)S(1)} %get-tuple-element.96), channel_id=1, source_target_pairs={{0,64},{64,0},{1,65},{65,1},{2,66},{66,2},{3,67},{67,3},{4,68},{68... | collective-permute-start | bytes 688136 | tf_op jit(solution)/shard_map/ppermute | solution.py:527
  74.9 2.6 %collective-permute-done.19.refs_4_ = bf16[8,64,128]{2,1,0:T(8,128)(2,1)S(1)} collective-permute-done((bf16[8,64,128]{2,1,0:T(8,128)(2,1)S(1)}, bf16[8,64,128]{2,1,0:T(8,128)(2,1)S(1)}, u32[]{:S(2)}, u32[]{:S(2)}) %collective-permute-start.19) | collective-permute-done | bytes 131104 | tf_op jit(solution)/shard_map/ppermute | solution.py:530
  77.5 2.4 %early_sums.8 = (f32[5,448,256]{2,1,0:T(8,128)S(1)}, f32[3,256,256]{2,1,0:T(8,128)S(1)}) custom-call(s32[3]{0:T(128)S(1)} %pad_add_fusion.sc.refs_0_, bf16[4,256,512]{2,1,0:T(8,128)(2,1)S(1)} %get-tuple-element.67.refs_1_, bf16[4,448,768]{2,1,0:T(8,128)(2,1)S(1)} %get-tuple-element.64.refs_2_.refs_1_, ...), custom_call_target="tpu_custom_call" | custom-call | tf_op jit(solution)/shard_map/early_sums/pallas_call | solution.py:272
  80.0 3.5 %two_layers.10 = (bf16[5,4,64,128]{3,2,1,0:T(8,128)(2,1)S(1)}, bf16[8,64,128]{2,1,0:T(8,128)(2,1)S(1)}, bf16[8,64,128]{2,1,0:T(8,128)(2,1)S(1)}) custom-call(s32[3]{0:T(128)S(1)} %pad_add_fusion.sc.refs_0_, bf16[4,448,768]{2,1,0:T(8,128)(2,1)S(1)} %get-tuple-element.64.refs_2_.refs_1_, bf16[4,192,448]{2,1,0:T(8,128)(2,1)S(1)} %get-tuple-element.65.refs_3_.refs_2_, ...), custom_call_target="tpu_custom_call" | custom-call | tf_op jit(solution)/shard_map/two_layers/pallas_call | solution.py:308
  83.4 2.3 %collective-permute-start.26 = (bf16[8,64,128]{2,1,0:T(8,128)(2,1)S(1)}, bf16[8,64,128]{2,1,0:T(8,128)(2,1)S(1)}, u32[]{:S(2)}, u32[]{:S(2)}) collective-permute-start(bf16[8,64,128]{2,1,0:T(8,128)(2,1)S(1)} %get-tuple-element.103), channel_id=1, source_target_pairs={{0,64},{64,0},{1,65},{65,1},{2,66},{66,2},{3,67},{67,3},{4,68},{68... | collective-permute-start | bytes 393224 | tf_op jit(solution)/shard_map/ppermute | solution.py:527
  87.3 2.7 %collective-permute-done.27.refs_7_ = bf16[8,64,128]{2,1,0:T(8,128)(2,1)S(1)} collective-permute-done((bf16[8,64,128]{2,1,0:T(8,128)(2,1)S(1)}, bf16[8,64,128]{2,1,0:T(8,128)(2,1)S(1)}, u32[]{:S(2)}, u32[]{:S(2)}) %collective-permute-start.27) | collective-permute-done | bytes 131104 | tf_op jit(solution)/shard_map/ppermute | solution.py:530
  90.1 4.3 %two_layers.11 = (bf16[5,4,64,128]{3,2,1,0:T(8,128)(2,1)S(1)}, bf16[5,4,64,128]{3,2,1,0:T(8,128)(2,1)S(1)}) custom-call(s32[3]{0:T(128)S(1)} %pad_add_fusion.sc.refs_0_, bf16[4,448,768]{2,1,0:T(8,128)(2,1)S(1)} %get-tuple-element.64.refs_2_.refs_1_, bf16[4,192,448]{2,1,0:T(8,128)(2,1)S(1)} %get-tuple-element.65.refs_3_.refs_2_, ...), custom_call_target="tpu_custom_call" | custom-call | tf_op jit(solution)/shard_map/two_layers/pallas_call | solution.py:308
  94.4 2.5 %collective-permute-start.28 = (bf16[5,4,64,128]{3,2,1,0:T(8,128)(2,1)S(1)}, bf16[5,4,64,128]{3,2,1,0:T(8,128)(2,1)S(1)}, u32[]{:S(2)}, u32[]{:S(2)}) collective-permute-start(bf16[5,4,64,128]{3,2,1,0:T(8,128)(2,1)S(1)} %get-tuple-element.108), channel_id=1, source_target_pairs={{0,64},{64,0},{1,65},{65,1},{2,66},{66,2},{3,67},{67,3},{4,68},{68... | collective-permute-start | bytes 983048 | tf_op jit(solution)/shard_map/ppermute | solution.py:527
  102.1 4.3 %collective-permute-done.29.refs_1_ = bf16[5,2,64,128]{3,2,1,0:T(8,128)(2,1)S(1)} collective-permute-done((bf16[5,2,64,128]{3,2,1,0:T(8,128)(2,1)S(1)}, bf16[5,2,64,128]{3,2,1,0:T(8,128)(2,1)S(1)}, u32[]{:S(2)}, u32[]{:S(2)}) %collective-permute-start.29) | collective-permute-done | bytes 163872 | tf_op jit(solution)/shard_map/ppermute | solution.py:534
  106.4 2.2 %collective-permute-done.30.refs_2_ = bf16[5,2,64,128]{3,2,1,0:T(8,128)(2,1)S(1)} collective-permute-done((bf16[5,2,64,128]{3,2,1,0:T(8,128)(2,1)S(1)}, bf16[5,2,64,128]{3,2,1,0:T(8,128)(2,1)S(1)}, u32[]{:S(2)}, u32[]{:S(2)}) %collective-permute-start.30) | collective-permute-done | bytes 163872 | tf_op jit(solution)/shard_map/ppermute | solution.py:534
  (57 shorter events, 34.0 us)
Async XLA Ops:
  0.7 23.3 %collective-permute-start = (bf16[2,448,576]{2,1,0:T(8,128)(2,1)}, bf16[2,448,576]{2,1,0:T(8,128)(2,1)S(1)}, u32[]{:S(2)}, u32[]{:S(2)}) collective-permute-start(bf16[2,448,576]{2,1,0:T(8,128)(2,1)} %bitcast.7), channel_id=1, source_target_pairs={{0,64},{64,0},{1,65},{65,1},{2,66},{66,2},{3,67},{67,3},{4,68},{68... | collective-permute-start | bytes 3096584 | tf_op jit(solution)/shard_map/ppermute | solution.py:527
  3.3 9.1 %collective-permute-start.5 = (bf16[6,2,64,128]{3,2,1,0:T(8,128)(2,1)S(1)}, bf16[6,2,64,128]{3,2,1,0:T(8,128)(2,1)S(1)}, u32[]{:S(2)}, u32[]{:S(2)}) collective-permute-start(bf16[6,2,64,128]{3,2,1,0:T(8,128)(2,1)S(1)} %get-tuple-element.69), channel_id=1, source_target_pairs={{0,1},{1,2},{2,3},{3,0},{4,5},{5,6},{6,7},{7,4},{8,9},{9,10},{10,1... | collective-permute-start | bytes 589832 | tf_op jit(solution)/shard_map/ppermute | solution.py:534
  5.0 12.5 %collective-permute-start.6 = (bf16[6,2,64,128]{3,2,1,0:T(8,128)(2,1)S(1)}, bf16[6,2,64,128]{3,2,1,0:T(8,128)(2,1)S(1)}, u32[]{:S(2)}, u32[]{:S(2)}) collective-permute-start(bf16[6,2,64,128]{3,2,1,0:T(8,128)(2,1)S(1)} %get-tuple-element.70), channel_id=1, source_target_pairs={{0,2},{1,3},{2,0},{3,1},{4,6},{5,7},{6,4},{7,5},{8,10},{9,11},{10,... | collective-permute-start | bytes 589832 | tf_op jit(solution)/shard_map/ppermute | solution.py:534
  8.3 10.1 %collective-permute-start.7 = (bf16[6,2,64,128]{3,2,1,0:T(8,128)(2,1)S(1)}, bf16[6,2,64,128]{3,2,1,0:T(8,128)(2,1)S(1)}, u32[]{:S(2)}, u32[]{:S(2)}) collective-permute-start(bf16[6,2,64,128]{3,2,1,0:T(8,128)(2,1)S(1)} %get-tuple-element.71), channel_id=1, source_target_pairs={{0,3},{1,0},{2,1},{3,2},{4,7},{5,4},{6,5},{7,6},{8,11},{9,8},{10,9... | collective-permute-start | bytes 589832 | tf_op jit(solution)/shard_map/ppermute | solution.py:534
  9.0 9.3 %collective-permute-start.8 = (bf16[6,2,64,128]{3,2,1,0:T(8,128)(2,1)S(1)}, bf16[6,2,64,128]{3,2,1,0:T(8,128)(2,1)S(1)}, u32[]{:S(2)}, u32[]{:S(2)}) collective-permute-start(bf16[6,2,64,128]{3,2,1,0:T(8,128)(2,1)S(1)} %get-tuple-element.68.refs_0_), channel_id=1, source_target_pairs={{0,64},{64,0},{1,65},{65,1},{2,66},{66,2},{3,67},{67,3},{4,68},{68... | collective-permute-start | bytes 589832 | tf_op jit(solution)/shard_map/ppermute | solution.py:527
  12.4 6.5 %collective-permute-start.9 = (bf16[6,2,64,128]{3,2,1,0:T(8,128)(2,1)S(1)}, bf16[6,2,64,128]{3,2,1,0:T(8,128)(2,1)S(1)}, u32[]{:S(2)}, u32[]{:S(2)}) collective-permute-start(bf16[6,2,64,128]{3,2,1,0:T(8,128)(2,1)S(1)} %collective-permute-done.5.refs_1_), channel_id=1, source_target_pairs={{0,64},{64,0},{1,65},{65,1},{2,66},{66,2},{3,67},{67,3},{4,68},{68... | collective-permute-start | bytes 589832 | tf_op jit(solution)/shard_map/ppermute | solution.py:527
  17.5 6.6 %collective-permute-start.1 = (bf16[2,576,256]{2,1,0:T(8,128)(2,1)}, bf16[2,576,256]{2,1,0:T(8,128)(2,1)S(1)}, u32[]{:S(2)}, u32[]{:S(2)}) collective-permute-start(bf16[2,576,256]{2,1,0:T(8,128)(2,1)} %refs_1_.1), channel_id=1, source_target_pairs={{0,64},{64,0},{1,65},{65,1},{2,66},{66,2},{3,67},{67,3},{4,68},{68... | collective-permute-start | bytes 1769480 | tf_op jit(solution)/shard_map/ppermute | solution.py:527
  18.9 5.1 %collective-permute-start.2 = (bf16[2,192,576]{2,1,0:T(8,128)(2,1)}, bf16[2,192,576]{2,1,0:T(8,128)(2,1)S(1)}, u32[]{:S(2)}, u32[]{:S(2)}) collective-permute-start(bf16[2,192,576]{2,1,0:T(8,128)(2,1)} %bitcast.9), channel_id=1, source_target_pairs={{0,64},{64,0},{1,65},{65,1},{2,66},{66,2},{3,67},{67,3},{4,68},{68... | collective-permute-start | bytes 1327112 | tf_op jit(solution)/shard_map/ppermute | solution.py:527
  21.9 6.5 %collective-permute-start.12 = (bf16[18,64,128]{2,1,0:T(8,128)(2,1)S(1)}, bf16[18,64,128]{2,1,0:T(8,128)(2,1)S(1)}, u32[]{:S(2)}, u32[]{:S(2)}) collective-permute-start(bf16[18,64,128]{2,1,0:T(8,128)(2,1)S(1)} %get-tuple-element.72), channel_id=1, source_target_pairs={{64,4},{0,1},{65,5},{1,0},{66,6},{2,3},{67,7},{3,2},{68,8},{4,64},... | collective-permute-start | bytes 884744 | tf_op jit(solution)/shard_map/ppermute | solution.py:530
  23.4 12.2 %collective-permute-start.15 = (bf16[18,64,128]{2,1,0:T(8,128)(2,1)S(1)}, bf16[18,64,128]{2,1,0:T(8,128)(2,1)S(1)}, u32[]{:S(2)}, u32[]{:S(2)}) collective-permute-start(bf16[18,64,128]{2,1,0:T(8,128)(2,1)S(1)} %get-tuple-element.77), channel_id=1, source_target_pairs={{64,4},{0,1},{65,5},{1,0},{66,6},{2,3},{67,7},{3,2},{68,8},{4,64},... | collective-permute-start | bytes 884744 | tf_op jit(solution)/shard_map/ppermute | solution.py:530
  33.4 6.5 %collective-permute-start.14 = (bf16[16,64,128]{2,1,0:T(8,128)(2,1)S(1)}, bf16[16,64,128]{2,1,0:T(8,128)(2,1)S(1)}, u32[]{:S(2)}, u32[]{:S(2)}) collective-permute-start(bf16[16,64,128]{2,1,0:T(8,128)(2,1)S(1)} %get-tuple-element.76), channel_id=1, source_target_pairs={{0,64},{64,0},{1,65},{65,1},{2,66},{66,2},{3,67},{67,3},{4,68},{68... | collective-permute-start | bytes 786440 | tf_op jit(solution)/shard_map/ppermute | solution.py:527
  35.5 4.4 %collective-permute-start.16 = (bf16[8,64,128]{2,1,0:T(8,128)(2,1)S(1)}, bf16[8,64,128]{2,1,0:T(8,128)(2,1)S(1)}, u32[]{:S(2)}, u32[]{:S(2)}) collective-permute-start(bf16[8,64,128]{2,1,0:T(8,128)(2,1)S(1)} %get-tuple-element.80), channel_id=1, source_target_pairs={{64,4},{0,1},{65,5},{1,0},{66,6},{2,3},{67,7},{3,2},{68,8},{4,64},... | collective-permute-start | bytes 393224 | tf_op jit(solution)/shard_map/ppermute | solution.py:530
  44.2 9.3 %collective-permute-start.17 = (bf16[14,64,128]{2,1,0:T(8,128)(2,1)S(1)}, bf16[14,64,128]{2,1,0:T(8,128)(2,1)S(1)}, u32[]{:S(2)}, u32[]{:S(2)}) collective-permute-start(bf16[14,64,128]{2,1,0:T(8,128)(2,1)S(1)} %get-tuple-element.84), channel_id=1, source_target_pairs={{0,64},{64,0},{1,65},{65,1},{2,66},{66,2},{3,67},{67,3},{4,68},{68... | collective-permute-start | bytes 688136 | tf_op jit(solution)/shard_map/ppermute | solution.py:527
  46.7 6.8 %collective-permute-start.18 = (bf16[4,64,128]{2,1,0:T(8,128)(2,1)S(1)}, bf16[4,64,128]{2,1,0:T(8,128)(2,1)S(1)}, u32[]{:S(2)}, u32[]{:S(2)}) collective-permute-start(bf16[4,64,128]{2,1,0:T(8,128)(2,1)S(1)} %get-tuple-element.85), channel_id=1, source_target_pairs={{64,4},{0,1},{65,5},{1,0},{66,6},{2,3},{67,7},{3,2},{68,8},{4,64},... | collective-permute-start | bytes 196616 | tf_op jit(solution)/shard_map/ppermute | solution.py:530
  57.0 9.0 %collective-permute-start.20 = (bf16[16,64,128]{2,1,0:T(8,128)(2,1)S(1)}, bf16[16,64,128]{2,1,0:T(8,128)(2,1)S(1)}, u32[]{:S(2)}, u32[]{:S(2)}) collective-permute-start(bf16[16,64,128]{2,1,0:T(8,128)(2,1)S(1)} %get-tuple-element.90), channel_id=1, source_target_pairs={{0,64},{64,0},{1,65},{65,1},{2,66},{66,2},{3,67},{67,3},{4,68},{68... | collective-permute-start | bytes 786440 | tf_op jit(solution)/shard_map/ppermute | solution.py:527
  59.3 5.0 %collective-permute-start.21 = (bf16[10,64,128]{2,1,0:T(8,128)(2,1)S(1)}, bf16[10,64,128]{2,1,0:T(8,128)(2,1)S(1)}, u32[]{:S(2)}, u32[]{:S(2)}) collective-permute-start(bf16[10,64,128]{2,1,0:T(8,128)(2,1)S(1)} %get-tuple-element.91), channel_id=1, source_target_pairs={{64,4},{0,1},{65,5},{1,0},{66,6},{2,3},{67,7},{3,2},{68,8},{4,64},... | collective-permute-start | bytes 491528 | tf_op jit(solution)/shard_map/ppermute | solution.py:530
  59.3 6.7 %collective-permute-start.22 = (bf16[8,64,128]{2,1,0:T(8,128)(2,1)S(1)}, bf16[8,64,128]{2,1,0:T(8,128)(2,1)S(1)}, u32[]{:S(2)}, u32[]{:S(2)}) collective-permute-start(bf16[8,64,128]{2,1,0:T(8,128)(2,1)S(1)} %get-tuple-element.92), channel_id=1, source_target_pairs={{64,4},{0,1},{65,5},{1,0},{66,6},{2,3},{67,7},{3,2},{68,8},{4,64},... | collective-permute-start | bytes 393224 | tf_op jit(solution)/shard_map/ppermute | solution.py:530
  70.3 9.6 %collective-permute-start.23 = (bf16[14,64,128]{2,1,0:T(8,128)(2,1)S(1)}, bf16[14,64,128]{2,1,0:T(8,128)(2,1)S(1)}, u32[]{:S(2)}, u32[]{:S(2)}) collective-permute-start(bf16[14,64,128]{2,1,0:T(8,128)(2,1)S(1)} %get-tuple-element.96), channel_id=1, source_target_pairs={{0,64},{64,0},{1,65},{65,1},{2,66},{66,2},{3,67},{67,3},{4,68},{68... | collective-permute-start | bytes 688136 | tf_op jit(solution)/shard_map/ppermute | solution.py:527
  73.1 6.8 %collective-permute-start.24 = (bf16[4,64,128]{2,1,0:T(8,128)(2,1)S(1)}, bf16[4,64,128]{2,1,0:T(8,128)(2,1)S(1)}, u32[]{:S(2)}, u32[]{:S(2)}) collective-permute-start(bf16[4,64,128]{2,1,0:T(8,128)(2,1)S(1)} %get-tuple-element.97), channel_id=1, source_target_pairs={{64,4},{0,1},{65,5},{1,0},{66,6},{2,3},{67,7},{3,2},{68,8},{4,64},... | collective-permute-start | bytes 196616 | tf_op jit(solution)/shard_map/ppermute | solution.py:530
  74.9 10.8 %collective-permute-start.25 = (bf16[10,64,128]{2,1,0:T(8,128)(2,1)S(1)}, bf16[10,64,128]{2,1,0:T(8,128)(2,1)S(1)}, u32[]{:S(2)}, u32[]{:S(2)}) collective-permute-start(bf16[10,64,128]{2,1,0:T(8,128)(2,1)S(1)} %get-tuple-element.102), channel_id=1, source_target_pairs={{64,4},{0,1},{65,5},{1,0},{66,6},{2,3},{67,7},{3,2},{68,8},{4,64},... | collective-permute-start | bytes 491528 | tf_op jit(solution)/shard_map/ppermute | solution.py:530
  85.7 4.4 %collective-permute-start.27 = (bf16[8,64,128]{2,1,0:T(8,128)(2,1)S(1)}, bf16[8,64,128]{2,1,0:T(8,128)(2,1)S(1)}, u32[]{:S(2)}, u32[]{:S(2)}) collective-permute-start(bf16[8,64,128]{2,1,0:T(8,128)(2,1)S(1)} %get-tuple-element.104), channel_id=1, source_target_pairs={{64,4},{0,1},{65,5},{1,0},{66,6},{2,3},{67,7},{3,2},{68,8},{4,64},... | collective-permute-start | bytes 393224 | tf_op jit(solution)/shard_map/ppermute | solution.py:530
  99.0 7.3 %collective-permute-start.29 = (bf16[5,2,64,128]{3,2,1,0:T(8,128)(2,1)S(1)}, bf16[5,2,64,128]{3,2,1,0:T(8,128)(2,1)S(1)}, u32[]{:S(2)}, u32[]{:S(2)}) collective-permute-start(bf16[5,2,64,128]{3,2,1,0:T(8,128)(2,1)S(1)} %get-tuple-element.110), channel_id=1, source_target_pairs={{0,1},{1,2},{2,3},{3,0},{4,5},{5,6},{6,7},{7,4},{8,9},{9,10},{10,1... | collective-permute-start | bytes 491528 | tf_op jit(solution)/shard_map/ppermute | solution.py:534
  99.1 9.5 %collective-permute-start.30 = (bf16[5,2,64,128]{3,2,1,0:T(8,128)(2,1)S(1)}, bf16[5,2,64,128]{3,2,1,0:T(8,128)(2,1)S(1)}, u32[]{:S(2)}, u32[]{:S(2)}) collective-permute-start(bf16[5,2,64,128]{3,2,1,0:T(8,128)(2,1)S(1)} %get-tuple-element.111), channel_id=1, source_target_pairs={{0,2},{1,3},{2,0},{3,1},{4,6},{5,7},{6,4},{7,5},{8,10},{9,11},{10,... | collective-permute-start | bytes 491528 | tf_op jit(solution)/shard_map/ppermute | solution.py:534
  101.1 8.4 %collective-permute-start.31 = (bf16[5,2,64,128]{3,2,1,0:T(8,128)(2,1)S(1)}, bf16[5,2,64,128]{3,2,1,0:T(8,128)(2,1)S(1)}, u32[]{:S(2)}, u32[]{:S(2)}) collective-permute-start(bf16[5,2,64,128]{3,2,1,0:T(8,128)(2,1)S(1)} %get-tuple-element.112), channel_id=1, source_target_pairs={{0,3},{1,0},{2,1},{3,2},{4,7},{5,4},{6,5},{7,6},{8,11},{9,8},{10,9... | collective-permute-start | bytes 491528 | tf_op jit(solution)/shard_map/ppermute | solution.py:534
  (8 other events, 25.1 us)

commit v7 on v6

--- a/solution.py
+++ b/solution.py
@@ -542,7 +542,9 @@
     wa, wb, wc, wo = pack_weights(scalars, own_w, other_w)
 
     pieces = cut_state(scalars, frames, hidden_in, cell_in, memory_in)
-    mine = [pieces[0]] + [around(pieces[k], k) for k in (1, 2, 3)]
+    mine = [pieces[0]] + [None] * 3
+    for k in (2, 1, 3):
+        mine[k] = around(pieces[k], k)
     theirs = [to_partner(piece) for piece in mine]
     low_own, high_own, near_a, near_b, message_a, message_b = open_state(scalars, mine, theirs)
     far_a = to_neighbour(message_a)
@@ -623,7 +625,9 @@
 
     taken = to_partner(outs["give"])
     pieces = cut_result(scalars, results[0], results[1], taken)
-    done = [pieces[0]] + [around(pieces[k], k) for k in (1, 2, 3)]
+    done = [pieces[0]] + [None] * 3
+    for k in (2, 1, 3):
+        done[k] = around(pieces[k], k)
     return tuple(close_result(scalars, done))
 
 

time: 112 us -> 112 us (level)
  no operation moved by 1% of the time
where the time goes in v7:
time: 112 us; the launch traced here: 111 us
  Pallas kernels  42.7 us (38%)
  starting transfers between devices  34.9 us (31%)
  waiting for transfers between devices  32.5 us (29%)
    pallas_call x6, Pallas kernels, run_phase(): pl.pallas_call(functools.partial(phase_kernel, plan), out_shape=[jax.Shap...  24.8 us
    ppermute x15, starting transfers between devices, to_partner(): return lax.ppermute(value, 'layer', swap)  18.8 us
    ppermute x11, waiting for transfers between devices, to_neighbour(): return lax.ppermute(value, ('layer', 'rows'), across)  15.2 us
    ppermute x6, waiting for transfers between devices, around(): return lax.ppermute(value, 'rows', turn)  14.5 us
    pallas_call x5, Pallas kernels, run_early(): pl.pallas_call(functools.partial(early_kernel, plan), out_shape=[jax.Shap...  9.71 us
    ppermute x6, starting transfers between devices, around(): return lax.ppermute(value, 'rows', turn)  8.78 us
    ppermute x11, starting transfers between devices, to_neighbour(): return lax.ppermute(value, ('layer', 'rows'), across)  7.36 us
    pallas_call x1, Pallas kernels, pack_weights(): pl.pallas_call(pack_weights_kernel, out_shape=[jax.ShapeDtypeStruct(s, BF...  3.3 us
  transfers between devices with their start and end apart: 32, of which 13 were waited for; matrix products, arithmetic and copies ran while one was open for 0% of the time, Pallas kernels for 22%

profile of v7, /device:TPU:25, one launch (start us, length us, event | category | flops | bytes accessed | tf_op | source)
XLA Modules:
  0.0 111.0 jit_solution(7517043178185530377)
XLA Ops:
  5.0 3.3 %collective-permute-start.6 = (bf16[6,2,64,128]{3,2,1,0:T(8,128)(2,1)S(1)}, bf16[6,2,64,128]{3,2,1,0:T(8,128)(2,1)S(1)}, u32[]{:S(2)}, u32[]{:S(2)}) collective-permute-start(bf16[6,2,64,128]{3,2,1,0:T(8,128)(2,1)S(1)} %get-tuple-element.70), channel_id=1, source_target_pairs={{0,2},{1,3},{2,0},{3,1},{4,6},{5,7},{6,4},{7,5},{8,10},{9,11},{10,... | collective-permute-start | bytes 589832 | tf_op jit(solution)/shard_map/ppermute | solution.py:534
  9.9 2.5 %collective-permute-done.5.refs_1_ = bf16[6,2,64,128]{3,2,1,0:T(8,128)(2,1)S(1)} collective-permute-done((bf16[6,2,64,128]{3,2,1,0:T(8,128)(2,1)S(1)}, bf16[6,2,64,128]{3,2,1,0:T(8,128)(2,1)S(1)}, u32[]{:S(2)}, u32[]{:S(2)}) %collective-permute-start.5) | collective-permute-done | bytes 196640 | tf_op jit(solution)/shard_map/ppermute | solution.py:534
  13.0 4.5 %collective-permute-done.6.refs_2_ = bf16[6,2,64,128]{3,2,1,0:T(8,128)(2,1)S(1)} collective-permute-done((bf16[6,2,64,128]{3,2,1,0:T(8,128)(2,1)S(1)}, bf16[6,2,64,128]{3,2,1,0:T(8,128)(2,1)S(1)}, u32[]{:S(2)}, u32[]{:S(2)}) %collective-permute-start.6) | collective-permute-done | bytes 196640 | tf_op jit(solution)/shard_map/ppermute | solution.py:534
  24.0 3.3 %pack_weights.1 = (bf16[4,256,512]{2,1,0:T(8,128)(2,1)S(1)}, bf16[4,448,768]{2,1,0:T(8,128)(2,1)S(1)}, bf16[4,192,448]{2,1,0:T(8,128)(2,1)S(1)}, bf16[4,256,384]{2,1,0:T(8,128)(2,1)S(1)}) custom-call(s32[3]{0:T(128)S(1)} %pad_add_fusion.sc.refs_0_, bf16[2,448,576]{2,1,0:T(8,128)(2,1)} %bitcast.8, bf16[2,576,256]{2,1,0:T(8,128)(2,1)} %refs_1_.1, ...), custom_call_target="tpu_custom_call" | custom-call | tf_op jit(solution)/shard_map/pack_weights/pallas_call | solution.py:374
  28.5 4.9 %two_layers.6 = (bf16[5,4,64,128]{3,2,1,0:T(8,128)(2,1)S(1)}, bf16[16,64,128]{2,1,0:T(8,128)(2,1)S(1)}, bf16[8,64,128]{2,1,0:T(8,128)(2,1)S(1)}, bf16[8,64,128]{2,1,0:T(8,128)(2,1)S(1)}) custom-call(s32[3]{0:T(128)S(1)} %pad_add_fusion.sc.refs_0_, bf16[4,256,512]{2,1,0:T(8,128)(2,1)S(1)} %get-tuple-element.67.refs_1_, ...), custom_call_target="tpu_custom_call" | custom-call | tf_op jit(solution)/shard_map/two_layers/pallas_call | solution.py:308
  37.2 2.8 %collective-permute-done.16.refs_8_ = bf16[8,64,128]{2,1,0:T(8,128)(2,1)S(1)} collective-permute-done((bf16[8,64,128]{2,1,0:T(8,128)(2,1)S(1)}, bf16[8,64,128]{2,1,0:T(8,128)(2,1)S(1)}, u32[]{:S(2)}, u32[]{:S(2)}) %collective-permute-start.16) | collective-permute-done | bytes 131104 | tf_op jit(solution)/shard_map/ppermute | solution.py:530
  39.9 4.3 %two_layers.7 = (bf16[5,4,64,128]{3,2,1,0:T(8,128)(2,1)S(1)}, bf16[14,64,128]{2,1,0:T(8,128)(2,1)S(1)}, bf16[4,64,128]{2,1,0:T(8,128)(2,1)S(1)}, bf16[10,64,128]{2,1,0:T(8,128)(2,1)S(1)}) custom-call(s32[3]{0:T(128)S(1)} %pad_add_fusion.sc.refs_0_, bf16[4,448,768]{2,1,0:T(8,128)(2,1)S(1)} %get-tuple-element.64.refs_2_.refs_1_, ...), custom_call_target="tpu_custom_call" | custom-call | tf_op jit(solution)/shard_map/two_layers/pallas_call | solution.py:308
  44.2 2.5 %collective-permute-start.17 = (bf16[14,64,128]{2,1,0:T(8,128)(2,1)S(1)}, bf16[14,64,128]{2,1,0:T(8,128)(2,1)S(1)}, u32[]{:S(2)}, u32[]{:S(2)}) collective-permute-start(bf16[14,64,128]{2,1,0:T(8,128)(2,1)S(1)} %get-tuple-element.84), channel_id=1, source_target_pairs={{0,64},{64,0},{1,65},{65,1},{2,66},{66,2},{3,67},{67,3},{4,68},{68... | collective-permute-start | bytes 688136 | tf_op jit(solution)/shard_map/ppermute | solution.py:527
  48.4 2.6 %collective-permute-done.13.refs_4_ = bf16[8,64,128]{2,1,0:T(8,128)(2,1)S(1)} collective-permute-done((bf16[8,64,128]{2,1,0:T(8,128)(2,1)S(1)}, bf16[8,64,128]{2,1,0:T(8,128)(2,1)S(1)}, u32[]{:S(2)}, u32[]{:S(2)}) %collective-permute-start.13) | collective-permute-done | bytes 131104 | tf_op jit(solution)/shard_map/ppermute | solution.py:530
  51.1 2.4 %early_sums.6 = (f32[5,448,256]{2,1,0:T(8,128)S(1)}, f32[3,256,256]{2,1,0:T(8,128)S(1)}) custom-call(s32[3]{0:T(128)S(1)} %pad_add_fusion.sc.refs_0_, bf16[4,256,512]{2,1,0:T(8,128)(2,1)S(1)} %get-tuple-element.67.refs_1_, bf16[4,448,768]{2,1,0:T(8,128)(2,1)S(1)} %get-tuple-element.64.refs_2_.refs_1_, ...), custom_call_target="tpu_custom_call" | custom-call | tf_op jit(solution)/shard_map/early_sums/pallas_call | solution.py:272
  53.5 3.5 %two_layers.8 = (bf16[5,4,64,128]{3,2,1,0:T(8,128)(2,1)S(1)}, bf16[16,64,128]{2,1,0:T(8,128)(2,1)S(1)}, bf16[8,64,128]{2,1,0:T(8,128)(2,1)S(1)}, bf16[8,64,128]{2,1,0:T(8,128)(2,1)S(1)}) custom-call(s32[3]{0:T(128)S(1)} %pad_add_fusion.sc.refs_0_, bf16[4,448,768]{2,1,0:T(8,128)(2,1)S(1)} %get-tuple-element.64.refs_2_.refs_1_, ...), custom_call_target="tpu_custom_call" | custom-call | tf_op jit(solution)/shard_map/two_layers/pallas_call | solution.py:308
  57.0 2.3 %collective-permute-start.20 = (bf16[16,64,128]{2,1,0:T(8,128)(2,1)S(1)}, bf16[16,64,128]{2,1,0:T(8,128)(2,1)S(1)}, u32[]{:S(2)}, u32[]{:S(2)}) collective-permute-start(bf16[16,64,128]{2,1,0:T(8,128)(2,1)S(1)} %get-tuple-element.90), channel_id=1, source_target_pairs={{0,64},{64,0},{1,65},{65,1},{2,66},{66,2},{3,67},{67,3},{4,68},{68... | collective-permute-start | bytes 786440 | tf_op jit(solution)/shard_map/ppermute | solution.py:527
  61.1 3.3 %collective-permute-done.21.refs_3_.refs_4_ = bf16[10,64,128]{2,1,0:T(8,128)(2,1)S(1)} collective-permute-done((bf16[10,64,128]{2,1,0:T(8,128)(2,1)S(1)}, bf16[10,64,128]{2,1,0:T(8,128)(2,1)S(1)}, u32[]{:S(2)}, u32[]{:S(2)}) %collective-permute-start.21) | collective-permute-done | bytes 163872 | tf_op jit(solution)/shard_map/ppermute | solution.py:530
  66.0 4.3 %two_layers.9 = (bf16[5,4,64,128]{3,2,1,0:T(8,128)(2,1)S(1)}, bf16[14,64,128]{2,1,0:T(8,128)(2,1)S(1)}, bf16[4,64,128]{2,1,0:T(8,128)(2,1)S(1)}, bf16[10,64,128]{2,1,0:T(8,128)(2,1)S(1)}) custom-call(s32[3]{0:T(128)S(1)} %pad_add_fusion.sc.refs_0_, bf16[4,448,768]{2,1,0:T(8,128)(2,1)S(1)} %get-tuple-element.64.refs_2_.refs_1_, ...), custom_call_target="tpu_custom_call" | custom-call | tf_op jit(solution)/shard_map/two_layers/pallas_call | solution.py:308
  70.3 2.8 %collective-permute-start.23 = (bf16[14,64,128]{2,1,0:T(8,128)(2,1)S(1)}, bf16[14,64,128]{2,1,0:T(8,128)(2,1)S(1)}, u32[]{:S(2)}, u32[]{:S(2)}) collective-permute-start(bf16[14,64,128]{2,1,0:T(8,128)(2,1)S(1)} %get-tuple-element.96), channel_id=1, source_target_pairs={{0,64},{64,0},{1,65},{65,1},{2,66},{66,2},{3,67},{67,3},{4,68},{68... | collective-permute-start | bytes 688136 | tf_op jit(solution)/shard_map/ppermute | solution.py:527
  74.9 2.6 %collective-permute-done.19.refs_4_ = bf16[8,64,128]{2,1,0:T(8,128)(2,1)S(1)} collective-permute-done((bf16[8,64,128]{2,1,0:T(8,128)(2,1)S(1)}, bf16[8,64,128]{2,1,0:T(8,128)(2,1)S(1)}, u32[]{:S(2)}, u32[]{:S(2)}) %collective-permute-start.19) | collective-permute-done | bytes 131104 | tf_op jit(solution)/shard_map/ppermute | solution.py:530
  77.5 2.4 %early_sums.8 = (f32[5,448,256]{2,1,0:T(8,128)S(1)}, f32[3,256,256]{2,1,0:T(8,128)S(1)}) custom-call(s32[3]{0:T(128)S(1)} %pad_add_fusion.sc.refs_0_, bf16[4,256,512]{2,1,0:T(8,128)(2,1)S(1)} %get-tuple-element.67.refs_1_, bf16[4,448,768]{2,1,0:T(8,128)(2,1)S(1)} %get-tuple-element.64.refs_2_.refs_1_, ...), custom_call_target="tpu_custom_call" | custom-call | tf_op jit(solution)/shard_map/early_sums/pallas_call | solution.py:272
  80.0 3.5 %two_layers.10 = (bf16[5,4,64,128]{3,2,1,0:T(8,128)(2,1)S(1)}, bf16[8,64,128]{2,1,0:T(8,128)(2,1)S(1)}, bf16[8,64,128]{2,1,0:T(8,128)(2,1)S(1)}) custom-call(s32[3]{0:T(128)S(1)} %pad_add_fusion.sc.refs_0_, bf16[4,448,768]{2,1,0:T(8,128)(2,1)S(1)} %get-tuple-element.64.refs_2_.refs_1_, bf16[4,192,448]{2,1,0:T(8,128)(2,1)S(1)} %get-tuple-element.65.refs_3_.refs_2_, ...), custom_call_target="tpu_custom_call" | custom-call | tf_op jit(solution)/shard_map/two_layers/pallas_call | solution.py:308
  83.4 2.3 %collective-permute-start.26 = (bf16[8,64,128]{2,1,0:T(8,128)(2,1)S(1)}, bf16[8,64,128]{2,1,0:T(8,128)(2,1)S(1)}, u32[]{:S(2)}, u32[]{:S(2)}) collective-permute-start(bf16[8,64,128]{2,1,0:T(8,128)(2,1)S(1)} %get-tuple-element.103), channel_id=1, source_target_pairs={{0,64},{64,0},{1,65},{65,1},{2,66},{66,2},{3,67},{67,3},{4,68},{68... | collective-permute-start | bytes 393224 | tf_op jit(solution)/shard_map/ppermute | solution.py:527
  87.3 2.7 %collective-permute-done.27.refs_7_ = bf16[8,64,128]{2,1,0:T(8,128)(2,1)S(1)} collective-permute-done((bf16[8,64,128]{2,1,0:T(8,128)(2,1)S(1)}, bf16[8,64,128]{2,1,0:T(8,128)(2,1)S(1)}, u32[]{:S(2)}, u32[]{:S(2)}) %collective-permute-start.27) | collective-permute-done | bytes 131104 | tf_op jit(solution)/shard_map/ppermute | solution.py:530
  90.1 4.3 %two_layers.11 = (bf16[5,4,64,128]{3,2,1,0:T(8,128)(2,1)S(1)}, bf16[5,4,64,128]{3,2,1,0:T(8,128)(2,1)S(1)}) custom-call(s32[3]{0:T(128)S(1)} %pad_add_fusion.sc.refs_0_, bf16[4,448,768]{2,1,0:T(8,128)(2,1)S(1)} %get-tuple-element.64.refs_2_.refs_1_, bf16[4,192,448]{2,1,0:T(8,128)(2,1)S(1)} %get-tuple-element.65.refs_3_.refs_2_, ...), custom_call_target="tpu_custom_call" | custom-call | tf_op jit(solution)/shard_map/two_layers/pallas_call | solution.py:308
  94.4 2.5 %collective-permute-start.28 = (bf16[5,4,64,128]{3,2,1,0:T(8,128)(2,1)S(1)}, bf16[5,4,64,128]{3,2,1,0:T(8,128)(2,1)S(1)}, u32[]{:S(2)}, u32[]{:S(2)}) collective-permute-start(bf16[5,4,64,128]{3,2,1,0:T(8,128)(2,1)S(1)} %get-tuple-element.108), channel_id=1, source_target_pairs={{0,64},{64,0},{1,65},{65,1},{2,66},{66,2},{3,67},{67,3},{4,68},{68... | collective-permute-start | bytes 983048 | tf_op jit(solution)/shard_map/ppermute | solution.py:527
  102.1 4.3 %collective-permute-done.29.refs_1_ = bf16[5,2,64,128]{3,2,1,0:T(8,128)(2,1)S(1)} collective-permute-done((bf16[5,2,64,128]{3,2,1,0:T(8,128)(2,1)S(1)}, bf16[5,2,64,128]{3,2,1,0:T(8,128)(2,1)S(1)}, u32[]{:S(2)}, u32[]{:S(2)}) %collective-permute-start.29) | collective-permute-done | bytes 163872 | tf_op jit(solution)/shard_map/ppermute | solution.py:534
  106.4 2.2 %collective-permute-done.30.refs_2_ = bf16[5,2,64,128]{3,2,1,0:T(8,128)(2,1)S(1)} collective-permute-done((bf16[5,2,64,128]{3,2,1,0:T(8,128)(2,1)S(1)}, bf16[5,2,64,128]{3,2,1,0:T(8,128)(2,1)S(1)}, u32[]{:S(2)}, u32[]{:S(2)}) %collective-permute-start.30) | collective-permute-done | bytes 163872 | tf_op jit(solution)/shard_map/ppermute | solution.py:534
  (57 shorter events, 34.0 us)
Async XLA Ops:
  0.7 23.3 %collective-permute-start = (bf16[2,448,576]{2,1,0:T(8,128)(2,1)}, bf16[2,448,576]{2,1,0:T(8,128)(2,1)S(1)}, u32[]{:S(2)}, u32[]{:S(2)}) collective-permute-start(bf16[2,448,576]{2,1,0:T(8,128)(2,1)} %bitcast.7), channel_id=1, source_target_pairs={{0,64},{64,0},{1,65},{65,1},{2,66},{66,2},{3,67},{67,3},{4,68},{68... | collective-permute-start | bytes 3096584 | tf_op jit(solution)/shard_map/ppermute | solution.py:527
  3.3 9.1 %collective-permute-start.5 = (bf16[6,2,64,128]{3,2,1,0:T(8,128)(2,1)S(1)}, bf16[6,2,64,128]{3,2,1,0:T(8,128)(2,1)S(1)}, u32[]{:S(2)}, u32[]{:S(2)}) collective-permute-start(bf16[6,2,64,128]{3,2,1,0:T(8,128)(2,1)S(1)} %get-tuple-element.69), channel_id=1, source_target_pairs={{0,1},{1,2},{2,3},{3,0},{4,5},{5,6},{6,7},{7,4},{8,9},{9,10},{10,1... | collective-permute-start | bytes 589832 | tf_op jit(solution)/shard_map/ppermute | solution.py:534
  5.0 12.5 %collective-permute-start.6 = (bf16[6,2,64,128]{3,2,1,0:T(8,128)(2,1)S(1)}, bf16[6,2,64,128]{3,2,1,0:T(8,128)(2,1)S(1)}, u32[]{:S(2)}, u32[]{:S(2)}) collective-permute-start(bf16[6,2,64,128]{3,2,1,0:T(8,128)(2,1)S(1)} %get-tuple-element.70), channel_id=1, source_target_pairs={{0,2},{1,3},{2,0},{3,1},{4,6},{5,7},{6,4},{7,5},{8,10},{9,11},{10,... | collective-permute-start | bytes 589832 | tf_op jit(solution)/shard_map/ppermute | solution.py:534
  8.3 10.1 %collective-permute-start.7 = (bf16[6,2,64,128]{3,2,1,0:T(8,128)(2,1)S(1)}, bf16[6,2,64,128]{3,2,1,0:T(8,128)(2,1)S(1)}, u32[]{:S(2)}, u32[]{:S(2)}) collective-permute-start(bf16[6,2,64,128]{3,2,1,0:T(8,128)(2,1)S(1)} %get-tuple-element.71), channel_id=1, source_target_pairs={{0,3},{1,0},{2,1},{3,2},{4,7},{5,4},{6,5},{7,6},{8,11},{9,8},{10,9... | collective-permute-start | bytes 589832 | tf_op jit(solution)/shard_map/ppermute | solution.py:534
  9.0 9.3 %collective-permute-start.8 = (bf16[6,2,64,128]{3,2,1,0:T(8,128)(2,1)S(1)}, bf16[6,2,64,128]{3,2,1,0:T(8,128)(2,1)S(1)}, u32[]{:S(2)}, u32[]{:S(2)}) collective-permute-start(bf16[6,2,64,128]{3,2,1,0:T(8,128)(2,1)S(1)} %get-tuple-element.68.refs_0_), channel_id=1, source_target_pairs={{0,64},{64,0},{1,65},{65,1},{2,66},{66,2},{3,67},{67,3},{4,68},{68... | collective-permute-start | bytes 589832 | tf_op jit(solution)/shard_map/ppermute | solution.py:527
  12.4 6.5 %collective-permute-start.9 = (bf16[6,2,64,128]{3,2,1,0:T(8,128)(2,1)S(1)}, bf16[6,2,64,128]{3,2,1,0:T(8,128)(2,1)S(1)}, u32[]{:S(2)}, u32[]{:S(2)}) collective-permute-start(bf16[6,2,64,128]{3,2,1,0:T(8,128)(2,1)S(1)} %collective-permute-done.5.refs_1_), channel_id=1, source_target_pairs={{0,64},{64,0},{1,65},{65,1},{2,66},{66,2},{3,67},{67,3},{4,68},{68... | collective-permute-start | bytes 589832 | tf_op jit(solution)/shard_map/ppermute | solution.py:527
  17.5 6.6 %collective-permute-start.1 = (bf16[2,576,256]{2,1,0:T(8,128)(2,1)}, bf16[2,576,256]{2,1,0:T(8,128)(2,1)S(1)}, u32[]{:S(2)}, u32[]{:S(2)}) collective-permute-start(bf16[2,576,256]{2,1,0:T(8,128)(2,1)} %refs_1_.1), channel_id=1, source_target_pairs={{0,64},{64,0},{1,65},{65,1},{2,66},{66,2},{3,67},{67,3},{4,68},{68... | collective-permute-start | bytes 1769480 | tf_op jit(solution)/shard_map/ppermute | solution.py:527
  18.9 5.1 %collective-permute-start.2 = (bf16[2,192,576]{2,1,0:T(8,128)(2,1)}, bf16[2,192,576]{2,1,0:T(8,128)(2,1)S(1)}, u32[]{:S(2)}, u32[]{:S(2)}) collective-permute-start(bf16[2,192,576]{2,1,0:T(8,128)(2,1)} %bitcast.9), channel_id=1, source_target_pairs={{0,64},{64,0},{1,65},{65,1},{2,66},{66,2},{3,67},{67,3},{4,68},{68... | collective-permute-start | bytes 1327112 | tf_op jit(solution)/shard_map/ppermute | solution.py:527
  21.9 6.5 %collective-permute-start.12 = (bf16[18,64,128]{2,1,0:T(8,128)(2,1)S(1)}, bf16[18,64,128]{2,1,0:T(8,128)(2,1)S(1)}, u32[]{:S(2)}, u32[]{:S(2)}) collective-permute-start(bf16[18,64,128]{2,1,0:T(8,128)(2,1)S(1)} %get-tuple-element.72), channel_id=1, source_target_pairs={{64,4},{0,1},{65,5},{1,0},{66,6},{2,3},{67,7},{3,2},{68,8},{4,64},... | collective-permute-start | bytes 884744 | tf_op jit(solution)/shard_map/ppermute | solution.py:530
  23.4 12.2 %collective-permute-start.15 = (bf16[18,64,128]{2,1,0:T(8,128)(2,1)S(1)}, bf16[18,64,128]{2,1,0:T(8,128)(2,1)S(1)}, u32[]{:S(2)}, u32[]{:S(2)}) collective-permute-start(bf16[18,64,128]{2,1,0:T(8,128)(2,1)S(1)} %get-tuple-element.77), channel_id=1, source_target_pairs={{64,4},{0,1},{65,5},{1,0},{66,6},{2,3},{67,7},{3,2},{68,8},{4,64},... | collective-permute-start | bytes 884744 | tf_op jit(solution)/shard_map/ppermute | solution.py:530
  33.4 6.5 %collective-permute-start.14 = (bf16[16,64,128]{2,1,0:T(8,128)(2,1)S(1)}, bf16[16,64,128]{2,1,0:T(8,128)(2,1)S(1)}, u32[]{:S(2)}, u32[]{:S(2)}) collective-permute-start(bf16[16,64,128]{2,1,0:T(8,128)(2,1)S(1)} %get-tuple-element.76), channel_id=1, source_target_pairs={{0,64},{64,0},{1,65},{65,1},{2,66},{66,2},{3,67},{67,3},{4,68},{68... | collective-permute-start | bytes 786440 | tf_op jit(solution)/shard_map/ppermute | solution.py:527
  35.5 4.4 %collective-permute-start.16 = (bf16[8,64,128]{2,1,0:T(8,128)(2,1)S(1)}, bf16[8,64,128]{2,1,0:T(8,128)(2,1)S(1)}, u32[]{:S(2)}, u32[]{:S(2)}) collective-permute-start(bf16[8,64,128]{2,1,0:T(8,128)(2,1)S(1)} %get-tuple-element.80), channel_id=1, source_target_pairs={{64,4},{0,1},{65,5},{1,0},{66,6},{2,3},{67,7},{3,2},{68,8},{4,64},... | collective-permute-start | bytes 393224 | tf_op jit(solution)/shard_map/ppermute | solution.py:530
  44.2 9.3 %collective-permute-start.17 = (bf16[14,64,128]{2,1,0:T(8,128)(2,1)S(1)}, bf16[14,64,128]{2,1,0:T(8,128)(2,1)S(1)}, u32[]{:S(2)}, u32[]{:S(2)}) collective-permute-start(bf16[14,64,128]{2,1,0:T(8,128)(2,1)S(1)} %get-tuple-element.84), channel_id=1, source_target_pairs={{0,64},{64,0},{1,65},{65,1},{2,66},{66,2},{3,67},{67,3},{4,68},{68... | collective-permute-start | bytes 688136 | tf_op jit(solution)/shard_map/ppermute | solution.py:527
  46.7 6.8 %collective-permute-start.18 = (bf16[4,64,128]{2,1,0:T(8,128)(2,1)S(1)}, bf16[4,64,128]{2,1,0:T(8,128)(2,1)S(1)}, u32[]{:S(2)}, u32[]{:S(2)}) collective-permute-start(bf16[4,64,128]{2,1,0:T(8,128)(2,1)S(1)} %get-tuple-element.85), channel_id=1, source_target_pairs={{64,4},{0,1},{65,5},{1,0},{66,6},{2,3},{67,7},{3,2},{68,8},{4,64},... | collective-permute-start | bytes 196616 | tf_op jit(solution)/shard_map/ppermute | solution.py:530
  57.0 9.0 %collective-permute-start.20 = (bf16[16,64,128]{2,1,0:T(8,128)(2,1)S(1)}, bf16[16,64,128]{2,1,0:T(8,128)(2,1)S(1)}, u32[]{:S(2)}, u32[]{:S(2)}) collective-permute-start(bf16[16,64,128]{2,1,0:T(8,128)(2,1)S(1)} %get-tuple-element.90), channel_id=1, source_target_pairs={{0,64},{64,0},{1,65},{65,1},{2,66},{66,2},{3,67},{67,3},{4,68},{68... | collective-permute-start | bytes 786440 | tf_op jit(solution)/shard_map/ppermute | solution.py:527
  59.3 5.0 %collective-permute-start.21 = (bf16[10,64,128]{2,1,0:T(8,128)(2,1)S(1)}, bf16[10,64,128]{2,1,0:T(8,128)(2,1)S(1)}, u32[]{:S(2)}, u32[]{:S(2)}) collective-permute-start(bf16[10,64,128]{2,1,0:T(8,128)(2,1)S(1)} %get-tuple-element.91), channel_id=1, source_target_pairs={{64,4},{0,1},{65,5},{1,0},{66,6},{2,3},{67,7},{3,2},{68,8},{4,64},... | collective-permute-start | bytes 491528 | tf_op jit(solution)/shard_map/ppermute | solution.py:530
  59.3 6.7 %collective-permute-start.22 = (bf16[8,64,128]{2,1,0:T(8,128)(2,1)S(1)}, bf16[8,64,128]{2,1,0:T(8,128)(2,1)S(1)}, u32[]{:S(2)}, u32[]{:S(2)}) collective-permute-start(bf16[8,64,128]{2,1,0:T(8,128)(2,1)S(1)} %get-tuple-element.92), channel_id=1, source_target_pairs={{64,4},{0,1},{65,5},{1,0},{66,6},{2,3},{67,7},{3,2},{68,8},{4,64},... | collective-permute-start | bytes 393224 | tf_op jit(solution)/shard_map/ppermute | solution.py:530
  70.3 9.6 %collective-permute-start.23 = (bf16[14,64,128]{2,1,0:T(8,128)(2,1)S(1)}, bf16[14,64,128]{2,1,0:T(8,128)(2,1)S(1)}, u32[]{:S(2)}, u32[]{:S(2)}) collective-permute-start(bf16[14,64,128]{2,1,0:T(8,128)(2,1)S(1)} %get-tuple-element.96), channel_id=1, source_target_pairs={{0,64},{64,0},{1,65},{65,1},{2,66},{66,2},{3,67},{67,3},{4,68},{68... | collective-permute-start | bytes 688136 | tf_op jit(solution)/shard_map/ppermute | solution.py:527
  73.1 6.8 %collective-permute-start.24 = (bf16[4,64,128]{2,1,0:T(8,128)(2,1)S(1)}, bf16[4,64,128]{2,1,0:T(8,128)(2,1)S(1)}, u32[]{:S(2)}, u32[]{:S(2)}) collective-permute-start(bf16[4,64,128]{2,1,0:T(8,128)(2,1)S(1)} %get-tuple-element.97), channel_id=1, source_target_pairs={{64,4},{0,1},{65,5},{1,0},{66,6},{2,3},{67,7},{3,2},{68,8},{4,64},... | collective-permute-start | bytes 196616 | tf_op jit(solution)/shard_map/ppermute | solution.py:530
  74.9 10.8 %collective-permute-start.25 = (bf16[10,64,128]{2,1,0:T(8,128)(2,1)S(1)}, bf16[10,64,128]{2,1,0:T(8,128)(2,1)S(1)}, u32[]{:S(2)}, u32[]{:S(2)}) collective-permute-start(bf16[10,64,128]{2,1,0:T(8,128)(2,1)S(1)} %get-tuple-element.102), channel_id=1, source_target_pairs={{64,4},{0,1},{65,5},{1,0},{66,6},{2,3},{67,7},{3,2},{68,8},{4,64},... | collective-permute-start | bytes 491528 | tf_op jit(solution)/shard_map/ppermute | solution.py:530
  85.7 4.4 %collective-permute-start.27 = (bf16[8,64,128]{2,1,0:T(8,128)(2,1)S(1)}, bf16[8,64,128]{2,1,0:T(8,128)(2,1)S(1)}, u32[]{:S(2)}, u32[]{:S(2)}) collective-permute-start(bf16[8,64,128]{2,1,0:T(8,128)(2,1)S(1)} %get-tuple-element.104), channel_id=1, source_target_pairs={{64,4},{0,1},{65,5},{1,0},{66,6},{2,3},{67,7},{3,2},{68,8},{4,64},... | collective-permute-start | bytes 393224 | tf_op jit(solution)/shard_map/ppermute | solution.py:530
  99.0 7.3 %collective-permute-start.29 = (bf16[5,2,64,128]{3,2,1,0:T(8,128)(2,1)S(1)}, bf16[5,2,64,128]{3,2,1,0:T(8,128)(2,1)S(1)}, u32[]{:S(2)}, u32[]{:S(2)}) collective-permute-start(bf16[5,2,64,128]{3,2,1,0:T(8,128)(2,1)S(1)} %get-tuple-element.110), channel_id=1, source_target_pairs={{0,1},{1,2},{2,3},{3,0},{4,5},{5,6},{6,7},{7,4},{8,9},{9,10},{10,1... | collective-permute-start | bytes 491528 | tf_op jit(solution)/shard_map/ppermute | solution.py:534
  99.1 9.5 %collective-permute-start.30 = (bf16[5,2,64,128]{3,2,1,0:T(8,128)(2,1)S(1)}, bf16[5,2,64,128]{3,2,1,0:T(8,128)(2,1)S(1)}, u32[]{:S(2)}, u32[]{:S(2)}) collective-permute-start(bf16[5,2,64,128]{3,2,1,0:T(8,128)(2,1)S(1)} %get-tuple-element.111), channel_id=1, source_target_pairs={{0,2},{1,3},{2,0},{3,1},{4,6},{5,7},{6,4},{7,5},{8,10},{9,11},{10,... | collective-permute-start | bytes 491528 | tf_op jit(solution)/shard_map/ppermute | solution.py:534
  101.1 8.4 %collective-permute-start.31 = (bf16[5,2,64,128]{3,2,1,0:T(8,128)(2,1)S(1)}, bf16[5,2,64,128]{3,2,1,0:T(8,128)(2,1)S(1)}, u32[]{:S(2)}, u32[]{:S(2)}) collective-permute-start(bf16[5,2,64,128]{3,2,1,0:T(8,128)(2,1)S(1)} %get-tuple-element.112), channel_id=1, source_target_pairs={{0,3},{1,0},{2,1},{3,2},{4,7},{5,4},{6,5},{7,6},{8,11},{9,8},{10,9... | collective-permute-start | bytes 491528 | tf_op jit(solution)/shard_map/ppermute | solution.py:534
  (8 other events, 25.1 us)

commit v8 on v7

--- a/solution.py
+++ b/solution.py
@@ -8,6 +8,7 @@
 from jax.sharding import PartitionSpec as P
 
 
+LAYER, ROWS = "layer", "rows"
 CH = 64
 GW = 128
 OWN = 4
@@ -95,7 +96,7 @@
                 buf[i] = taps_of(fetch(field, i - reach))
 
     for index in range(2):
-        layer = plan["layer"] + index
+        layer = plan["base"] + index
         for q in range(0, OWN + 2 * REACH[index], 2):
             with_x = half == 0 and index == 0
             fill((th, th2)[index], ("HB", "HT")[index], REACH[index] + 1, q + 4)
@@ -142,7 +143,7 @@
 
     def matmuls(index, q):
         bx, bh, bm, _, _ = bufs[index]
-        layer = plan["layer"] + index
+        layer = plan["base"] + index
         add = lambda w, rhs: jnp.dot(w, rhs, preferred_element_type=F32)
         if index == 0:
             fill(tm, "m", "M", 4, q + 4)
@@ -204,7 +205,7 @@
                 )
             )
         y_buf[:, lanes] = jnp.dot(
-            ref["wo"][plan["layer"] + index],
+            ref["wo"][plan["base"] + index],
             jnp.concatenate(blocks, axis=1),
             preferred_element_type=F32,
         )
@@ -514,9 +515,9 @@
 
 
 def program(frames, hidden_in, cell_in, memory_in, w_x, w_h, w_m, w_o, w_last):
-    core = lax.axis_index("layer")
-    chip = lax.axis_index("rows")
-    chips = lax.axis_size("rows")
+    core = lax.axis_index(LAYER)
+    chip = lax.axis_index(ROWS)
+    chips = lax.axis_size(ROWS)
     swap = [(0, 1), (1, 0)]
     across = []
     for i in range(chips):
@@ -524,14 +525,14 @@
         across.append((i, chips + i - 4 if i >= 4 else i ^ 1))
 
     def to_partner(value):
-        return lax.ppermute(value, "layer", swap)
+        return lax.ppermute(value, LAYER, swap)
 
     def to_neighbour(value):
-        return lax.ppermute(value, ("layer", "rows"), across)
+        return lax.ppermute(value, (LAYER, ROWS), across)
 
     def around(value, k):
         turn = [(i, 4 * (i // 4) + (i + k) % 4) for i in range(chips)]
-        return lax.ppermute(value, "rows", turn)
+        return lax.ppermute(value, ROWS, turn)
 
     scalars = jnp.stack([core, 8 * (chip // 4) + 4 * core, chip % 4]).astype(jnp.int32)
     turned = [jnp.swapaxes(w, 1, 2) for w in (w_x, w_m, w_o, w_last)]
@@ -588,7 +589,7 @@
                 operands.update({name: arrays[name] for name in sorted(needed)})
                 return used, operands
 
-            plan = {"half": half, "layer": 2 * half, "send": send, "early": early}
+            plan = {"half": half, "base": 2 * half, "send": send, "early": early}
             if early:
                 used, operands = gather(ahead, ("wa", "wb"))
                 sums = run_early(operands, dict(plan, fields=used))
@@ -636,20 +637,20 @@
         program,
         mesh=mesh,
         in_specs=(
-            P(None, None, "rows", None, None),
-            P("layer", None, "rows", None, None),
-            P("layer", None, "rows", None, None),
-            P(None, "rows", None, None),
-            P("layer", None, None),
-            P("layer", None, None),
-            P("layer", None, None),
-            P("layer", None, None),
-            P("layer", None, None),
+            P(None, None, ROWS, None, None),
+            P(LAYER, None, ROWS, None, None),
+            P(LAYER, None, ROWS, None, None),
+            P(None, ROWS, None, None),
+            P(LAYER, None, None),
+            P(LAYER, None, None),
+            P(LAYER, None, None),
+            P(LAYER, None, None),
+            P(LAYER, None, None),
         ),
         out_specs=(
-            P("layer", None, "rows", None, None),
-            P("layer", None, "rows", None, None),
-            P("layer", None, "rows", None, None),
+            P(LAYER, None, ROWS, None, None),
+            P(LAYER, None, ROWS, None, None),
+            P(LAYER, None, ROWS, None, None),
         ),
         check_vma=False,
     )

time: 112 us -> 112 us (level)
  no operation moved by 1% of the time
where the time goes in v8:
time: 112 us; the launch traced here: 111 us
  Pallas kernels  42.7 us (38%)
  starting transfers between devices  34.9 us (31%)
  waiting for transfers between devices  32.5 us (29%)
    pallas_call x6, Pallas kernels, run_phase(): pl.pallas_call(functools.partial(phase_kernel, plan), out_shape=[jax.Shap...  24.8 us
    ppermute x15, starting transfers between devices, to_partner(): return lax.ppermute(value, LAYER, swap)  18.8 us
    ppermute x11, waiting for transfers between devices, to_neighbour(): return lax.ppermute(value, (LAYER, ROWS), across)  15.2 us
    ppermute x6, waiting for transfers between devices, around(): return lax.ppermute(value, ROWS, turn)  14.5 us
    pallas_call x5, Pallas kernels, run_early(): pl.pallas_call(functools.partial(early_kernel, plan), out_shape=[jax.Shap...  9.71 us
    ppermute x6, starting transfers between devices, around(): return lax.ppermute(value, ROWS, turn)  8.78 us
    ppermute x11, starting transfers between devices, to_neighbour(): return lax.ppermute(value, (LAYER, ROWS), across)  7.36 us
    pallas_call x1, Pallas kernels, pack_weights(): pl.pallas_call(pack_weights_kernel, out_shape=[jax.ShapeDtypeStruct(s, BF...  3.3 us
  transfers between devices with their start and end apart: 32, of which 13 were waited for; matrix products, arithmetic and copies ran while one was open for 0% of the time, Pallas kernels for 22%

profile of v8, /device:TPU:25, one launch (start us, length us, event | category | flops | bytes accessed | tf_op | source)
XLA Modules:
  0.0 111.0 jit_solution(7517043178185530377)
XLA Ops:
  5.0 3.3 %collective-permute-start.6 = (bf16[6,2,64,128]{3,2,1,0:T(8,128)(2,1)S(1)}, bf16[6,2,64,128]{3,2,1,0:T(8,128)(2,1)S(1)}, u32[]{:S(2)}, u32[]{:S(2)}) collective-permute-start(bf16[6,2,64,128]{3,2,1,0:T(8,128)(2,1)S(1)} %get-tuple-element.70), channel_id=1, source_target_pairs={{0,2},{1,3},{2,0},{3,1},{4,6},{5,7},{6,4},{7,5},{8,10},{9,11},{10,... | collective-permute-start | bytes 589832 | tf_op jit(solution)/shard_map/ppermute | solution.py:535
  9.9 2.5 %collective-permute-done.5.refs_1_ = bf16[6,2,64,128]{3,2,1,0:T(8,128)(2,1)S(1)} collective-permute-done((bf16[6,2,64,128]{3,2,1,0:T(8,128)(2,1)S(1)}, bf16[6,2,64,128]{3,2,1,0:T(8,128)(2,1)S(1)}, u32[]{:S(2)}, u32[]{:S(2)}) %collective-permute-start.5) | collective-permute-done | bytes 196640 | tf_op jit(solution)/shard_map/ppermute | solution.py:535
  13.0 4.5 %collective-permute-done.6.refs_2_ = bf16[6,2,64,128]{3,2,1,0:T(8,128)(2,1)S(1)} collective-permute-done((bf16[6,2,64,128]{3,2,1,0:T(8,128)(2,1)S(1)}, bf16[6,2,64,128]{3,2,1,0:T(8,128)(2,1)S(1)}, u32[]{:S(2)}, u32[]{:S(2)}) %collective-permute-start.6) | collective-permute-done | bytes 196640 | tf_op jit(solution)/shard_map/ppermute | solution.py:535
  24.0 3.3 %pack_weights.1 = (bf16[4,256,512]{2,1,0:T(8,128)(2,1)S(1)}, bf16[4,448,768]{2,1,0:T(8,128)(2,1)S(1)}, bf16[4,192,448]{2,1,0:T(8,128)(2,1)S(1)}, bf16[4,256,384]{2,1,0:T(8,128)(2,1)S(1)}) custom-call(s32[3]{0:T(128)S(1)} %pad_add_fusion.sc.refs_0_, bf16[2,448,576]{2,1,0:T(8,128)(2,1)} %bitcast.8, bf16[2,576,256]{2,1,0:T(8,128)(2,1)} %refs_1_.1, ...), custom_call_target="tpu_custom_call" | custom-call | tf_op jit(solution)/shard_map/pack_weights/pallas_call | solution.py:375
  28.5 4.9 %two_layers.6 = (bf16[5,4,64,128]{3,2,1,0:T(8,128)(2,1)S(1)}, bf16[16,64,128]{2,1,0:T(8,128)(2,1)S(1)}, bf16[8,64,128]{2,1,0:T(8,128)(2,1)S(1)}, bf16[8,64,128]{2,1,0:T(8,128)(2,1)S(1)}) custom-call(s32[3]{0:T(128)S(1)} %pad_add_fusion.sc.refs_0_, bf16[4,256,512]{2,1,0:T(8,128)(2,1)S(1)} %get-tuple-element.67.refs_1_, ...), custom_call_target="tpu_custom_call" | custom-call | tf_op jit(solution)/shard_map/two_layers/pallas_call | solution.py:309
  37.2 2.8 %collective-permute-done.16.refs_8_ = bf16[8,64,128]{2,1,0:T(8,128)(2,1)S(1)} collective-permute-done((bf16[8,64,128]{2,1,0:T(8,128)(2,1)S(1)}, bf16[8,64,128]{2,1,0:T(8,128)(2,1)S(1)}, u32[]{:S(2)}, u32[]{:S(2)}) %collective-permute-start.16) | collective-permute-done | bytes 131104 | tf_op jit(solution)/shard_map/ppermute | solution.py:531
  39.9 4.3 %two_layers.7 = (bf16[5,4,64,128]{3,2,1,0:T(8,128)(2,1)S(1)}, bf16[14,64,128]{2,1,0:T(8,128)(2,1)S(1)}, bf16[4,64,128]{2,1,0:T(8,128)(2,1)S(1)}, bf16[10,64,128]{2,1,0:T(8,128)(2,1)S(1)}) custom-call(s32[3]{0:T(128)S(1)} %pad_add_fusion.sc.refs_0_, bf16[4,448,768]{2,1,0:T(8,128)(2,1)S(1)} %get-tuple-element.64.refs_2_.refs_1_, ...), custom_call_target="tpu_custom_call" | custom-call | tf_op jit(solution)/shard_map/two_layers/pallas_call | solution.py:309
  44.2 2.5 %collective-permute-start.17 = (bf16[14,64,128]{2,1,0:T(8,128)(2,1)S(1)}, bf16[14,64,128]{2,1,0:T(8,128)(2,1)S(1)}, u32[]{:S(2)}, u32[]{:S(2)}) collective-permute-start(bf16[14,64,128]{2,1,0:T(8,128)(2,1)S(1)} %get-tuple-element.84), channel_id=1, source_target_pairs={{0,64},{64,0},{1,65},{65,1},{2,66},{66,2},{3,67},{67,3},{4,68},{68... | collective-permute-start | bytes 688136 | tf_op jit(solution)/shard_map/ppermute | solution.py:528
  48.4 2.6 %collective-permute-done.13.refs_4_ = bf16[8,64,128]{2,1,0:T(8,128)(2,1)S(1)} collective-permute-done((bf16[8,64,128]{2,1,0:T(8,128)(2,1)S(1)}, bf16[8,64,128]{2,1,0:T(8,128)(2,1)S(1)}, u32[]{:S(2)}, u32[]{:S(2)}) %collective-permute-start.13) | collective-permute-done | bytes 131104 | tf_op jit(solution)/shard_map/ppermute | solution.py:531
  51.1 2.4 %early_sums.6 = (f32[5,448,256]{2,1,0:T(8,128)S(1)}, f32[3,256,256]{2,1,0:T(8,128)S(1)}) custom-call(s32[3]{0:T(128)S(1)} %pad_add_fusion.sc.refs_0_, bf16[4,256,512]{2,1,0:T(8,128)(2,1)S(1)} %get-tuple-element.67.refs_1_, bf16[4,448,768]{2,1,0:T(8,128)(2,1)S(1)} %get-tuple-element.64.refs_2_.refs_1_, ...), custom_call_target="tpu_custom_call" | custom-call | tf_op jit(solution)/shard_map/early_sums/pallas_call | solution.py:273
  53.5 3.5 %two_layers.8 = (bf16[5,4,64,128]{3,2,1,0:T(8,128)(2,1)S(1)}, bf16[16,64,128]{2,1,0:T(8,128)(2,1)S(1)}, bf16[8,64,128]{2,1,0:T(8,128)(2,1)S(1)}, bf16[8,64,128]{2,1,0:T(8,128)(2,1)S(1)}) custom-call(s32[3]{0:T(128)S(1)} %pad_add_fusion.sc.refs_0_, bf16[4,448,768]{2,1,0:T(8,128)(2,1)S(1)} %get-tuple-element.64.refs_2_.refs_1_, ...), custom_call_target="tpu_custom_call" | custom-call | tf_op jit(solution)/shard_map/two_layers/pallas_call | solution.py:309
  57.0 2.3 %collective-permute-start.20 = (bf16[16,64,128]{2,1,0:T(8,128)(2,1)S(1)}, bf16[16,64,128]{2,1,0:T(8,128)(2,1)S(1)}, u32[]{:S(2)}, u32[]{:S(2)}) collective-permute-start(bf16[16,64,128]{2,1,0:T(8,128)(2,1)S(1)} %get-tuple-element.90), channel_id=1, source_target_pairs={{0,64},{64,0},{1,65},{65,1},{2,66},{66,2},{3,67},{67,3},{4,68},{68... | collective-permute-start | bytes 786440 | tf_op jit(solution)/shard_map/ppermute | solution.py:528
  61.1 3.3 %collective-permute-done.21.refs_3_.refs_4_ = bf16[10,64,128]{2,1,0:T(8,128)(2,1)S(1)} collective-permute-done((bf16[10,64,128]{2,1,0:T(8,128)(2,1)S(1)}, bf16[10,64,128]{2,1,0:T(8,128)(2,1)S(1)}, u32[]{:S(2)}, u32[]{:S(2)}) %collective-permute-start.21) | collective-permute-done | bytes 163872 | tf_op jit(solution)/shard_map/ppermute | solution.py:531
  66.0 4.3 %two_layers.9 = (bf16[5,4,64,128]{3,2,1,0:T(8,128)(2,1)S(1)}, bf16[14,64,128]{2,1,0:T(8,128)(2,1)S(1)}, bf16[4,64,128]{2,1,0:T(8,128)(2,1)S(1)}, bf16[10,64,128]{2,1,0:T(8,128)(2,1)S(1)}) custom-call(s32[3]{0:T(128)S(1)} %pad_add_fusion.sc.refs_0_, bf16[4,448,768]{2,1,0:T(8,128)(2,1)S(1)} %get-tuple-element.64.refs_2_.refs_1_, ...), custom_call_target="tpu_custom_call" | custom-call | tf_op jit(solution)/shard_map/two_layers/pallas_call | solution.py:309
  70.3 2.8 %collective-permute-start.23 = (bf16[14,64,128]{2,1,0:T(8,128)(2,1)S(1)}, bf16[14,64,128]{2,1,0:T(8,128)(2,1)S(1)}, u32[]{:S(2)}, u32[]{:S(2)}) collective-permute-start(bf16[14,64,128]{2,1,0:T(8,128)(2,1)S(1)} %get-tuple-element.96), channel_id=1, source_target_pairs={{0,64},{64,0},{1,65},{65,1},{2,66},{66,2},{3,67},{67,3},{4,68},{68... | collective-permute-start | bytes 688136 | tf_op jit(solution)/shard_map/ppermute | solution.py:528
  74.9 2.6 %collective-permute-done.19.refs_4_ = bf16[8,64,128]{2,1,0:T(8,128)(2,1)S(1)} collective-permute-done((bf16[8,64,128]{2,1,0:T(8,128)(2,1)S(1)}, bf16[8,64,128]{2,1,0:T(8,128)(2,1)S(1)}, u32[]{:S(2)}, u32[]{:S(2)}) %collective-permute-start.19) | collective-permute-done | bytes 131104 | tf_op jit(solution)/shard_map/ppermute | solution.py:531
  77.5 2.4 %early_sums.8 = (f32[5,448,256]{2,1,0:T(8,128)S(1)}, f32[3,256,256]{2,1,0:T(8,128)S(1)}) custom-call(s32[3]{0:T(128)S(1)} %pad_add_fusion.sc.refs_0_, bf16[4,256,512]{2,1,0:T(8,128)(2,1)S(1)} %get-tuple-element.67.refs_1_, bf16[4,448,768]{2,1,0:T(8,128)(2,1)S(1)} %get-tuple-element.64.refs_2_.refs_1_, ...), custom_call_target="tpu_custom_call" | custom-call | tf_op jit(solution)/shard_map/early_sums/pallas_call | solution.py:273
  80.0 3.5 %two_layers.10 = (bf16[5,4,64,128]{3,2,1,0:T(8,128)(2,1)S(1)}, bf16[8,64,128]{2,1,0:T(8,128)(2,1)S(1)}, bf16[8,64,128]{2,1,0:T(8,128)(2,1)S(1)}) custom-call(s32[3]{0:T(128)S(1)} %pad_add_fusion.sc.refs_0_, bf16[4,448,768]{2,1,0:T(8,128)(2,1)S(1)} %get-tuple-element.64.refs_2_.refs_1_, bf16[4,192,448]{2,1,0:T(8,128)(2,1)S(1)} %get-tuple-element.65.refs_3_.refs_2_, ...), custom_call_target="tpu_custom_call" | custom-call | tf_op jit(solution)/shard_map/two_layers/pallas_call | solution.py:309
  83.4 2.3 %collective-permute-start.26 = (bf16[8,64,128]{2,1,0:T(8,128)(2,1)S(1)}, bf16[8,64,128]{2,1,0:T(8,128)(2,1)S(1)}, u32[]{:S(2)}, u32[]{:S(2)}) collective-permute-start(bf16[8,64,128]{2,1,0:T(8,128)(2,1)S(1)} %get-tuple-element.103), channel_id=1, source_target_pairs={{0,64},{64,0},{1,65},{65,1},{2,66},{66,2},{3,67},{67,3},{4,68},{68... | collective-permute-start | bytes 393224 | tf_op jit(solution)/shard_map/ppermute | solution.py:528
  87.3 2.7 %collective-permute-done.27.refs_7_ = bf16[8,64,128]{2,1,0:T(8,128)(2,1)S(1)} collective-permute-done((bf16[8,64,128]{2,1,0:T(8,128)(2,1)S(1)}, bf16[8,64,128]{2,1,0:T(8,128)(2,1)S(1)}, u32[]{:S(2)}, u32[]{:S(2)}) %collective-permute-start.27) | collective-permute-done | bytes 131104 | tf_op jit(solution)/shard_map/ppermute | solution.py:531
  90.1 4.3 %two_layers.11 = (bf16[5,4,64,128]{3,2,1,0:T(8,128)(2,1)S(1)}, bf16[5,4,64,128]{3,2,1,0:T(8,128)(2,1)S(1)}) custom-call(s32[3]{0:T(128)S(1)} %pad_add_fusion.sc.refs_0_, bf16[4,448,768]{2,1,0:T(8,128)(2,1)S(1)} %get-tuple-element.64.refs_2_.refs_1_, bf16[4,192,448]{2,1,0:T(8,128)(2,1)S(1)} %get-tuple-element.65.refs_3_.refs_2_, ...), custom_call_target="tpu_custom_call" | custom-call | tf_op jit(solution)/shard_map/two_layers/pallas_call | solution.py:309
  94.4 2.5 %collective-permute-start.28 = (bf16[5,4,64,128]{3,2,1,0:T(8,128)(2,1)S(1)}, bf16[5,4,64,128]{3,2,1,0:T(8,128)(2,1)S(1)}, u32[]{:S(2)}, u32[]{:S(2)}) collective-permute-start(bf16[5,4,64,128]{3,2,1,0:T(8,128)(2,1)S(1)} %get-tuple-element.108), channel_id=1, source_target_pairs={{0,64},{64,0},{1,65},{65,1},{2,66},{66,2},{3,67},{67,3},{4,68},{68... | collective-permute-start | bytes 983048 | tf_op jit(solution)/shard_map/ppermute | solution.py:528
  102.1 4.3 %collective-permute-done.29.refs_1_ = bf16[5,2,64,128]{3,2,1,0:T(8,128)(2,1)S(1)} collective-permute-done((bf16[5,2,64,128]{3,2,1,0:T(8,128)(2,1)S(1)}, bf16[5,2,64,128]{3,2,1,0:T(8,128)(2,1)S(1)}, u32[]{:S(2)}, u32[]{:S(2)}) %collective-permute-start.29) | collective-permute-done | bytes 163872 | tf_op jit(solution)/shard_map/ppermute | solution.py:535
  106.4 2.2 %collective-permute-done.30.refs_2_ = bf16[5,2,64,128]{3,2,1,0:T(8,128)(2,1)S(1)} collective-permute-done((bf16[5,2,64,128]{3,2,1,0:T(8,128)(2,1)S(1)}, bf16[5,2,64,128]{3,2,1,0:T(8,128)(2,1)S(1)}, u32[]{:S(2)}, u32[]{:S(2)}) %collective-permute-start.30) | collective-permute-done | bytes 163872 | tf_op jit(solution)/shard_map/ppermute | solution.py:535
  (57 shorter events, 34.0 us)
Async XLA Ops:
  0.7 23.3 %collective-permute-start = (bf16[2,448,576]{2,1,0:T(8,128)(2,1)}, bf16[2,448,576]{2,1,0:T(8,128)(2,1)S(1)}, u32[]{:S(2)}, u32[]{:S(2)}) collective-permute-start(bf16[2,448,576]{2,1,0:T(8,128)(2,1)} %bitcast.7), channel_id=1, source_target_pairs={{0,64},{64,0},{1,65},{65,1},{2,66},{66,2},{3,67},{67,3},{4,68},{68... | collective-permute-start | bytes 3096584 | tf_op jit(solution)/shard_map/ppermute | solution.py:528
  3.3 9.1 %collective-permute-start.5 = (bf16[6,2,64,128]{3,2,1,0:T(8,128)(2,1)S(1)}, bf16[6,2,64,128]{3,2,1,0:T(8,128)(2,1)S(1)}, u32[]{:S(2)}, u32[]{:S(2)}) collective-permute-start(bf16[6,2,64,128]{3,2,1,0:T(8,128)(2,1)S(1)} %get-tuple-element.69), channel_id=1, source_target_pairs={{0,1},{1,2},{2,3},{3,0},{4,5},{5,6},{6,7},{7,4},{8,9},{9,10},{10,1... | collective-permute-start | bytes 589832 | tf_op jit(solution)/shard_map/ppermute | solution.py:535
  5.0 12.5 %collective-permute-start.6 = (bf16[6,2,64,128]{3,2,1,0:T(8,128)(2,1)S(1)}, bf16[6,2,64,128]{3,2,1,0:T(8,128)(2,1)S(1)}, u32[]{:S(2)}, u32[]{:S(2)}) collective-permute-start(bf16[6,2,64,128]{3,2,1,0:T(8,128)(2,1)S(1)} %get-tuple-element.70), channel_id=1, source_target_pairs={{0,2},{1,3},{2,0},{3,1},{4,6},{5,7},{6,4},{7,5},{8,10},{9,11},{10,... | collective-permute-start | bytes 589832 | tf_op jit(solution)/shard_map/ppermute | solution.py:535
  8.3 10.1 %collective-permute-start.7 = (bf16[6,2,64,128]{3,2,1,0:T(8,128)(2,1)S(1)}, bf16[6,2,64,128]{3,2,1,0:T(8,128)(2,1)S(1)}, u32[]{:S(2)}, u32[]{:S(2)}) collective-permute-start(bf16[6,2,64,128]{3,2,1,0:T(8,128)(2,1)S(1)} %get-tuple-element.71), channel_id=1, source_target_pairs={{0,3},{1,0},{2,1},{3,2},{4,7},{5,4},{6,5},{7,6},{8,11},{9,8},{10,9... | collective-permute-start | bytes 589832 | tf_op jit(solution)/shard_map/ppermute | solution.py:535
  9.0 9.3 %collective-permute-start.8 = (bf16[6,2,64,128]{3,2,1,0:T(8,128)(2,1)S(1)}, bf16[6,2,64,128]{3,2,1,0:T(8,128)(2,1)S(1)}, u32[]{:S(2)}, u32[]{:S(2)}) collective-permute-start(bf16[6,2,64,128]{3,2,1,0:T(8,128)(2,1)S(1)} %get-tuple-element.68.refs_0_), channel_id=1, source_target_pairs={{0,64},{64,0},{1,65},{65,1},{2,66},{66,2},{3,67},{67,3},{4,68},{68... | collective-permute-start | bytes 589832 | tf_op jit(solution)/shard_map/ppermute | solution.py:528
  12.4 6.5 %collective-permute-start.9 = (bf16[6,2,64,128]{3,2,1,0:T(8,128)(2,1)S(1)}, bf16[6,2,64,128]{3,2,1,0:T(8,128)(2,1)S(1)}, u32[]{:S(2)}, u32[]{:S(2)}) collective-permute-start(bf16[6,2,64,128]{3,2,1,0:T(8,128)(2,1)S(1)} %collective-permute-done.5.refs_1_), channel_id=1, source_target_pairs={{0,64},{64,0},{1,65},{65,1},{2,66},{66,2},{3,67},{67,3},{4,68},{68... | collective-permute-start | bytes 589832 | tf_op jit(solution)/shard_map/ppermute | solution.py:528
  17.5 6.6 %collective-permute-start.1 = (bf16[2,576,256]{2,1,0:T(8,128)(2,1)}, bf16[2,576,256]{2,1,0:T(8,128)(2,1)S(1)}, u32[]{:S(2)}, u32[]{:S(2)}) collective-permute-start(bf16[2,576,256]{2,1,0:T(8,128)(2,1)} %refs_1_.1), channel_id=1, source_target_pairs={{0,64},{64,0},{1,65},{65,1},{2,66},{66,2},{3,67},{67,3},{4,68},{68... | collective-permute-start | bytes 1769480 | tf_op jit(solution)/shard_map/ppermute | solution.py:528
  18.9 5.1 %collective-permute-start.2 = (bf16[2,192,576]{2,1,0:T(8,128)(2,1)}, bf16[2,192,576]{2,1,0:T(8,128)(2,1)S(1)}, u32[]{:S(2)}, u32[]{:S(2)}) collective-permute-start(bf16[2,192,576]{2,1,0:T(8,128)(2,1)} %bitcast.9), channel_id=1, source_target_pairs={{0,64},{64,0},{1,65},{65,1},{2,66},{66,2},{3,67},{67,3},{4,68},{68... | collective-permute-start | bytes 1327112 | tf_op jit(solution)/shard_map/ppermute | solution.py:528
  21.9 6.5 %collective-permute-start.12 = (bf16[18,64,128]{2,1,0:T(8,128)(2,1)S(1)}, bf16[18,64,128]{2,1,0:T(8,128)(2,1)S(1)}, u32[]{:S(2)}, u32[]{:S(2)}) collective-permute-start(bf16[18,64,128]{2,1,0:T(8,128)(2,1)S(1)} %get-tuple-element.72), channel_id=1, source_target_pairs={{64,4},{0,1},{65,5},{1,0},{66,6},{2,3},{67,7},{3,2},{68,8},{4,64},... | collective-permute-start | bytes 884744 | tf_op jit(solution)/shard_map/ppermute | solution.py:531
  23.4 12.2 %collective-permute-start.15 = (bf16[18,64,128]{2,1,0:T(8,128)(2,1)S(1)}, bf16[18,64,128]{2,1,0:T(8,128)(2,1)S(1)}, u32[]{:S(2)}, u32[]{:S(2)}) collective-permute-start(bf16[18,64,128]{2,1,0:T(8,128)(2,1)S(1)} %get-tuple-element.77), channel_id=1, source_target_pairs={{64,4},{0,1},{65,5},{1,0},{66,6},{2,3},{67,7},{3,2},{68,8},{4,64},... | collective-permute-start | bytes 884744 | tf_op jit(solution)/shard_map/ppermute | solution.py:531
  33.4 6.5 %collective-permute-start.14 = (bf16[16,64,128]{2,1,0:T(8,128)(2,1)S(1)}, bf16[16,64,128]{2,1,0:T(8,128)(2,1)S(1)}, u32[]{:S(2)}, u32[]{:S(2)}) collective-permute-start(bf16[16,64,128]{2,1,0:T(8,128)(2,1)S(1)} %get-tuple-element.76), channel_id=1, source_target_pairs={{0,64},{64,0},{1,65},{65,1},{2,66},{66,2},{3,67},{67,3},{4,68},{68... | collective-permute-start | bytes 786440 | tf_op jit(solution)/shard_map/ppermute | solution.py:528
  35.5 4.4 %collective-permute-start.16 = (bf16[8,64,128]{2,1,0:T(8,128)(2,1)S(1)}, bf16[8,64,128]{2,1,0:T(8,128)(2,1)S(1)}, u32[]{:S(2)}, u32[]{:S(2)}) collective-permute-start(bf16[8,64,128]{2,1,0:T(8,128)(2,1)S(1)} %get-tuple-element.80), channel_id=1, source_target_pairs={{64,4},{0,1},{65,5},{1,0},{66,6},{2,3},{67,7},{3,2},{68,8},{4,64},... | collective-permute-start | bytes 393224 | tf_op jit(solution)/shard_map/ppermute | solution.py:531
  44.2 9.3 %collective-permute-start.17 = (bf16[14,64,128]{2,1,0:T(8,128)(2,1)S(1)}, bf16[14,64,128]{2,1,0:T(8,128)(2,1)S(1)}, u32[]{:S(2)}, u32[]{:S(2)}) collective-permute-start(bf16[14,64,128]{2,1,0:T(8,128)(2,1)S(1)} %get-tuple-element.84), channel_id=1, source_target_pairs={{0,64},{64,0},{1,65},{65,1},{2,66},{66,2},{3,67},{67,3},{4,68},{68... | collective-permute-start | bytes 688136 | tf_op jit(solution)/shard_map/ppermute | solution.py:528
  46.7 6.8 %collective-permute-start.18 = (bf16[4,64,128]{2,1,0:T(8,128)(2,1)S(1)}, bf16[4,64,128]{2,1,0:T(8,128)(2,1)S(1)}, u32[]{:S(2)}, u32[]{:S(2)}) collective-permute-start(bf16[4,64,128]{2,1,0:T(8,128)(2,1)S(1)} %get-tuple-element.85), channel_id=1, source_target_pairs={{64,4},{0,1},{65,5},{1,0},{66,6},{2,3},{67,7},{3,2},{68,8},{4,64},... | collective-permute-start | bytes 196616 | tf_op jit(solution)/shard_map/ppermute | solution.py:531
  57.0 9.0 %collective-permute-start.20 = (bf16[16,64,128]{2,1,0:T(8,128)(2,1)S(1)}, bf16[16,64,128]{2,1,0:T(8,128)(2,1)S(1)}, u32[]{:S(2)}, u32[]{:S(2)}) collective-permute-start(bf16[16,64,128]{2,1,0:T(8,128)(2,1)S(1)} %get-tuple-element.90), channel_id=1, source_target_pairs={{0,64},{64,0},{1,65},{65,1},{2,66},{66,2},{3,67},{67,3},{4,68},{68... | collective-permute-start | bytes 786440 | tf_op jit(solution)/shard_map/ppermute | solution.py:528
  59.3 5.0 %collective-permute-start.21 = (bf16[10,64,128]{2,1,0:T(8,128)(2,1)S(1)}, bf16[10,64,128]{2,1,0:T(8,128)(2,1)S(1)}, u32[]{:S(2)}, u32[]{:S(2)}) collective-permute-start(bf16[10,64,128]{2,1,0:T(8,128)(2,1)S(1)} %get-tuple-element.91), channel_id=1, source_target_pairs={{64,4},{0,1},{65,5},{1,0},{66,6},{2,3},{67,7},{3,2},{68,8},{4,64},... | collective-permute-start | bytes 491528 | tf_op jit(solution)/shard_map/ppermute | solution.py:531
  59.3 6.7 %collective-permute-start.22 = (bf16[8,64,128]{2,1,0:T(8,128)(2,1)S(1)}, bf16[8,64,128]{2,1,0:T(8,128)(2,1)S(1)}, u32[]{:S(2)}, u32[]{:S(2)}) collective-permute-start(bf16[8,64,128]{2,1,0:T(8,128)(2,1)S(1)} %get-tuple-element.92), channel_id=1, source_target_pairs={{64,4},{0,1},{65,5},{1,0},{66,6},{2,3},{67,7},{3,2},{68,8},{4,64},... | collective-permute-start | bytes 393224 | tf_op jit(solution)/shard_map/ppermute | solution.py:531
  70.3 9.6 %collective-permute-start.23 = (bf16[14,64,128]{2,1,0:T(8,128)(2,1)S(1)}, bf16[14,64,128]{2,1,0:T(8,128)(2,1)S(1)}, u32[]{:S(2)}, u32[]{:S(2)}) collective-permute-start(bf16[14,64,128]{2,1,0:T(8,128)(2,1)S(1)} %get-tuple-element.96), channel_id=1, source_target_pairs={{0,64},{64,0},{1,65},{65,1},{2,66},{66,2},{3,67},{67,3},{4,68},{68... | collective-permute-start | bytes 688136 | tf_op jit(solution)/shard_map/ppermute | solution.py:528
  73.1 6.8 %collective-permute-start.24 = (bf16[4,64,128]{2,1,0:T(8,128)(2,1)S(1)}, bf16[4,64,128]{2,1,0:T(8,128)(2,1)S(1)}, u32[]{:S(2)}, u32[]{:S(2)}) collective-permute-start(bf16[4,64,128]{2,1,0:T(8,128)(2,1)S(1)} %get-tuple-element.97), channel_id=1, source_target_pairs={{64,4},{0,1},{65,5},{1,0},{66,6},{2,3},{67,7},{3,2},{68,8},{4,64},... | collective-permute-start | bytes 196616 | tf_op jit(solution)/shard_map/ppermute | solution.py:531
  74.9 10.8 %collective-permute-start.25 = (bf16[10,64,128]{2,1,0:T(8,128)(2,1)S(1)}, bf16[10,64,128]{2,1,0:T(8,128)(2,1)S(1)}, u32[]{:S(2)}, u32[]{:S(2)}) collective-permute-start(bf16[10,64,128]{2,1,0:T(8,128)(2,1)S(1)} %get-tuple-element.102), channel_id=1, source_target_pairs={{64,4},{0,1},{65,5},{1,0},{66,6},{2,3},{67,7},{3,2},{68,8},{4,64},... | collective-permute-start | bytes 491528 | tf_op jit(solution)/shard_map/ppermute | solution.py:531
  85.7 4.4 %collective-permute-start.27 = (bf16[8,64,128]{2,1,0:T(8,128)(2,1)S(1)}, bf16[8,64,128]{2,1,0:T(8,128)(2,1)S(1)}, u32[]{:S(2)}, u32[]{:S(2)}) collective-permute-start(bf16[8,64,128]{2,1,0:T(8,128)(2,1)S(1)} %get-tuple-element.104), channel_id=1, source_target_pairs={{64,4},{0,1},{65,5},{1,0},{66,6},{2,3},{67,7},{3,2},{68,8},{4,64},... | collective-permute-start | bytes 393224 | tf_op jit(solution)/shard_map/ppermute | solution.py:531
  99.0 7.3 %collective-permute-start.29 = (bf16[5,2,64,128]{3,2,1,0:T(8,128)(2,1)S(1)}, bf16[5,2,64,128]{3,2,1,0:T(8,128)(2,1)S(1)}, u32[]{:S(2)}, u32[]{:S(2)}) collective-permute-start(bf16[5,2,64,128]{3,2,1,0:T(8,128)(2,1)S(1)} %get-tuple-element.110), channel_id=1, source_target_pairs={{0,1},{1,2},{2,3},{3,0},{4,5},{5,6},{6,7},{7,4},{8,9},{9,10},{10,1... | collective-permute-start | bytes 491528 | tf_op jit(solution)/shard_map/ppermute | solution.py:535
  99.1 9.5 %collective-permute-start.30 = (bf16[5,2,64,128]{3,2,1,0:T(8,128)(2,1)S(1)}, bf16[5,2,64,128]{3,2,1,0:T(8,128)(2,1)S(1)}, u32[]{:S(2)}, u32[]{:S(2)}) collective-permute-start(bf16[5,2,64,128]{3,2,1,0:T(8,128)(2,1)S(1)} %get-tuple-element.111), channel_id=1, source_target_pairs={{0,2},{1,3},{2,0},{3,1},{4,6},{5,7},{6,4},{7,5},{8,10},{9,11},{10,... | collective-permute-start | bytes 491528 | tf_op jit(solution)/shard_map/ppermute | solution.py:535
  101.1 8.4 %collective-permute-start.31 = (bf16[5,2,64,128]{3,2,1,0:T(8,128)(2,1)S(1)}, bf16[5,2,64,128]{3,2,1,0:T(8,128)(2,1)S(1)}, u32[]{:S(2)}, u32[]{:S(2)}) collective-permute-start(bf16[5,2,64,128]{3,2,1,0:T(8,128)(2,1)S(1)} %get-tuple-element.112), channel_id=1, source_target_pairs={{0,3},{1,0},{2,1},{3,2},{4,7},{5,4},{6,5},{7,6},{8,11},{9,8},{10,9... | collective-permute-start | bytes 491528 | tf_op jit(solution)/shard_map/ppermute | solution.py:535
  (8 other events, 25.1 us)
